TPU v7x, 32 devices: a whole 2x2x4 slice. The times are simulated.
32 devices in a mesh: head: 4 (over y, x), batch: 8 (over z, core).
Axes of the slice: x: 2, y: 2, z: 4, core: 2. Of those that a mesh axis runs over, the one named last changes fastest.
Arguments:
- hidden_in: bfloat16 [8, 256, 4096], P('batch', None, 'head')
- w_query: bfloat16 [4096, 4096], P('batch', 'head'), may hold values from -0.09375 to 0.09375
- w_key: bfloat16 [4096, 4096], P('batch', 'head'), may hold values from -0.09375 to 0.09375
- w_value: bfloat16 [4096, 4096], P('batch', 'head'), may hold values from -0.09375 to 0.09375
- w_beta: bfloat16 [4096, 32], P('batch', 'head'), may hold values from -0.09375 to 0.09375
- w_out: bfloat16 [4096, 4096], P('head', 'batch'), may hold values from -0.125 to 0.125
- mem_pos: int32 [8, 2, 64], P('batch'), may hold values from 0 to 127, as said below
- memory_in: float32 [8, 32, 128, 128], P('batch', 'head'), may hold values from -6 to 6
Outputs:
- hidden_out: bfloat16 [8, 256, 4096], P('batch', None, 'head')
- memory_out: float32 [8, 32, 128, 128], P('batch', 'head')
Inputs may be any that keep to these rules, and one draw needn't show every extreme that they name: `mem_pos`: within each sequence and segment the 64 positions are distinct and ascending.
All inputs are finite; a program needn't handle non-finite values.
Results may differ from a plain program's by a relative error of at most 0.005.
Values may be sent and summed in bfloat16 or wider, within the bound.
No kernel may reach another device: no remote copies, remote signals or barrier semaphores. Data moves between devices by JAX's collectives and lax.ppermute only.
A program may use at most 128 MiB of HBM per device.

v0:
```python
import functools

import jax
import jax.numpy as jnp
from jax import lax
from jax.experimental import pallas as pl
from jax.experimental.pallas import tpu as pltpu
from jax.sharding import PartitionSpec as P

SEGS = 2
CORES = 2
PAD = 8
epsilon = 1e-05


def recur(query, keys, values, beta, state):
    highest = lax.Precision.HIGHEST
    readouts = []
    for segment in range(query.shape[1]):
        readouts.append(
            jnp.einsum("bhij,blhj->blhi", state, query[:, segment], precision=highest).astype(
                jnp.bfloat16
            )
        )
        recalled = jnp.einsum("bhij,bmhj->bmhi", state, keys[:, segment], precision=highest)
        change = beta[:, segment][..., None] * (values[:, segment] - recalled)
        state = state + jnp.einsum("bmhi,bmhj->bhij", change, keys[:, segment], precision=highest)
    return (jnp.stack(readouts, axis=1), state)


def general_body(hidden_in, w_query, w_key, w_value, w_beta, w_out, mem_pos, memory_in):
    seq_count, row_count, local_width = hidden_in.shape
    seg_rows = row_count // SEGS
    mem_count = mem_pos.shape[2]
    local_heads = w_beta.shape[1]
    local_features = w_query.shape[1]
    head_size = local_features // local_heads
    x_float = hidden_in.astype(jnp.float32)
    whole = lax.all_gather(hidden_in, "head", axis=2, tiled=True)
    whole_float = whole.astype(jnp.float32)
    mean_square = jnp.mean(whole_float * whole_float, axis=2, keepdims=True)
    normed = (whole_float * lax.rsqrt(mean_square + epsilon)).astype(jnp.bfloat16)
    full_width = normed.shape[2]
    offsets = (jnp.arange(SEGS, dtype=jnp.int32) * seg_rows)[None, :, None]
    picked = (mem_pos + offsets).reshape(seq_count, SEGS * mem_count)
    memory_rows = jax.vmap(lambda block, where: jnp.take(block, where, axis=0))(normed, picked)
    memory_rows = memory_rows.reshape(seq_count * SEGS * mem_count, full_width)
    token_rows = normed.reshape(seq_count * row_count, full_width)
    piece_query = lax.all_gather(w_query, "batch", axis=0, tiled=True)
    piece_key = lax.all_gather(w_key, "batch", axis=0, tiled=True)
    piece_value = lax.all_gather(w_value, "batch", axis=0, tiled=True)
    piece_beta = lax.all_gather(w_beta, "batch", axis=0, tiled=True)
    query = jnp.dot(token_rows, piece_query, preferred_element_type=jnp.float32)
    keys = jnp.dot(memory_rows, piece_key, preferred_element_type=jnp.float32)
    values = jnp.dot(memory_rows, piece_value, preferred_element_type=jnp.float32)
    logits = jnp.dot(memory_rows, piece_beta, preferred_element_type=jnp.float32)
    query = (query * head_size ** (-0.5)).reshape(seq_count, SEGS, seg_rows, local_heads, head_size)
    keys = keys.reshape(seq_count, SEGS, mem_count, local_heads, head_size)
    keys = keys * lax.rsqrt(jnp.sum(keys * keys, axis=-1, keepdims=True) + 1e-06)
    values = values.reshape(seq_count, SEGS, mem_count, local_heads, head_size)
    beta = jax.nn.sigmoid(logits).reshape(seq_count, SEGS, mem_count, local_heads)
    readout, state = recur(query, keys, values, beta, memory_in)
    readout = readout.reshape(seq_count * row_count, local_features)
    terms = jnp.dot(
        readout,
        lax.all_gather(w_out, "batch", axis=1, tiled=True),
        preferred_element_type=jnp.float32,
    )
    mixed = lax.psum_scatter(terms, "head", scatter_dimension=1, tiled=True)
    hidden_out = (mixed + x_float.reshape(seq_count * row_count, local_width)).astype(jnp.bfloat16)
    return (hidden_out.reshape(hidden_in.shape), state)


VM = pl.BlockSpec(memory_space=pltpu.VMEM)
SM = pl.BlockSpec(memory_space=pltpu.SMEM)


def call(kernel, args, outs, scratch=(), flops=0, grid=(), specs=None, out_specs=None):
    size = sum(a.size * a.dtype.itemsize for a in list(args[1:]) + list(outs))
    return pl.pallas_call(
        kernel,
        out_shape=outs,
        grid=grid,
        in_specs=[SM] + list(specs or [VM] * (len(args) - 1)),
        out_specs=list(out_specs or [VM] * len(outs)),
        scratch_shapes=list(scratch),
        cost_estimate=pl.CostEstimate(flops=flops, bytes_accessed=size, transcendentals=0),
    )(*args)


def whole(value):
    return pl.BlockSpec(value.shape, lambda n: (0,) * len(value.shape))


def columns_of(value, tile):
    return pl.BlockSpec((value.shape[0], tile), lambda n: (0, n))


def norm_kernel(heads, width, ids, *refs):
    blocks = refs[:heads]
    outs = refs[heads:-1]
    held = refs[-1]
    square = None
    for block in blocks:
        value = block[...].astype(jnp.float32)
        part = jnp.sum(value * value, axis=-1, keepdims=True)
        square = part if square is None else square + part
    scale = lax.rsqrt(square / width + epsilon)
    for m, block in enumerate(blocks):
        held[m] = (block[...].astype(jnp.float32) * scale).astype(jnp.bfloat16)
    mix = ids[0] ^ ids[1]
    for s in range(SEGS):
        for j in range(heads):
            outs[s * heads + j][...] = held[mix ^ j, s]


def project_kernel(heads, seg, size, groups, ids, *refs):
    pieces = refs[:heads]
    pos = refs[heads : 2 * heads]
    own = refs[2 * heads : 2 * heads + 4]
    other = refs[2 * heads + 4 : 2 * heads + 8]
    outs = refs[2 * heads + 8 : -3]
    rows, picked, logits = refs[-3:]
    piece = pieces[0].shape[1]
    seg_rows = piece * heads
    mem_rows = pos[0].shape[1]
    depth = own[0].shape[0]
    mine = pl.ds(pl.multiple_of(ids[2] * depth, depth), depth)
    theirs = pl.ds(pl.multiple_of((1 - ids[2]) * depth, depth), depth)
    n = pl.program_id(0)

    @pl.when(n == 0)
    def _():
        for m in range(heads):
            start = pl.multiple_of((ids[0] ^ m) * piece, piece)
            for j in range(heads):
                rows[j, pl.ds(start, piece), :] = pieces[m][j]
        token = lax.broadcasted_iota(jnp.int32, (seg_rows, mem_rows), 0)
        contract = (((0,), (1,)), ((), ()))
        for j in range(heads):
            hot = jnp.where(token == pos[j][seg : seg + 1, :], 1.0, 0.0).astype(jnp.bfloat16)
            picked[j] = lax.dot_general(
                hot, rows[j], (((0,), (0,)), ((), ())), preferred_element_type=jnp.float32
            ).astype(jnp.bfloat16)
            logits[j] = lax.dot_general(
                own[3][...], picked[j, :, mine], contract, preferred_element_type=jnp.float32
            ) + lax.dot_general(
                other[3][...], picked[j, :, theirs], contract, preferred_element_type=jnp.float32
            )

    flat = lambda ref, part: ref[:, :, part].reshape(-1, depth)

    def product(source, weight):
        return jnp.dot(
            flat(source, mine), own[weight][...], preferred_element_type=jnp.float32
        ) + jnp.dot(
            flat(source, theirs), other[weight][...], preferred_element_type=jnp.float32
        )

    results = (
        (product(rows, 0).astype(jnp.bfloat16), seg_rows),
        (product(picked, 1).astype(jnp.bfloat16), mem_rows),
        (product(picked, 2).astype(jnp.bfloat16), mem_rows),
    )
    tile = own[0].shape[1]
    for g, group in enumerate(groups):
        for j in range(heads):
            out = outs[g * heads + j]
            top = 0
            for kind in group:
                result, count = results[kind]
                out[top : top + count, :] = result[j * count : (j + 1) * count]
                top += count
            if 2 in group:
                for k in range(tile // size):
                    logit = logits[j, pl.ds(n * (tile // size) + k, 1), :]
                    shown = jnp.broadcast_to(logit, (out.shape[0] - top, mem_rows))
                    shown = jnp.concatenate([shown, jnp.zeros_like(shown)], axis=1)
                    out[top:, k * size : (k + 1) * size] = shown[:, :size].astype(jnp.bfloat16)


HIGHEST = lax.Precision.HIGHEST
ACROSS = (((1,), (1,)), ((), ()))


def summed(parts, held):
    value = parts[0][...].astype(jnp.float32)
    for part in parts[1:]:
        value = value + part[...].astype(jnp.float32)
    held[...] = value


def read_states(held, states, readout, seg_rows):
    size = readout.shape[1] // len(states)
    for head, state in enumerate(states):
        columns = slice(head * size, (head + 1) * size)
        query = held[:seg_rows, columns] * size ** (-0.5)
        readout[:, columns] = lax.dot_general(
            query, state, ACROSS, precision=HIGHEST, preferred_element_type=jnp.float32
        ).astype(jnp.bfloat16)


def update_states(held, states, state_out, first, mem_rows):
    size = states[0].shape[-1]
    kept = []
    for head, state in enumerate(states):
        columns = slice(head * size, (head + 1) * size)
        keys = held[first : first + mem_rows, columns]
        keys = keys * lax.rsqrt(jnp.sum(keys * keys, axis=-1, keepdims=True) + 1e-06)
        recalled = lax.dot_general(
            keys, state, ACROSS, precision=HIGHEST, preferred_element_type=jnp.float32
        )
        kept.append((keys, recalled))
    changes = []
    for head, (keys, recalled) in enumerate(kept):
        columns = slice(head * size, (head + 1) * size)
        values = held[first + mem_rows : first + 2 * mem_rows, columns]
        logits = held[first + 2 * mem_rows :, columns]
        beta = jax.nn.sigmoid(logits).T[:mem_rows, :1]
        changes.append(beta * (values - recalled))
    for head, state in enumerate(states):
        state_out[head] = state + lax.dot_general(
            changes[head],
            kept[head][0],
            (((0,), (0,)), ((), ())),
            precision=HIGHEST,
            preferred_element_type=jnp.float32,
        )


def heads_in(state_in):
    return [state_in[head] for head in range(state_in.shape[0])]


def both_kernel(count, seg_rows, mem_rows, ids, *refs):
    state_in, readout, state_out, held = refs[count:]
    summed(refs[:count], held)
    states = heads_in(state_in)
    read_states(held, states, readout, seg_rows)
    update_states(held, states, state_out, seg_rows, mem_rows)


def read_kernel(count, seg_rows, ids, *refs):
    state_in, readout, held = refs[count:]
    summed(refs[:count], held)
    read_states(held, heads_in(state_in), readout, seg_rows)


def update_kernel(count, mem_rows, ids, *refs):
    state_in, state_out, held = refs[count:]
    summed(refs[:count], held)
    update_states(held, heads_in(state_in), state_out, 0, mem_rows)


def out_kernel(heads, ids, *refs):
    readout = refs[0]
    own = refs[1 : 1 + heads]
    other = refs[1 + heads : 1 + 2 * heads]
    outs = refs[1 + 2 * heads : 1 + 3 * heads]
    held = refs[-1]
    tile = own[0].shape[1]
    n = pl.program_id(0)
    steps = pl.num_programs(0)
    mix = ids[0] ^ ids[1]
    rows = readout[...]
    for j in range(heads):
        for core, weights in ((ids[2], own[j]), (1 - ids[2], other[j])):
            start = pl.multiple_of((core * steps + n) * tile, tile)
            held[mix ^ j, :, pl.ds(start, tile)] = jnp.dot(
                rows, weights[...], preferred_element_type=jnp.float32
            )

    @pl.when(n == steps - 1)
    def _():
        for m in range(heads):
            outs[m][...] = held[m].astype(outs[m].dtype)


def line_body(planes, heads, *arrays):
    hidden_in, w_query, w_key, w_value, w_beta, w_out, mem_pos, memory_in = arrays
    row_count, width = hidden_in.shape[1:]
    seg_rows, mem_rows = row_count // SEGS, mem_pos.shape[2]
    piece = seg_rows // heads
    local_heads = w_beta.shape[1]
    features = w_query.shape[1]
    full_width = width * heads
    size = features // local_heads
    tile = min(256, features)
    bf16, f32 = jnp.bfloat16, jnp.float32
    h, b = lax.axis_index("head"), lax.axis_index("batch")
    z, core = b // CORES, b % CORES
    ids = jnp.stack([h, z, core]).astype(jnp.int32)
    shape = jax.ShapeDtypeStruct

    def over_head(value, m):
        return lax.ppermute(value, "head", [(i, i ^ m) for i in range(heads)])

    def over_z(value, j):
        pairs = [(i, i ^ (j * CORES)) for i in range(planes * CORES)]
        return lax.ppermute(value, "batch", pairs)

    def over_core(value):
        return lax.ppermute(value, "batch", [(i, i ^ 1) for i in range(planes * CORES)])

    def edge(value, i):
        pairs = []
        for c in range(CORES):
            pairs.append((i * CORES + c, (i + 1) * CORES + c))
            pairs.append(((planes - 1 - i) * CORES + c, (planes - 2 - i) * CORES + c))
        return lax.ppermute(value, "batch", pairs)

    x = hidden_in.reshape(SEGS, heads, piece, width)
    quarter = lambda m: lax.dynamic_index_in_dim(x, h ^ m, axis=1, keepdims=False)
    blocks = [quarter(0)] + [over_head(quarter(m), m) for m in range(1, heads)]
    weights = [w_query, w_key, w_value, w_beta]
    partner = [over_core(w) for w in weights]
    pos = [mem_pos[0]] + [over_z(mem_pos[0], j) for j in range(1, planes)]
    normed = call(
        functools.partial(norm_kernel, heads, full_width),
        [ids] + blocks,
        [shape((piece, width), bf16)] * (SEGS * planes),
        [pltpu.VMEM((heads, SEGS, piece, width), bf16)],
    )
    y = [w_out, over_z(w_out, 1)]
    parts = []
    last = SEGS - 1
    groups = [((0, 1, 2),)] * last + [((0,), (1, 2))]
    for s in range(SEGS):
        kinds = (seg_rows, mem_rows, mem_rows + PAD)
        counts = [sum(kinds[kind] for kind in group) for group in groups[s]]
        mine = normed[s * planes : (s + 1) * planes]
        held = [mine[0]] + [over_z(mine[j], j) for j in range(1, planes)]
        held = jnp.stack(held)
        pieces = [held] + [over_head(held, m) for m in range(1, heads)]
        parts.append(
            call(
                functools.partial(project_kernel, heads, s, size, groups[s]),
                [ids] + pieces + pos + weights + partner,
                [shape((count, features), bf16) for count in counts for _ in range(planes)],
                [
                    pltpu.VMEM((planes, seg_rows, width), bf16),
                    pltpu.VMEM((planes, mem_rows, width), bf16),
                    pltpu.VMEM((planes, local_heads, mem_rows), f32),
                ],
                flops=2 * planes * width * features * (seg_rows + 2 * mem_rows),
                grid=(features // tile,),
                specs=[whole(v) for v in pieces + pos]
                + [columns_of(v, tile) for v in weights[:3]]
                + [whole(w_beta)]
                + [columns_of(v, tile) for v in weights[:3]]
                + [whole(w_beta)],
                out_specs=[
                    pl.BlockSpec((count, tile), lambda n: (0, n))
                    for count in counts
                    for _ in range(planes)
                ],
            )
        )
    r11, r10 = edge(w_out, 1), edge(y[1], 1)
    r21, r20 = edge(r11, 2), edge(r10, 2)
    outer = (z == 0) | (z == planes - 1)
    y = y + [jnp.where(outer, r21, r10), jnp.where(outer, r20, r11)]
    y_partner = [over_core(v) for v in y]
    add = lambda a, c: (a.astype(f32) + c.astype(f32)).astype(bf16)

    def line_sum(u):
        t03 = edge(u[3], 0)
        t02 = edge(u[2], 0)
        t01 = edge(u[1], 0)
        t13 = edge(add(u[2], t03), 1)
        t12 = edge(add(u[3], t02), 1)
        t23 = edge(add(u[1], t13), 2)
        return [u[0], t01, t12, t23]

    read_shape = shape((seg_rows, features), bf16)
    state_shape = shape(memory_in.shape[1:], f32)

    def emit(readout, s):
        mixed = call(
            functools.partial(out_kernel, heads),
            [ids, readout] + y + y_partner,
            [shape((seg_rows, width), f32)] + [shape((seg_rows, width), bf16)] * (heads - 1),
            [pltpu.VMEM((heads, seg_rows, width), f32)],
            flops=2 * seg_rows * features * full_width,
            grid=(w_out.shape[1] // tile,),
            specs=[whole(readout)] + [columns_of(v, tile) for v in y + y_partner],
            out_specs=[pl.BlockSpec((seg_rows, width), lambda n: (0, 0))] * heads,
        )
        total = mixed[0]
        for m in range(1, heads):
            total = total + over_head(mixed[m], m).astype(f32)
        rows = hidden_in[0, s * seg_rows : (s + 1) * seg_rows].astype(f32)
        return (total + rows).astype(bf16)

    state = memory_in[0]
    outs = []
    for s in range(last):
        sums = line_sum(parts[s])
        readout, state = call(
            functools.partial(both_kernel, 4, seg_rows, mem_rows),
            [ids] + sums + [state],
            [read_shape, state_shape],
            scratch=[pltpu.VMEM(sums[0].shape, f32)],
        )
        outs.append(emit(readout, s))
    sums = line_sum(parts[last][:planes])
    readout = call(
        functools.partial(read_kernel, 4, seg_rows),
        [ids] + sums + [state],
        [read_shape],
        scratch=[pltpu.VMEM(sums[0].shape, f32)],
    )[0]
    outs.append(emit(readout, last))
    sums = line_sum(parts[last][planes:])
    state = call(
        functools.partial(update_kernel, 4, mem_rows),
        [ids] + sums + [state],
        [state_shape],
        scratch=[pltpu.VMEM(sums[0].shape, f32)],
    )[0]
    return (jnp.concatenate(outs, axis=0)[None], state[None])


def solution(mesh):
    heads, batch = mesh.shape["head"], mesh.shape["batch"]
    planes = batch // CORES
    lined = planes == heads == 4

    def body(*arrays):
        if not lined:
            return general_body(*arrays)
        return line_body(planes, heads, *arrays)

    in_specs = (
        P("batch", None, "head"),
        P("batch", "head"),
        P("batch", "head"),
        P("batch", "head"),
        P("batch", "head"),
        P("head", "batch"),
        P("batch", None, None),
        P("batch", "head", None, None),
    )
    out_specs = (P("batch", None, "head"), P("batch", "head", None, None))
    return jax.shard_map(body, mesh=mesh, in_specs=in_specs, out_specs=out_specs, check_vma=False)
```

profile of v0, /device:TPU:0, one launch (start us, length us, event | category | flops | bytes accessed | tf_op | source)
XLA Modules:
  0.0 264.6 jit_solution(9089020853624973567)
XLA Ops:
  0.7 1.9 dynamic-slice_bitcast_fusion
  2.6 3.0 %collective-permute-start = (bf16[2,32,1024]{2,1,0:T(8,128)(2,1)S(1)}, bf16[2,32,1024]{2,1,0:T(8,128)(2,1)S(1)}, u32[]{:S(2)}, u32[]{:S(2)}) collective-permute-start(bf16[2,32,1024]{2,1,0:T(8,128)(2,1)S(1)} %get-tuple-element.66), channel_id=1, source_target_pairs={{0,8},{8,0},{16,24},{24,16},{1,9},{9,1},{17,25},{25,17},{2,10},{10... | collective-permute-start | bytes 393224 | tf_op jit(solution)/shard_map/ppermute | solution.py:296
  5.5 1.5 collective-permute-start.1
  7.7 1.7 collective-permute-done.refs_1_
  9.4 3.9 %collective-permute-done.1.refs_2_ = bf16[2,32,1024]{2,1,0:T(8,128)(2,1)S(1)} collective-permute-done((bf16[2,32,1024]{2,1,0:T(8,128)(2,1)S(1)}, bf16[2,32,1024]{2,1,0:T(8,128)(2,1)S(1)}, u32[]{:S(2)}, u32[]{:S(2)}) %collective-permute-start.1) | collective-permute-done | bytes 131104 | tf_op jit(solution)/shard_map/ppermute | solution.py:296
  14.0 2.2 shard_map.95
  16.2 1.6 collective-permute-start.34
  17.8 2.6 collective-permute-start.35
  21.1 3.5 %collective-permute-done.35 = bf16[32,1024]{1,0:T(8,128)(2,1)S(1)} collective-permute-done((bf16[32,1024]{1,0:T(8,128)(2,1)}, bf16[32,1024]{1,0:T(8,128)(2,1)S(1)}, u32[]{:S(2)}, u32[]{:S(2)}) %collective-permute-start.35) | collective-permute-done | bytes 65568 | tf_op jit(solution)/shard_map/ppermute | solution.py:300
  24.6 2.1 collective-permute-done.36
  26.6 0.9 pad_maximum_fusion.1.refs_0_
  27.5 1.2 collective-permute-start.37
  28.8 1.5 collective-permute-start.4
  30.3 2.9 %collective-permute-start.5 = (bf16[32,1024]{1,0:T(8,128)(2,1)}, bf16[32,1024]{1,0:T(8,128)(2,1)S(1)}, u32[]{:S(2)}, u32[]{:S(2)}) collective-permute-start(bf16[32,1024]{1,0:T(8,128)(2,1)} %get-tuple-element.35), channel_id=1, source_target_pairs={{0,6},{1,7},{2,4},{3,5},{4,2},{5,3},{6,0},{7,1},{8,14},{9,15},{10,... | collective-permute-start | bytes 196616 | tf_op jit(solution)/shard_map/ppermute | solution.py:300
  33.2 18.5 %collective-permute-done.10.refs_6_ = s32[2,64]{1,0:T(2,128)S(1)} collective-permute-done((s32[2,64]{1,0:T(2,128)S(1)}, s32[2,64]{1,0:T(2,128)S(1)}, u32[]{:S(2)}, u32[]{:S(2)}) %collective-permute-start.10) | collective-permute-done | bytes 544 | tf_op jit(solution)/shard_map/ppermute | solution.py:300
  51.7 1.3 collective-permute-start.11
  53.0 4.1 %collective-permute-done.11.refs_7_ = s32[2,64]{1,0:T(2,128)S(1)} collective-permute-done((s32[2,64]{1,0:T(2,128)S(1)}, s32[2,64]{1,0:T(2,128)S(1)}, u32[]{:S(2)}, u32[]{:S(2)}) %collective-permute-start.11) | collective-permute-done | bytes 544 | tf_op jit(solution)/shard_map/ppermute | solution.py:300
  57.7 3.0 %collective-permute-done.9.refs_5_ = s32[2,64]{1,0:T(2,128)} collective-permute-done((s32[2,64]{1,0:T(2,128)S(1)}, s32[2,64]{1,0:T(2,128)}, u32[]{:S(2)}, u32[]{:S(2)}) %collective-permute-start.9) | collective-permute-done | bytes 544 | tf_op jit(solution)/shard_map/ppermute | solution.py:300
  60.7 1.3 collective-permute-done.15.refs_15_
  62.7 0.9 collective-permute-start.38
  63.6 2.9 %collective-permute-done.3 = bf16[32,1024]{1,0:T(8,128)(2,1)S(1)} collective-permute-done((bf16[32,1024]{1,0:T(8,128)(2,1)}, bf16[32,1024]{1,0:T(8,128)(2,1)S(1)}, u32[]{:S(2)}, u32[]{:S(2)}) %collective-permute-start.3) | collective-permute-done | bytes 65568 | tf_op jit(solution)/shard_map/ppermute | solution.py:300
  67.1 4.0 %collective-permute-done.38.refs_2_ = bf16[4,32,1024]{2,1,0:T(8,128)(2,1)S(1)} collective-permute-done((bf16[4,32,1024]{2,1,0:T(8,128)(2,1)S(1)}, bf16[4,32,1024]{2,1,0:T(8,128)(2,1)S(1)}, u32[]{:S(2)}, u32[]{:S(2)}) %collective-permute-start.38) | collective-permute-done | bytes 262176 | tf_op jit(solution)/shard_map/ppermute | solution.py:296
  71.1 0.9 collective-permute-start.39
  72.0 7.5 %collective-permute-done.39.refs_3_ = bf16[4,32,1024]{2,1,0:T(8,128)(2,1)S(1)} collective-permute-done((bf16[4,32,1024]{2,1,0:T(8,128)(2,1)S(1)}, bf16[4,32,1024]{2,1,0:T(8,128)(2,1)S(1)}, u32[]{:S(2)}, u32[]{:S(2)}) %collective-permute-start.39) | collective-permute-done | bytes 262176 | tf_op jit(solution)/shard_map/ppermute | solution.py:296
  81.0 1.7 pad_maximum_fusion.refs_0_
  82.7 0.9 collective-permute-start.6
  84.1 2.1 collective-permute-start.8
  86.2 7.3 %shard_map.99 = (bf16[128,1024]{1,0:T(8,128)(2,1)}, bf16[128,1024]{1,0:T(8,128)(2,1)}, bf16[128,1024]{1,0:T(8,128)(2,1)}, bf16[128,1024]{1,0:T(8,128)(2,1)}, bf1...) custom-call(s32[3]{0:T(128)} %pad_add_fusion.ids, ...), custom_call_target="tpu_custom_call" | custom-call | flops 2147483648 | bytes 9521152 | tf_op jit(solution)/shard_map/pallas_call | solution.py:80
  93.5 7.9 %collective-permute-start.43 = (bf16[128,1024]{1,0:T(8,128)(2,1)}, bf16[128,1024]{1,0:T(8,128)(2,1)}, u32[]{:S(2)}, u32[]{:S(2)}) collective-permute-start(bf16[128,1024]{1,0:T(8,128)(2,1)} %get-tuple-element.51), channel_id=1, source_target_pairs={{0,2},{6,4},{1,3},{7,5},{8,10},{14,12},{9,11},{15,13},{16,18},{22,... | collective-permute-start | bytes 786440 | tf_op jit(solution)/shard_map/ppermute | solution.py:310
  101.4 1.3 collective-permute-start.52
  102.7 2.0 collective-permute-start.41
  104.7 7.4 %shard_map.96 = (bf16[264,1024]{1,0:T(8,128)(2,1)}, bf16[264,1024]{1,0:T(8,128)(2,1)}, bf16[264,1024]{1,0:T(8,128)(2,1)}, bf16[264,1024]{1,0:T(8,128)(2,1)}) custom-call(s32[3]{0:T(128)} %pad_add_fusion.ids, bf16[4,32,1024]{2,1,0:T(8,128)(2,1)} %pad_maximum_fusion.refs_0_, bf16[4,32,1024]{2,1,0:T(8,128)(2,1)} %collective-permute-done.6.refs_1_, ...), custom_call_target="tpu_custom_call" | custom-call | flops 2147483648 | bytes 9521152 | tf_op jit(solution)/shard_map/pallas_call | solution.py:80
  112.2 1.5 collective-permute-start.19
  113.6 1.3 collective-permute-start.24
  114.9 1.1 add_convert_fusion.7
  116.0 3.2 %collective-permute-done.41 = bf16[128,1024]{1,0:T(8,128)(2,1)} collective-permute-done((bf16[128,1024]{1,0:T(8,128)(2,1)}, bf16[128,1024]{1,0:T(8,128)(2,1)}, u32[]{:S(2)}, u32[]{:S(2)}) %collective-permute-start.41) | collective-permute-done | bytes 262176 | tf_op jit(solution)/shard_map/ppermute | solution.py:310
  119.3 4.4 %collective-permute-start.17 = (bf16[264,1024]{1,0:T(8,128)(2,1)}, bf16[264,1024]{1,0:T(8,128)(2,1)S(1)}, u32[]{:S(2)}, u32[]{:S(2)}) collective-permute-start(bf16[264,1024]{1,0:T(8,128)(2,1)} %get-tuple-element.39), channel_id=1, source_target_pairs={{0,2},{6,4},{1,3},{7,5},{8,10},{14,12},{9,11},{15,13},{16,18},{22,... | collective-permute-start | bytes 1622024 | tf_op jit(solution)/shard_map/ppermute | solution.py:310
  123.7 1.1 add_convert_fusion.8
  124.8 1.4 collective-permute-start.50
  126.3 1.3 collective-permute-start.26
  127.7 3.2 %collective-permute-done.19 = bf16[264,1024]{1,0:T(8,128)(2,1)S(1)} collective-permute-done((bf16[264,1024]{1,0:T(8,128)(2,1)}, bf16[264,1024]{1,0:T(8,128)(2,1)S(1)}, u32[]{:S(2)}, u32[]{:S(2)}) %collective-permute-start.19) | collective-permute-done | bytes 540704 | tf_op jit(solution)/shard_map/ppermute | solution.py:310
  130.9 4.3 %collective-permute-start.16 = (bf16[264,1024]{1,0:T(8,128)(2,1)S(1)}, bf16[264,1024]{1,0:T(8,128)(2,1)S(1)}, u32[]{:S(2)}, u32[]{:S(2)}) collective-permute-start(bf16[264,1024]{1,0:T(8,128)(2,1)S(1)} %copy-done.6), channel_id=1, source_target_pairs={{0,2},{6,4},{1,3},{7,5},{8,10},{14,12},{9,11},{15,13},{16,18},{22,... | collective-permute-start | bytes 1622024 | tf_op jit(solution)/shard_map/ppermute | solution.py:310
  135.4 7.1 %collective-permute-done.17 = bf16[264,1024]{1,0:T(8,128)(2,1)S(1)} collective-permute-done((bf16[264,1024]{1,0:T(8,128)(2,1)}, bf16[264,1024]{1,0:T(8,128)(2,1)S(1)}, u32[]{:S(2)}, u32[]{:S(2)}) %collective-permute-start.17) | collective-permute-done | bytes 540704 | tf_op jit(solution)/shard_map/ppermute | solution.py:310
  142.5 4.3 %collective-permute-start.40 = (bf16[128,1024]{1,0:T(8,128)(2,1)S(1)}, bf16[128,1024]{1,0:T(8,128)(2,1)S(1)}, u32[]{:S(2)}, u32[]{:S(2)}) collective-permute-start(bf16[128,1024]{1,0:T(8,128)(2,1)S(1)} %copy-done.20), channel_id=1, source_target_pairs={{0,2},{6,4},{1,3},{7,5},{8,10},{14,12},{9,11},{15,13},{16,18},{22,... | collective-permute-start | bytes 786440 | tf_op jit(solution)/shard_map/ppermute | solution.py:310
  147.0 14.3 %collective-permute-done.40.refs_1_ = bf16[128,1024]{1,0:T(8,128)(2,1)S(1)} collective-permute-done((bf16[128,1024]{1,0:T(8,128)(2,1)S(1)}, bf16[128,1024]{1,0:T(8,128)(2,1)S(1)}, u32[]{:S(2)}, u32[]{:S(2)}) %collective-permute-start.40) | collective-permute-done | bytes 262176 | tf_op jit(solution)/shard_map/ppermute | solution.py:310
  166.5 1.4 collective-permute-start.21
  168.0 46.9 %collective-permute-done.21.refs_3_ = bf16[264,1024]{1,0:T(8,128)(2,1)S(1)} collective-permute-done((bf16[264,1024]{1,0:T(8,128)(2,1)S(1)}, bf16[264,1024]{1,0:T(8,128)(2,1)S(1)}, u32[]{:S(2)}, u32[]{:S(2)}) %collective-permute-start.21) | collective-permute-done | bytes 540704 | tf_op jit(solution)/shard_map/ppermute | solution.py:310
  214.9 1.3 collective-permute-start.45
  216.2 0.8 add_convert_fusion.5
  217.8 5.1 %shard_map.97 = (bf16[128,1024]{1,0:T(8,128)(2,1)}, f32[8,128,128]{2,1,0:T(8,128)}) custom-call(s32[3]{0:T(128)} %pad_add_fusion.ids, bf16[264,1024]{1,0:T(8,128)(2,1)} %get-tuple-element.36.refs_0_, bf16[264,1024]{1,0:T(8,128)(2,1)} %copy-done.9, bf16[264,1024]{1,0:T(8,128)(2,1)} %copy-done.10, bf16[264,1024]{1,0:T(8,128)(2,1)} %copy-done.11, ...), custom_call_target="tpu_custom_call" | custom-call | bytes 3473408 | tf_op jit(solution)/shard_map/pallas_call | solution.py:80
  223.3 5.1 %collective-permute-start.49 = (bf16[136,1024]{1,0:T(8,128)(2,1)}, bf16[136,1024]{1,0:T(8,128)(2,1)S(1)}, u32[]{:S(2)}, u32[]{:S(2)}) collective-permute-start(bf16[136,1024]{1,0:T(8,128)(2,1)} %get-tuple-element.59), channel_id=1, source_target_pairs={{0,2},{6,4},{1,3},{7,5},{8,10},{14,12},{9,11},{15,13},{16,18},{22,... | collective-permute-start | bytes 835592 | tf_op jit(solution)/shard_map/ppermute | solution.py:310
  228.4 3.3 %shard_map.100.refs_0_ = bf16[128,1024]{1,0:T(8,128)(2,1)} custom-call(s32[3]{0:T(128)} %pad_add_fusion.ids, bf16[128,1024]{1,0:T(8,128)(2,1)} %get-tuple-element.49.refs_0_, bf16[128,1024]{1,0:T(8,128)(2,1)} %copy-done.22, bf16[128,1024]{1,0:T(8,128)(2,1)} %copy-done.23, bf16[128,1024]{1,0:T(8,128)(2,1)} %collective-permute-done.45.refs_3_, ...), custom_call_target="tpu_custom_call" | custom-call | bytes 1835008 | tf_op jit(solution)/shard_map/pallas_call | solution.py:80
  232.4 1.3 collective-permute-start.54
  233.7 5.6 %shard_map.101 = (f32[128,1024]{1,0:T(8,128)}, bf16[128,1024]{1,0:T(8,128)(2,1)}, bf16[128,1024]{1,0:T(8,128)(2,1)}, bf16[128,1024]{1,0:T(8,128)(2,1)}) custom-call(s32[3]{0:T(128)} %pad_add_fusion.ids, bf16[128,1024]{1,0:T(8,128)(2,1)} %shard_map.100.refs_0_, bf16[1024,512]{1,0:T(8,128)(2,1)} %refs_1_.3, bf16[1024,512]{1,0:T(8,128)(2,1)} %collective-permute-done.22.refs_2_, ...), custom_call_target="tpu_custom_call" | custom-call | flops 1073741824 | bytes 9961472 | tf_op jit(solution)/shard_map/pallas_call | solution.py:80
  239.3 0.9 collective-permute-start.46
  240.8 5.5 %shard_map.98 = (f32[128,1024]{1,0:T(8,128)}, bf16[128,1024]{1,0:T(8,128)(2,1)}, bf16[128,1024]{1,0:T(8,128)(2,1)}, bf16[128,1024]{1,0:T(8,128)(2,1)}) custom-call(s32[3]{0:T(128)} %pad_add_fusion.ids, bf16[128,1024]{1,0:T(8,128)(2,1)} %get-tuple-element.40.refs_0_, bf16[1024,512]{1,0:T(8,128)(2,1)} %refs_1_.3, ...), custom_call_target="tpu_custom_call" | custom-call | flops 1073741824 | bytes 9961472 | tf_op jit(solution)/shard_map/pallas_call | solution.py:80
  246.3 2.1 collective-permute-start.48
  248.5 0.9 collective-permute-start.31
  249.9 2.1 collective-permute-start.33
  252.0 3.9 %shard_map.102 = f32[8,128,128]{2,1,0:T(8,128)} custom-call(s32[3]{0:T(128)} %pad_add_fusion.ids, bf16[136,1024]{1,0:T(8,128)(2,1)} %get-tuple-element.58.refs_0_, bf16[136,1024]{1,0:T(8,128)(2,1)} %copy-done.14, bf16[136,1024]{1,0:T(8,128)(2,1)} %copy-done.15, bf16[136,1024]{1,0:T(8,128)(2,1)} %copy-done.16, f32[8,128,128]{2,1,0:T(8,128)} %get-tuple-element.53.refs_4_), custom_call_target="tpu_custom_call" | custom-call | bytes 2162688 | tf_op jit(solution)/shard_map/pallas_call | solution.py:80
  255.9 0.9 collective-permute-done.48
  256.8 3.2 %collective-permute-done.31 = bf16[128,1024]{1,0:T(8,128)(2,1)S(1)} collective-permute-done((bf16[128,1024]{1,0:T(8,128)(2,1)}, bf16[128,1024]{1,0:T(8,128)(2,1)S(1)}, u32[]{:S(2)}, u32[]{:S(2)}) %collective-permute-start.31) | collective-permute-done | bytes 262176 | tf_op jit(solution)/shard_map/ppermute | solution.py:296
  260.0 3.3 %collective-permute-done.32 = bf16[128,1024]{1,0:T(8,128)(2,1)S(1)} collective-permute-done((bf16[128,1024]{1,0:T(8,128)(2,1)}, bf16[128,1024]{1,0:T(8,128)(2,1)S(1)}, u32[]{:S(2)}, u32[]{:S(2)}) %collective-permute-start.32) | collective-permute-done | bytes 262176 | tf_op jit(solution)/shard_map/ppermute | solution.py:296
  263.8 0.8 maximum_bitcast_fusion
  (148 shorter events, 14.9 us)
Async XLA Ops:
  0.6 28.1 %copy-start.2 = (bf16[1024,512]{1,0:T(8,128)(2,1)S(1)}, bf16[1024,512]{1,0:T(8,128)(2,1)}, u32[]{:S(2)}) copy-start(bf16[1024,512]{1,0:T(8,128)(2,1)} %refs_1_.3) | copy-start | bytes 3145732
  0.7 32.5 %copy-start.35 = (s32[1,2,64]{2,1,0:T(2,128)S(1)}, s32[1,2,64]{2,1,0:T(2,128)}, u32[]{:S(2)}) copy-start(s32[1,2,64]{2,1,0:T(2,128)} %param.14) | copy-start | bytes 1540
  0.7 56.8 %copy-start.30 = (bf16[512,8]{0,1:T(8,128)(2,1)S(1)}, bf16[512,8]{0,1:T(8,128)(2,1)}, u32[]{:S(2)}) copy-start(bf16[512,8]{0,1:T(8,128)(2,1)} %param.12) | copy-start | bytes 24580
  2.6 6.9 %collective-permute-start = (bf16[2,32,1024]{2,1,0:T(8,128)(2,1)S(1)}, bf16[2,32,1024]{2,1,0:T(8,128)(2,1)S(1)}, u32[]{:S(2)}, u32[]{:S(2)}) collective-permute-start(bf16[2,32,1024]{2,1,0:T(8,128)(2,1)S(1)} %get-tuple-element.66), channel_id=1, source_target_pairs={{0,8},{8,0},{16,24},{24,16},{1,9},{9,1},{17,25},{25,17},{2,10},{10... | collective-permute-start | bytes 393224 | tf_op jit(solution)/shard_map/ppermute | solution.py:296
  5.5 7.8 %collective-permute-start.1 = (bf16[2,32,1024]{2,1,0:T(8,128)(2,1)S(1)}, bf16[2,32,1024]{2,1,0:T(8,128)(2,1)S(1)}, u32[]{:S(2)}, u32[]{:S(2)}) collective-permute-start(bf16[2,32,1024]{2,1,0:T(8,128)(2,1)S(1)} %get-tuple-element.65), channel_id=1, source_target_pairs={{0,16},{8,24},{16,0},{24,8},{1,17},{9,25},{17,1},{25,9},{2,18},{10... | collective-permute-start | bytes 393224 | tf_op jit(solution)/shard_map/ppermute | solution.py:296
  7.1 6.3 %collective-permute-start.2 = (bf16[2,32,1024]{2,1,0:T(8,128)(2,1)S(1)}, bf16[2,32,1024]{2,1,0:T(8,128)(2,1)S(1)}, u32[]{:S(2)}, u32[]{:S(2)}) collective-permute-start(bf16[2,32,1024]{2,1,0:T(8,128)(2,1)S(1)} %get-tuple-element.64), channel_id=1, source_target_pairs={{0,24},{8,16},{16,8},{24,0},{1,25},{9,17},{17,9},{25,1},{2,26},{10... | collective-permute-start | bytes 393224 | tf_op jit(solution)/shard_map/ppermute | solution.py:296
  16.2 4.9 %collective-permute-start.34 = (bf16[32,1024]{1,0:T(8,128)(2,1)}, bf16[32,1024]{1,0:T(8,128)(2,1)S(1)}, u32[]{:S(2)}, u32[]{:S(2)}) collective-permute-start(bf16[32,1024]{1,0:T(8,128)(2,1)} %get-tuple-element.46), channel_id=1, source_target_pairs={{0,2},{1,3},{2,0},{3,1},{4,6},{5,7},{6,4},{7,5},{8,10},{9,11},{10,... | collective-permute-start | bytes 196616 | tf_op jit(solution)/shard_map/ppermute | solution.py:300
  17.8 6.8 %collective-permute-start.35 = (bf16[32,1024]{1,0:T(8,128)(2,1)}, bf16[32,1024]{1,0:T(8,128)(2,1)S(1)}, u32[]{:S(2)}, u32[]{:S(2)}) collective-permute-start(bf16[32,1024]{1,0:T(8,128)(2,1)} %get-tuple-element.47), channel_id=1, source_target_pairs={{0,4},{1,5},{2,6},{3,7},{4,0},{5,1},{6,2},{7,3},{8,12},{9,13},{10,... | collective-permute-start | bytes 196616 | tf_op jit(solution)/shard_map/ppermute | solution.py:300
  20.4 6.3 %collective-permute-start.36 = (bf16[32,1024]{1,0:T(8,128)(2,1)}, bf16[32,1024]{1,0:T(8,128)(2,1)S(1)}, u32[]{:S(2)}, u32[]{:S(2)}) collective-permute-start(bf16[32,1024]{1,0:T(8,128)(2,1)} %get-tuple-element.48), channel_id=1, source_target_pairs={{0,6},{1,7},{2,4},{3,5},{4,2},{5,3},{6,0},{7,1},{8,14},{9,15},{10,... | collective-permute-start | bytes 196616 | tf_op jit(solution)/shard_map/ppermute | solution.py:300
  27.5 58.7 %copy-start.21 = (bf16[4,32,1024]{2,1,0:T(8,128)(2,1)}, bf16[4,32,1024]{2,1,0:T(8,128)(2,1)S(1)}, u32[]{:S(2)}) copy-start(bf16[4,32,1024]{2,1,0:T(8,128)(2,1)S(1)} %pad_maximum_fusion.1.refs_0_) | copy-start | bytes 786436
  27.5 39.0 %collective-permute-start.37 = (bf16[4,32,1024]{2,1,0:T(8,128)(2,1)S(1)}, bf16[4,32,1024]{2,1,0:T(8,128)(2,1)S(1)}, u32[]{:S(2)}, u32[]{:S(2)}) collective-permute-start(bf16[4,32,1024]{2,1,0:T(8,128)(2,1)S(1)} %pad_maximum_fusion.1.refs_0_), channel_id=1, source_target_pairs={{0,8},{8,0},{16,24},{24,16},{1,9},{9,1},{17,25},{25,17},{2,10},{10... | collective-permute-start | bytes 786440 | tf_op jit(solution)/shard_map/ppermute | solution.py:296
  28.8 51.5 %collective-permute-start.22 = (bf16[1024,512]{1,0:T(8,128)(2,1)S(1)}, bf16[1024,512]{1,0:T(8,128)(2,1)}, u32[]{:S(2)}, u32[]{:S(2)}) collective-permute-start(bf16[1024,512]{1,0:T(8,128)(2,1)S(1)} %copy-done.2), channel_id=1, source_target_pairs={{0,2},{1,3},{2,0},{3,1},{4,6},{5,7},{6,4},{7,5},{8,10},{9,11},{10,... | collective-permute-start | bytes 3145736 | tf_op jit(solution)/shard_map/ppermute | solution.py:300
  28.8 34.0 %collective-permute-start.4 = (bf16[32,1024]{1,0:T(8,128)(2,1)}, bf16[32,1024]{1,0:T(8,128)(2,1)S(1)}, u32[]{:S(2)}, u32[]{:S(2)}) collective-permute-start(bf16[32,1024]{1,0:T(8,128)(2,1)} %get-tuple-element.34), channel_id=1, source_target_pairs={{0,4},{1,5},{2,6},{3,7},{4,0},{5,1},{6,2},{7,3},{8,12},{9,13},{10,... | collective-permute-start | bytes 196616 | tf_op jit(solution)/shard_map/ppermute | solution.py:300
  30.3 33.3 %collective-permute-start.5 = (bf16[32,1024]{1,0:T(8,128)(2,1)}, bf16[32,1024]{1,0:T(8,128)(2,1)S(1)}, u32[]{:S(2)}, u32[]{:S(2)}) collective-permute-start(bf16[32,1024]{1,0:T(8,128)(2,1)} %get-tuple-element.35), channel_id=1, source_target_pairs={{0,6},{1,7},{2,4},{3,5},{4,2},{5,3},{6,0},{7,1},{8,14},{9,15},{10,... | collective-permute-start | bytes 196616 | tf_op jit(solution)/shard_map/ppermute | solution.py:300
  33.2 18.5 %collective-permute-start.10 = (s32[2,64]{1,0:T(2,128)S(1)}, s32[2,64]{1,0:T(2,128)S(1)}, u32[]{:S(2)}, u32[]{:S(2)}) collective-permute-start(s32[2,64]{1,0:T(2,128)S(1)} %bitcast.52), channel_id=1, source_target_pairs={{0,4},{1,5},{2,6},{3,7},{4,0},{5,1},{6,2},{7,3},{8,12},{9,13},{10,... | collective-permute-start | bytes 1544 | tf_op jit(solution)/shard_map/ppermute | solution.py:300
  51.7 34.5 %copy-start.36 = (s32[2,64]{1,0:T(2,128)}, s32[2,64]{1,0:T(2,128)S(1)}, u32[]{:S(2)}) copy-start(s32[2,64]{1,0:T(2,128)S(1)} %collective-permute-done.10.refs_6_) | copy-start | bytes 1540
  51.7 5.4 %collective-permute-start.11 = (s32[2,64]{1,0:T(2,128)S(1)}, s32[2,64]{1,0:T(2,128)S(1)}, u32[]{:S(2)}, u32[]{:S(2)}) collective-permute-start(s32[2,64]{1,0:T(2,128)S(1)} %bitcast.53), channel_id=1, source_target_pairs={{0,6},{1,7},{2,4},{3,5},{4,2},{5,3},{6,0},{7,1},{8,14},{9,15},{10,... | collective-permute-start | bytes 1544 | tf_op jit(solution)/shard_map/ppermute | solution.py:300
  57.1 3.7 %collective-permute-start.9 = (s32[2,64]{1,0:T(2,128)S(1)}, s32[2,64]{1,0:T(2,128)}, u32[]{:S(2)}, u32[]{:S(2)}) collective-permute-start(s32[2,64]{1,0:T(2,128)S(1)} %bitcast.54), channel_id=1, source_target_pairs={{0,2},{1,3},{2,0},{3,1},{4,6},{5,7},{6,4},{7,5},{8,10},{9,11},{10,... | collective-permute-start | bytes 1544 | tf_op jit(solution)/shard_map/ppermute | solution.py:300
  57.7 28.5 %copy-start.27 = (bf16[512,8]{1,0:T(8,128)(2,1)}, bf16[512,8]{1,0:T(8,128)(2,1)S(1)}, u32[]{:S(2)}) copy-start(bf16[512,8]{1,0:T(8,128)(2,1)S(1)} %copy.15.refs_11_) | copy-start | bytes 24580
  60.7 1.3 collective-permute-start.15
  62.1 4.5 %collective-permute-start.3 = (bf16[32,1024]{1,0:T(8,128)(2,1)}, bf16[32,1024]{1,0:T(8,128)(2,1)S(1)}, u32[]{:S(2)}, u32[]{:S(2)}) collective-permute-start(bf16[32,1024]{1,0:T(8,128)(2,1)} %get-tuple-element.33), channel_id=1, source_target_pairs={{0,2},{1,3},{2,0},{3,1},{4,6},{5,7},{6,4},{7,5},{8,10},{9,11},{10,... | collective-permute-start | bytes 196616 | tf_op jit(solution)/shard_map/ppermute | solution.py:300
  62.7 8.4 %collective-permute-start.38 = (bf16[4,32,1024]{2,1,0:T(8,128)(2,1)S(1)}, bf16[4,32,1024]{2,1,0:T(8,128)(2,1)S(1)}, u32[]{:S(2)}, u32[]{:S(2)}) collective-permute-start(bf16[4,32,1024]{2,1,0:T(8,128)(2,1)S(1)} %pad_maximum_fusion.1.refs_0_), channel_id=1, source_target_pairs={{0,16},{8,24},{16,0},{24,8},{1,17},{9,25},{17,1},{25,9},{2,18},{10... | collective-permute-start | bytes 786440 | tf_op jit(solution)/shard_map/ppermute | solution.py:296
  63.6 19.1 %collective-permute-start.12 = (bf16[512,1024]{1,0:T(8,128)(2,1)}, bf16[512,1024]{1,0:T(8,128)(2,1)}, u32[]{:S(2)}, u32[]{:S(2)}) collective-permute-start(bf16[512,1024]{1,0:T(8,128)(2,1)} %refs_8_.3), channel_id=1, source_target_pairs={{0,1},{1,0},{2,3},{3,2},{4,5},{5,4},{6,7},{7,6},{8,9},{9,8},{10,11... | collective-permute-start | bytes 3145736 | tf_op jit(solution)/shard_map/ppermute | solution.py:303
  66.6 17.0 %collective-permute-start.13 = (bf16[512,1024]{1,0:T(8,128)(2,1)}, bf16[512,1024]{1,0:T(8,128)(2,1)}, u32[]{:S(2)}, u32[]{:S(2)}) collective-permute-start(bf16[512,1024]{1,0:T(8,128)(2,1)} %refs_9_.3), channel_id=1, source_target_pairs={{0,1},{1,0},{2,3},{3,2},{4,5},{5,4},{6,7},{7,6},{8,9},{9,8},{10,11... | collective-permute-start | bytes 3145736 | tf_op jit(solution)/shard_map/ppermute | solution.py:303
  66.6 17.5 %collective-permute-start.14 = (bf16[512,1024]{1,0:T(8,128)(2,1)}, bf16[512,1024]{1,0:T(8,128)(2,1)}, u32[]{:S(2)}, u32[]{:S(2)}) collective-permute-start(bf16[512,1024]{1,0:T(8,128)(2,1)} %refs_10_.3), channel_id=1, source_target_pairs={{0,1},{1,0},{2,3},{3,2},{4,5},{5,4},{6,7},{7,6},{8,9},{9,8},{10,11... | collective-permute-start | bytes 3145736 | tf_op jit(solution)/shard_map/ppermute | solution.py:303
  71.1 8.4 %collective-permute-start.39 = (bf16[4,32,1024]{2,1,0:T(8,128)(2,1)S(1)}, bf16[4,32,1024]{2,1,0:T(8,128)(2,1)S(1)}, u32[]{:S(2)}, u32[]{:S(2)}) collective-permute-start(bf16[4,32,1024]{2,1,0:T(8,128)(2,1)S(1)} %pad_maximum_fusion.1.refs_0_), channel_id=1, source_target_pairs={{0,24},{8,16},{16,8},{24,0},{1,25},{9,17},{17,9},{25,1},{2,26},{10... | collective-permute-start | bytes 786440 | tf_op jit(solution)/shard_map/ppermute | solution.py:296
  79.5 32.6 %collective-permute-start.23 = (bf16[1024,512]{1,0:T(8,128)(2,1)S(1)}, bf16[1024,512]{1,0:T(8,128)(2,1)S(1)}, u32[]{:S(2)}, u32[]{:S(2)}) collective-permute-start(bf16[1024,512]{1,0:T(8,128)(2,1)S(1)} %copy-done.2), channel_id=1, source_target_pairs={{2,4},{4,2},{3,5},{5,3},{10,12},{12,10},{11,13},{13,11},{18,20},{2... | collective-permute-start | bytes 3145736 | tf_op jit(solution)/shard_map/ppermute | solution.py:310
  80.3 46.0 %collective-permute-start.25 = (bf16[1024,512]{1,0:T(8,128)(2,1)}, bf16[1024,512]{1,0:T(8,128)(2,1)S(1)}, u32[]{:S(2)}, u32[]{:S(2)}) collective-permute-start(bf16[1024,512]{1,0:T(8,128)(2,1)} %collective-permute-done.22.refs_2_), channel_id=1, source_target_pairs={{2,4},{4,2},{3,5},{5,3},{10,12},{12,10},{11,13},{13,11},{18,20},{2... | collective-permute-start | bytes 3145736 | tf_op jit(solution)/shard_map/ppermute | solution.py:310
  82.7 10.8 %collective-permute-start.6 = (bf16[4,32,1024]{2,1,0:T(8,128)(2,1)}, bf16[4,32,1024]{2,1,0:T(8,128)(2,1)}, u32[]{:S(2)}, u32[]{:S(2)}) collective-permute-start(bf16[4,32,1024]{2,1,0:T(8,128)(2,1)} %pad_maximum_fusion.refs_0_), channel_id=1, source_target_pairs={{0,8},{8,0},{16,24},{24,16},{1,9},{9,1},{17,25},{25,17},{2,10},{10... | collective-permute-start | bytes 786440 | tf_op jit(solution)/shard_map/ppermute | solution.py:296
  83.5 17.9 %collective-permute-start.7 = (bf16[4,32,1024]{2,1,0:T(8,128)(2,1)}, bf16[4,32,1024]{2,1,0:T(8,128)(2,1)}, u32[]{:S(2)}, u32[]{:S(2)}) collective-permute-start(bf16[4,32,1024]{2,1,0:T(8,128)(2,1)} %pad_maximum_fusion.refs_0_), channel_id=1, source_target_pairs={{0,16},{8,24},{16,0},{24,8},{1,17},{9,25},{17,1},{25,9},{2,18},{10... | collective-permute-start | bytes 786440 | tf_op jit(solution)/shard_map/ppermute | solution.py:296
  84.1 18.6 %collective-permute-start.8 = (bf16[4,32,1024]{2,1,0:T(8,128)(2,1)}, bf16[4,32,1024]{2,1,0:T(8,128)(2,1)}, u32[]{:S(2)}, u32[]{:S(2)}) collective-permute-start(bf16[4,32,1024]{2,1,0:T(8,128)(2,1)} %pad_maximum_fusion.refs_0_), channel_id=1, source_target_pairs={{0,24},{8,16},{16,8},{24,0},{1,25},{9,17},{17,9},{25,1},{2,26},{10... | collective-permute-start | bytes 786440 | tf_op jit(solution)/shard_map/ppermute | solution.py:296
  93.5 20.1 %collective-permute-start.43 = (bf16[128,1024]{1,0:T(8,128)(2,1)}, bf16[128,1024]{1,0:T(8,128)(2,1)}, u32[]{:S(2)}, u32[]{:S(2)}) collective-permute-start(bf16[128,1024]{1,0:T(8,128)(2,1)} %get-tuple-element.51), channel_id=1, source_target_pairs={{0,2},{6,4},{1,3},{7,5},{8,10},{14,12},{9,11},{15,13},{16,18},{22,... | collective-permute-start | bytes 786440 | tf_op jit(solution)/shard_map/ppermute | solution.py:310
  101.4 23.4 %collective-permute-start.52 = (bf16[136,1024]{1,0:T(8,128)(2,1)}, bf16[136,1024]{1,0:T(8,128)(2,1)S(1)}, u32[]{:S(2)}, u32[]{:S(2)}) collective-permute-start(bf16[136,1024]{1,0:T(8,128)(2,1)} %get-tuple-element.60), channel_id=1, source_target_pairs={{0,2},{6,4},{1,3},{7,5},{8,10},{14,12},{9,11},{15,13},{16,18},{22,... | collective-permute-start | bytes 835592 | tf_op jit(solution)/shard_map/ppermute | solution.py:310
  102.7 16.6 %collective-permute-start.41 = (bf16[128,1024]{1,0:T(8,128)(2,1)}, bf16[128,1024]{1,0:T(8,128)(2,1)}, u32[]{:S(2)}, u32[]{:S(2)}) collective-permute-start(bf16[128,1024]{1,0:T(8,128)(2,1)} %get-tuple-element.52), channel_id=1, source_target_pairs={{0,2},{6,4},{1,3},{7,5},{8,10},{14,12},{9,11},{15,13},{16,18},{22,... | collective-permute-start | bytes 786440 | tf_op jit(solution)/shard_map/ppermute | solution.py:310
  112.2 18.7 %collective-permute-start.19 = (bf16[264,1024]{1,0:T(8,128)(2,1)}, bf16[264,1024]{1,0:T(8,128)(2,1)S(1)}, u32[]{:S(2)}, u32[]{:S(2)}) collective-permute-start(bf16[264,1024]{1,0:T(8,128)(2,1)} %get-tuple-element.38), channel_id=1, source_target_pairs={{0,2},{6,4},{1,3},{7,5},{8,10},{14,12},{9,11},{15,13},{16,18},{22,... | collective-permute-start | bytes 1622024 | tf_op jit(solution)/shard_map/ppermute | solution.py:310
  113.6 48.4 %collective-permute-start.24 = (bf16[1024,512]{1,0:T(8,128)(2,1)S(1)}, bf16[1024,512]{1,0:T(8,128)(2,1)S(1)}, u32[]{:S(2)}, u32[]{:S(2)}) collective-permute-start(bf16[1024,512]{1,0:T(8,128)(2,1)S(1)} %collective-permute-done.23), channel_id=1, source_target_pairs={{4,6},{2,0},{5,7},{3,1},{12,14},{10,8},{13,15},{11,9},{20,22},{18,... | collective-permute-start | bytes 3145736 | tf_op jit(solution)/shard_map/ppermute | solution.py:310
  119.3 23.2 %collective-permute-start.17 = (bf16[264,1024]{1,0:T(8,128)(2,1)}, bf16[264,1024]{1,0:T(8,128)(2,1)S(1)}, u32[]{:S(2)}, u32[]{:S(2)}) collective-permute-start(bf16[264,1024]{1,0:T(8,128)(2,1)} %get-tuple-element.39), channel_id=1, source_target_pairs={{0,2},{6,4},{1,3},{7,5},{8,10},{14,12},{9,11},{15,13},{16,18},{22,... | collective-permute-start | bytes 1622024 | tf_op jit(solution)/shard_map/ppermute | solution.py:310
  124.8 38.0 %collective-permute-start.50 = (bf16[136,1024]{1,0:T(8,128)(2,1)S(1)}, bf16[136,1024]{1,0:T(8,128)(2,1)S(1)}, u32[]{:S(2)}, u32[]{:S(2)}) collective-permute-start(bf16[136,1024]{1,0:T(8,128)(2,1)S(1)} %copy-done.19), channel_id=1, source_target_pairs={{0,2},{6,4},{1,3},{7,5},{8,10},{14,12},{9,11},{15,13},{16,18},{22,... | collective-permute-start | bytes 835592 | tf_op jit(solution)/shard_map/ppermute | solution.py:310
  126.3 38.0 %collective-permute-start.26 = (bf16[1024,512]{1,0:T(8,128)(2,1)S(1)}, bf16[1024,512]{1,0:T(8,128)(2,1)S(1)}, u32[]{:S(2)}, u32[]{:S(2)}) collective-permute-start(bf16[1024,512]{1,0:T(8,128)(2,1)S(1)} %collective-permute-done.25), channel_id=1, source_target_pairs={{4,6},{2,0},{5,7},{3,1},{12,14},{10,8},{13,15},{11,9},{20,22},{18,... | collective-permute-start | bytes 3145736 | tf_op jit(solution)/shard_map/ppermute | solution.py:310
  130.9 34.4 %collective-permute-start.16 = (bf16[264,1024]{1,0:T(8,128)(2,1)S(1)}, bf16[264,1024]{1,0:T(8,128)(2,1)S(1)}, u32[]{:S(2)}, u32[]{:S(2)}) collective-permute-start(bf16[264,1024]{1,0:T(8,128)(2,1)S(1)} %copy-done.6), channel_id=1, source_target_pairs={{0,2},{6,4},{1,3},{7,5},{8,10},{14,12},{9,11},{15,13},{16,18},{22,... | collective-permute-start | bytes 1622024 | tf_op jit(solution)/shard_map/ppermute | solution.py:310
  142.5 18.9 %collective-permute-start.40 = (bf16[128,1024]{1,0:T(8,128)(2,1)S(1)}, bf16[128,1024]{1,0:T(8,128)(2,1)S(1)}, u32[]{:S(2)}, u32[]{:S(2)}) collective-permute-start(bf16[128,1024]{1,0:T(8,128)(2,1)S(1)} %copy-done.20), channel_id=1, source_target_pairs={{0,2},{6,4},{1,3},{7,5},{8,10},{14,12},{9,11},{15,13},{16,18},{22,... | collective-permute-start | bytes 786440 | tf_op jit(solution)/shard_map/ppermute | solution.py:310
  161.3 2.3 collective-permute-start.44
  162.0 3.8 %collective-permute-start.20 = (bf16[264,1024]{1,0:T(8,128)(2,1)S(1)}, bf16[264,1024]{1,0:T(8,128)(2,1)S(1)}, u32[]{:S(2)}, u32[]{:S(2)}) collective-permute-start(bf16[264,1024]{1,0:T(8,128)(2,1)S(1)} %add_convert_fusion.1), channel_id=1, source_target_pairs={{2,4},{4,2},{3,5},{5,3},{10,12},{12,10},{11,13},{13,11},{18,20},{2... | collective-permute-start | bytes 1622024 | tf_op jit(solution)/shard_map/ppermute | solution.py:310
  162.9 2.3 collective-permute-start.42
  163.6 2.2 collective-permute-start.53
  164.3 2.2 collective-permute-start.18
  165.1 51.1 %copy-start.18 = (bf16[136,1024]{1,0:T(8,128)(2,1)S(1)}, bf16[136,1024]{1,0:T(8,128)(2,1)}, u32[]{:S(2)}) copy-start(bf16[136,1024]{1,0:T(8,128)(2,1)} %get-tuple-element.60) | copy-start | bytes 835588
  165.1 66.6 %collective-permute-start.27 = (bf16[1024,512]{1,0:T(8,128)(2,1)S(1)}, bf16[1024,512]{1,0:T(8,128)(2,1)}, u32[]{:S(2)}, u32[]{:S(2)}) collective-permute-start(bf16[1024,512]{1,0:T(8,128)(2,1)S(1)} %copy-done.2), channel_id=1, source_target_pairs={{0,1},{1,0},{2,3},{3,2},{4,5},{5,4},{6,7},{7,6},{8,9},{9,8},{10,11... | collective-permute-start | bytes 3145736 | tf_op jit(solution)/shard_map/ppermute | solution.py:303
  165.2 67.1 %collective-permute-start.28 = (bf16[1024,512]{1,0:T(8,128)(2,1)}, bf16[1024,512]{1,0:T(8,128)(2,1)}, u32[]{:S(2)}, u32[]{:S(2)}) collective-permute-start(bf16[1024,512]{1,0:T(8,128)(2,1)} %collective-permute-done.22.refs_2_), channel_id=1, source_target_pairs={{0,1},{1,0},{2,3},{3,2},{4,5},{5,4},{6,7},{7,6},{8,9},{9,8},{10,11... | collective-permute-start | bytes 3145736 | tf_op jit(solution)/shard_map/ppermute | solution.py:303
  165.7 68.0 %collective-permute-start.29 = (bf16[1024,512]{1,0:T(8,128)(2,1)S(1)}, bf16[1024,512]{1,0:T(8,128)(2,1)}, u32[]{:S(2)}, u32[]{:S(2)}) collective-permute-start(bf16[1024,512]{1,0:T(8,128)(2,1)S(1)} %broadcast_select_fusion.1.refs_3_), channel_id=1, source_target_pairs={{0,1},{1,0},{2,3},{3,2},{4,5},{5,4},{6,7},{7,6},{8,9},{9,8},{10,11... | collective-permute-start | bytes 3145736 | tf_op jit(solution)/shard_map/ppermute | solution.py:303
  165.8 67.9 %collective-permute-start.30 = (bf16[1024,512]{1,0:T(8,128)(2,1)S(1)}, bf16[1024,512]{1,0:T(8,128)(2,1)}, u32[]{:S(2)}, u32[]{:S(2)}) collective-permute-start(bf16[1024,512]{1,0:T(8,128)(2,1)S(1)} %broadcast_select_fusion.refs_4_), channel_id=1, source_target_pairs={{0,1},{1,0},{2,3},{3,2},{4,5},{5,4},{6,7},{7,6},{8,9},{9,8},{10,11... | collective-permute-start | bytes 3145736 | tf_op jit(solution)/shard_map/ppermute | solution.py:303
  166.4 50.6 %copy-start.17 = (bf16[136,1024]{1,0:T(8,128)(2,1)S(1)}, bf16[136,1024]{1,0:T(8,128)(2,1)}, u32[]{:S(2)}) copy-start(bf16[136,1024]{1,0:T(8,128)(2,1)} %get-tuple-element.59) | copy-start | bytes 835588
  166.5 51.3 %copy-start.10 = (bf16[264,1024]{1,0:T(8,128)(2,1)}, bf16[264,1024]{1,0:T(8,128)(2,1)S(1)}, u32[]{:S(2)}) copy-start(bf16[264,1024]{1,0:T(8,128)(2,1)S(1)} %collective-permute-done.18.refs_2_) | copy-start | bytes 1622020
  166.5 48.4 %collective-permute-start.21 = (bf16[264,1024]{1,0:T(8,128)(2,1)S(1)}, bf16[264,1024]{1,0:T(8,128)(2,1)S(1)}, u32[]{:S(2)}, u32[]{:S(2)}) collective-permute-start(bf16[264,1024]{1,0:T(8,128)(2,1)S(1)} %add_convert_fusion), channel_id=1, source_target_pairs={{4,6},{2,0},{5,7},{3,1},{12,14},{10,8},{13,15},{11,9},{20,22},{18,... | collective-permute-start | bytes 1622024 | tf_op jit(solution)/shard_map/ppermute | solution.py:310
  214.9 8.4 %collective-permute-start.45 = (bf16[128,1024]{1,0:T(8,128)(2,1)S(1)}, bf16[128,1024]{1,0:T(8,128)(2,1)}, u32[]{:S(2)}, u32[]{:S(2)}) collective-permute-start(bf16[128,1024]{1,0:T(8,128)(2,1)S(1)} %add_convert_fusion.6), channel_id=1, source_target_pairs={{4,6},{2,0},{5,7},{3,1},{12,14},{10,8},{13,15},{11,9},{20,22},{18,... | collective-permute-start | bytes 786440 | tf_op jit(solution)/shard_map/ppermute | solution.py:310
  223.3 23.0 %collective-permute-start.49 = (bf16[136,1024]{1,0:T(8,128)(2,1)}, bf16[136,1024]{1,0:T(8,128)(2,1)S(1)}, u32[]{:S(2)}, u32[]{:S(2)}) collective-permute-start(bf16[136,1024]{1,0:T(8,128)(2,1)} %get-tuple-element.59), channel_id=1, source_target_pairs={{0,2},{6,4},{1,3},{7,5},{8,10},{14,12},{9,11},{15,13},{16,18},{22,... | collective-permute-start | bytes 835592 | tf_op jit(solution)/shard_map/ppermute | solution.py:310
  231.7 16.8 %collective-permute-start.51 = (bf16[136,1024]{1,0:T(8,128)(2,1)}, bf16[136,1024]{1,0:T(8,128)(2,1)S(1)}, u32[]{:S(2)}, u32[]{:S(2)}) collective-permute-start(bf16[136,1024]{1,0:T(8,128)(2,1)} %add_convert_fusion.5), channel_id=1, source_target_pairs={{2,4},{4,2},{3,5},{5,3},{10,12},{12,10},{11,13},{13,11},{18,20},{2... | collective-permute-start | bytes 835592 | tf_op jit(solution)/shard_map/ppermute | solution.py:310
  232.4 16.9 %collective-permute-start.54 = (bf16[136,1024]{1,0:T(8,128)(2,1)}, bf16[136,1024]{1,0:T(8,128)(2,1)S(1)}, u32[]{:S(2)}, u32[]{:S(2)}) collective-permute-start(bf16[136,1024]{1,0:T(8,128)(2,1)} %add_convert_fusion.3), channel_id=1, source_target_pairs={{4,6},{2,0},{5,7},{3,1},{12,14},{10,8},{13,15},{11,9},{20,22},{18,... | collective-permute-start | bytes 835592 | tf_op jit(solution)/shard_map/ppermute | solution.py:310
  239.3 10.6 %collective-permute-start.46 = (bf16[128,1024]{1,0:T(8,128)(2,1)}, bf16[128,1024]{1,0:T(8,128)(2,1)S(1)}, u32[]{:S(2)}, u32[]{:S(2)}) collective-permute-start(bf16[128,1024]{1,0:T(8,128)(2,1)} %get-tuple-element.55), channel_id=1, source_target_pairs={{0,8},{8,0},{16,24},{24,16},{1,9},{9,1},{17,25},{25,17},{2,10},{10... | collective-permute-start | bytes 786440 | tf_op jit(solution)/shard_map/ppermute | solution.py:296
  240.2 15.7 %collective-permute-start.47 = (bf16[128,1024]{1,0:T(8,128)(2,1)}, bf16[128,1024]{1,0:T(8,128)(2,1)S(1)}, u32[]{:S(2)}, u32[]{:S(2)}) collective-permute-start(bf16[128,1024]{1,0:T(8,128)(2,1)} %get-tuple-element.56), channel_id=1, source_target_pairs={{0,16},{8,24},{16,0},{24,8},{1,17},{9,25},{17,1},{25,9},{2,18},{10... | collective-permute-start | bytes 786440 | tf_op jit(solution)/shard_map/ppermute | solution.py:296
  246.3 10.5 %collective-permute-start.48 = (bf16[128,1024]{1,0:T(8,128)(2,1)}, bf16[128,1024]{1,0:T(8,128)(2,1)S(1)}, u32[]{:S(2)}, u32[]{:S(2)}) collective-permute-start(bf16[128,1024]{1,0:T(8,128)(2,1)} %get-tuple-element.57), channel_id=1, source_target_pairs={{0,24},{8,16},{16,8},{24,0},{1,25},{9,17},{17,9},{25,1},{2,26},{10... | collective-permute-start | bytes 786440 | tf_op jit(solution)/shard_map/ppermute | solution.py:296
  248.5 11.5 %collective-permute-start.31 = (bf16[128,1024]{1,0:T(8,128)(2,1)}, bf16[128,1024]{1,0:T(8,128)(2,1)S(1)}, u32[]{:S(2)}, u32[]{:S(2)}) collective-permute-start(bf16[128,1024]{1,0:T(8,128)(2,1)} %get-tuple-element.42), channel_id=1, source_target_pairs={{0,8},{8,0},{16,24},{24,16},{1,9},{9,1},{17,25},{25,17},{2,10},{10... | collective-permute-start | bytes 786440 | tf_op jit(solution)/shard_map/ppermute | solution.py:296
  249.3 14.0 %collective-permute-start.32 = (bf16[128,1024]{1,0:T(8,128)(2,1)}, bf16[128,1024]{1,0:T(8,128)(2,1)S(1)}, u32[]{:S(2)}, u32[]{:S(2)}) collective-permute-start(bf16[128,1024]{1,0:T(8,128)(2,1)} %get-tuple-element.43), channel_id=1, source_target_pairs={{0,16},{8,24},{16,0},{24,8},{1,17},{9,25},{17,1},{25,9},{2,18},{10... | collective-permute-start | bytes 786440 | tf_op jit(solution)/shard_map/ppermute | solution.py:296
  249.9 13.4 %collective-permute-start.33 = (bf16[128,1024]{1,0:T(8,128)(2,1)}, bf16[128,1024]{1,0:T(8,128)(2,1)S(1)}, u32[]{:S(2)}, u32[]{:S(2)}) collective-permute-start(bf16[128,1024]{1,0:T(8,128)(2,1)} %get-tuple-element.44), channel_id=1, source_target_pairs={{0,24},{8,16},{16,8},{24,0},{1,25},{9,17},{17,9},{25,1},{2,26},{10... | collective-permute-start | bytes 786440 | tf_op jit(solution)/shard_map/ppermute | solution.py:296
  (29 other events, 250.9 us)
where the time goes:
time: 266 us; the launch traced here: 265 us
  waiting for transfers between devices  136 us (51%)
  starting transfers between devices  74.9 us (28%)
  Pallas kernels  40.4 us (15%)
  other arithmetic  9.2 us (3%)
  local copies, waits for them, and re-layouts  3.09 us (1%)
    ppermute x22, waiting for transfers between devices, edge(): return lax.ppermute(value, 'batch', pairs)  75.1 us
    ppermute x22, starting transfers between devices, edge(): return lax.ppermute(value, 'batch', pairs)  44.3 us
    pallas_call x8, Pallas kernels, call(): pl.pallas_call(kernel, out_shape=outs, grid=grid, in_specs=[SM] + list(sp...  40.4 us
    ppermute x10, waiting for transfers between devices, over_z(): return lax.ppermute(value, 'batch', pairs)  34.6 us
    ppermute x15, waiting for transfers between devices, over_head(): return lax.ppermute(value, 'head', [(i, i ^ m) for i in range(heads)])  24.5 us
    ppermute x15, starting transfers between devices, over_head(): return lax.ppermute(value, 'head', [(i, i ^ m) for i in range(heads)])  18.1 us
    ppermute x10, starting transfers between devices, over_z(): return lax.ppermute(value, 'batch', pairs)  11 us
  transfers between devices with their start and end apart: 55, of which 21 were waited for; matrix products, arithmetic and copies ran while one was open for 3% of the time, Pallas kernels for 14%

commit v1 on v0

--- a/solution.py
+++ b/solution.py
@@ -75,7 +75,7 @@
 SM = pl.BlockSpec(memory_space=pltpu.SMEM)
 
 
-def call(kernel, args, outs, scratch=(), flops=0, grid=(), specs=None, out_specs=None):
+def call(kernel, args, outs, scratch=(), flops=0, grid=(), specs=None, out_specs=None, room=24):
     size = sum(a.size * a.dtype.itemsize for a in list(args[1:]) + list(outs))
     return pl.pallas_call(
         kernel,
@@ -84,6 +84,7 @@
         in_specs=[SM] + list(specs or [VM] * (len(args) - 1)),
         out_specs=list(out_specs or [VM] * len(outs)),
         scratch_shapes=list(scratch),
+        compiler_params=pltpu.CompilerParams(vmem_limit_bytes=room << 20),
         cost_estimate=pl.CostEstimate(flops=flops, bytes_accessed=size, transcendentals=0),
     )(*args)
 
@@ -98,7 +99,8 @@
 
 def norm_kernel(heads, width, ids, *refs):
     blocks = refs[:heads]
-    outs = refs[heads:-1]
+    places = refs[heads]
+    outs = refs[heads + 1 : -1]
     held = refs[-1]
     square = None
     for block in blocks:
@@ -109,74 +111,113 @@
     for m, block in enumerate(blocks):
         held[m] = (block[...].astype(jnp.float32) * scale).astype(jnp.bfloat16)
     mix = ids[0] ^ ids[1]
+    rows, mem = held.shape[2], places.shape[1]
     for s in range(SEGS):
         for j in range(heads):
-            outs[s * heads + j][...] = held[mix ^ j, s]
-
-
-def project_kernel(heads, seg, size, groups, ids, *refs):
-    pieces = refs[:heads]
-    pos = refs[heads : 2 * heads]
-    own = refs[2 * heads : 2 * heads + 4]
-    other = refs[2 * heads + 4 : 2 * heads + 8]
-    outs = refs[2 * heads + 8 : -3]
-    rows, picked, logits = refs[-3:]
+            out = outs[s * heads + j]
+            out[:rows, :] = held[mix ^ j, s]
+            if s == 0:
+                out[rows:, :] = jnp.zeros((PAD, out.shape[1]), jnp.bfloat16)
+                shown = places[...].astype(jnp.float32).astype(jnp.bfloat16)
+                out[rows : rows + SEGS, :mem] = shown
+
+
+def gather_pieces(heads, ids, pieces, rows):
     piece = pieces[0].shape[1]
-    seg_rows = piece * heads
-    mem_rows = pos[0].shape[1]
-    depth = own[0].shape[0]
+    for m in range(heads):
+        start = pl.multiple_of((ids[0] ^ m) * piece, piece)
+        for j in range(heads):
+            rows[j, pl.ds(start, piece), :] = pieces[m][j]
+
+
+def weight_rows(ids, depth):
     mine = pl.ds(pl.multiple_of(ids[2] * depth, depth), depth)
     theirs = pl.ds(pl.multiple_of((1 - ids[2]) * depth, depth), depth)
+    return mine, theirs
+
+
+def product(source, parts, own, other):
+    depth = own.shape[0]
+    mine, theirs = parts
+    return (
+        jnp.dot(
+            source[:, :, mine].reshape(-1, depth), own[...], preferred_element_type=jnp.float32
+        )
+        + jnp.dot(
+            source[:, :, theirs].reshape(-1, depth), other[...], preferred_element_type=jnp.float32
+        )
+    ).astype(jnp.bfloat16)
+
+
+def query_kernel(heads, ids, *refs):
+    pieces = refs[:heads]
+    own, other = refs[heads : heads + 2]
+    outs = refs[heads + 2 : -1]
+    rows = refs[-1]
+
+    @pl.when(pl.program_id(0) == 0)
+    def _():
+        gather_pieces(heads, ids, pieces, rows)
+
+    result = product(rows, weight_rows(ids, own.shape[0]), own, other)
+    count = rows.shape[1]
+    for j in range(heads):
+        outs[j][...] = result[j * count : (j + 1) * count]
+
+
+def project_kernel(heads, mem, size, ids, *refs):
+    pieces = [refs[:heads], refs[heads : 2 * heads]]
+    pos = refs[2 * heads : 3 * heads]
+    own = refs[3 * heads : 3 * heads + 4]
+    other = refs[3 * heads + 4 : 3 * heads + 8]
+    outs = refs[3 * heads + 8 : -4]
+    first, rows, picked, logits = refs[-4:]
+    seg_rows = rows.shape[1]
+    piece = pieces[0][0].shape[1]
+    parts = weight_rows(ids, own[0].shape[0])
     n = pl.program_id(0)
 
     @pl.when(n == 0)
     def _():
-        for m in range(heads):
-            start = pl.multiple_of((ids[0] ^ m) * piece, piece)
+        token = lax.broadcasted_iota(jnp.int32, (seg_rows, mem), 0).astype(jnp.float32)
+        contract = (((0,), (1,)), ((), ()))
+        for s, source in enumerate((first, rows)):
+            gather_pieces(heads, ids, pieces[s], source)
             for j in range(heads):
-                rows[j, pl.ds(start, piece), :] = pieces[m][j]
-        token = lax.broadcasted_iota(jnp.int32, (seg_rows, mem_rows), 0)
-        contract = (((0,), (1,)), ((), ()))
-        for j in range(heads):
-            hot = jnp.where(token == pos[j][seg : seg + 1, :], 1.0, 0.0).astype(jnp.bfloat16)
-            picked[j] = lax.dot_general(
-                hot, rows[j], (((0,), (0,)), ((), ())), preferred_element_type=jnp.float32
-            ).astype(jnp.bfloat16)
-            logits[j] = lax.dot_general(
-                own[3][...], picked[j, :, mine], contract, preferred_element_type=jnp.float32
-            ) + lax.dot_general(
-                other[3][...], picked[j, :, theirs], contract, preferred_element_type=jnp.float32
+                where = pos[j][piece:, :][s : s + 1, :mem].astype(jnp.float32)
+                hot = jnp.where(token == where, 1.0, 0.0).astype(jnp.bfloat16)
+                chosen = lax.dot_general(
+                    hot, source[j], (((0,), (0,)), ((), ())), preferred_element_type=jnp.float32
+                ).astype(jnp.bfloat16)
+                picked[s * heads + j] = chosen
+                logits[s * heads + j] = sum(
+                    lax.dot_general(
+                        weight[...],
+                        picked[s * heads + j, :, part],
+                        contract,
+                        preferred_element_type=jnp.float32,
+                    )
+                    for weight, part in ((own[3], parts[0]), (other[3], parts[1]))
+                )
+
+    query = product(rows, parts, own[0], other[0])
+    pairs = [product(picked, parts, own[kind], other[kind]) for kind in (1, 2)]
+    tile = own[0].shape[1]
+    for j in range(heads):
+        outs[j][:seg_rows, :] = query[j * seg_rows : (j + 1) * seg_rows]
+    for index in range(SEGS * heads):
+        out = outs[index]
+        top = seg_rows if index < heads else 0
+        for result in pairs:
+            out[top : top + mem, :] = result[index * mem : (index + 1) * mem]
+            top += mem
+        for k in range(tile // size):
+            logit = logits[index, pl.ds(n * (tile // size) + k, 1), :]
+            shown = jnp.broadcast_to(logit, (PAD, mem)).astype(jnp.bfloat16)
+            out[top:, k * size : k * size + mem] = shown
+            out[top:, k * size + mem : (k + 1) * size] = jnp.zeros(
+                (PAD, size - mem), jnp.bfloat16
             )
-
-    flat = lambda ref, part: ref[:, :, part].reshape(-1, depth)
-
-    def product(source, weight):
-        return jnp.dot(
-            flat(source, mine), own[weight][...], preferred_element_type=jnp.float32
-        ) + jnp.dot(
-            flat(source, theirs), other[weight][...], preferred_element_type=jnp.float32
-        )
-
-    results = (
-        (product(rows, 0).astype(jnp.bfloat16), seg_rows),
-        (product(picked, 1).astype(jnp.bfloat16), mem_rows),
-        (product(picked, 2).astype(jnp.bfloat16), mem_rows),
-    )
-    tile = own[0].shape[1]
-    for g, group in enumerate(groups):
-        for j in range(heads):
-            out = outs[g * heads + j]
-            top = 0
-            for kind in group:
-                result, count = results[kind]
-                out[top : top + count, :] = result[j * count : (j + 1) * count]
-                top += count
-            if 2 in group:
-                for k in range(tile // size):
-                    logit = logits[j, pl.ds(n * (tile // size) + k, 1), :]
-                    shown = jnp.broadcast_to(logit, (out.shape[0] - top, mem_rows))
-                    shown = jnp.concatenate([shown, jnp.zeros_like(shown)], axis=1)
-                    out[top:, k * size : (k + 1) * size] = shown[:, :size].astype(jnp.bfloat16)
 
 
 HIGHEST = lax.Precision.HIGHEST
@@ -218,14 +259,20 @@
         logits = held[first + 2 * mem_rows :, columns]
         beta = jax.nn.sigmoid(logits).T[:mem_rows, :1]
         changes.append(beta * (values - recalled))
+    later = []
     for head, state in enumerate(states):
-        state_out[head] = state + lax.dot_general(
-            changes[head],
-            kept[head][0],
-            (((0,), (0,)), ((), ())),
-            precision=HIGHEST,
-            preferred_element_type=jnp.float32,
+        later.append(
+            state
+            + lax.dot_general(
+                changes[head],
+                kept[head][0],
+                (((0,), (0,)), ((), ())),
+                precision=HIGHEST,
+                preferred_element_type=jnp.float32,
+            )
         )
+        state_out[head] = later[head]
+    return later
 
 
 def heads_in(state_in):
@@ -235,9 +282,8 @@
 def both_kernel(count, seg_rows, mem_rows, ids, *refs):
     state_in, readout, state_out, held = refs[count:]
     summed(refs[:count], held)
-    states = heads_in(state_in)
+    states = update_states(held, heads_in(state_in), state_out, seg_rows, mem_rows)
     read_states(held, states, readout, seg_rows)
-    update_states(held, states, state_out, seg_rows, mem_rows)
 
 
 def read_kernel(count, seg_rows, ids, *refs):
@@ -309,54 +355,65 @@
             pairs.append(((planes - 1 - i) * CORES + c, (planes - 2 - i) * CORES + c))
         return lax.ppermute(value, "batch", pairs)
 
+    halves = jnp.split(w_out, 2, axis=0)
+    near = [over_z(half, 1) for half in halves]
+    across = [edge(half, 1) for half in halves]
     x = hidden_in.reshape(SEGS, heads, piece, width)
     quarter = lambda m: lax.dynamic_index_in_dim(x, h ^ m, axis=1, keepdims=False)
     blocks = [quarter(0)] + [over_head(quarter(m), m) for m in range(1, heads)]
     weights = [w_query, w_key, w_value, w_beta]
     partner = [over_core(w) for w in weights]
-    pos = [mem_pos[0]] + [over_z(mem_pos[0], j) for j in range(1, planes)]
     normed = call(
         functools.partial(norm_kernel, heads, full_width),
-        [ids] + blocks,
-        [shape((piece, width), bf16)] * (SEGS * planes),
+        [ids] + blocks + [mem_pos[0]],
+        [shape((piece + PAD, width), bf16)] * planes + [shape((piece, width), bf16)] * planes,
         [pltpu.VMEM((heads, SEGS, piece, width), bf16)],
+        room=8,
     )
-    y = [w_out, over_z(w_out, 1)]
-    parts = []
-    last = SEGS - 1
-    groups = [((0, 1, 2),)] * last + [((0,), (1, 2))]
+    pieces = []
     for s in range(SEGS):
-        kinds = (seg_rows, mem_rows, mem_rows + PAD)
-        counts = [sum(kinds[kind] for kind in group) for group in groups[s]]
         mine = normed[s * planes : (s + 1) * planes]
-        held = [mine[0]] + [over_z(mine[j], j) for j in range(1, planes)]
-        held = jnp.stack(held)
-        pieces = [held] + [over_head(held, m) for m in range(1, heads)]
-        parts.append(
-            call(
-                functools.partial(project_kernel, heads, s, size, groups[s]),
-                [ids] + pieces + pos + weights + partner,
-                [shape((count, features), bf16) for count in counts for _ in range(planes)],
-                [
-                    pltpu.VMEM((planes, seg_rows, width), bf16),
-                    pltpu.VMEM((planes, mem_rows, width), bf16),
-                    pltpu.VMEM((planes, local_heads, mem_rows), f32),
-                ],
-                flops=2 * planes * width * features * (seg_rows + 2 * mem_rows),
-                grid=(features // tile,),
-                specs=[whole(v) for v in pieces + pos]
-                + [columns_of(v, tile) for v in weights[:3]]
-                + [whole(w_beta)]
-                + [columns_of(v, tile) for v in weights[:3]]
-                + [whole(w_beta)],
-                out_specs=[
-                    pl.BlockSpec((count, tile), lambda n: (0, n))
-                    for count in counts
-                    for _ in range(planes)
-                ],
-            )
-        )
-    r11, r10 = edge(w_out, 1), edge(y[1], 1)
+        got = [mine[0]] + [over_z(mine[j], j) for j in range(1, planes)]
+        if s == 0:
+            pos = got
+        held = jnp.stack([value[:piece] for value in got])
+        pieces.append([held] + [over_head(held, m) for m in range(1, heads)])
+    tiles = lambda values: [columns_of(v, tile) for v in values]
+    column_tile = lambda count: pl.BlockSpec((count, tile), lambda n: (0, n))
+    queries = call(
+        functools.partial(query_kernel, heads),
+        [ids] + pieces[0] + [w_query, partner[0]],
+        [shape((seg_rows, features), bf16)] * planes,
+        [pltpu.VMEM((planes, seg_rows, width), bf16)],
+        flops=2 * planes * width * features * seg_rows,
+        room=16,
+        grid=(features // tile,),
+        specs=[whole(v) for v in pieces[0]] + tiles([w_query, partner[0]]),
+        out_specs=[column_tile(seg_rows)] * planes,
+    )
+    few = 2 * mem_rows + PAD
+    counts = [seg_rows + few] * planes + [few] * planes
+    products = call(
+        functools.partial(project_kernel, heads, mem_rows, size),
+        [ids] + pieces[0] + pieces[1] + pos + weights + partner,
+        [shape((count, features), bf16) for count in counts],
+        [
+            pltpu.VMEM((planes, seg_rows, width), bf16),
+            pltpu.VMEM((planes, seg_rows, width), bf16),
+            pltpu.VMEM((SEGS * planes, mem_rows, width), bf16),
+            pltpu.VMEM((SEGS * planes, local_heads, mem_rows), f32),
+        ],
+        flops=2 * planes * width * features * (seg_rows + 4 * mem_rows),
+        grid=(features // tile,),
+        specs=[whole(v) for v in pieces[0] + pieces[1] + pos]
+        + tiles(weights[:3])
+        + [whole(w_beta)]
+        + tiles(partner[:3])
+        + [whole(w_beta)],
+        out_specs=[column_tile(count) for count in counts],
+    )
+    y = [w_out, jnp.concatenate(near, axis=0)]
+    r11, r10 = jnp.concatenate(across, axis=0), edge(y[1], 1)
     r21, r20 = edge(r11, 2), edge(r10, 2)
     outer = (z == 0) | (z == planes - 1)
     y = y + [jnp.where(outer, r21, r10), jnp.where(outer, r20, r11)]
@@ -366,11 +423,10 @@
     def line_sum(u):
         t03 = edge(u[3], 0)
         t02 = edge(u[2], 0)
-        t01 = edge(u[1], 0)
         t13 = edge(add(u[2], t03), 1)
         t12 = edge(add(u[3], t02), 1)
-        t23 = edge(add(u[1], t13), 2)
-        return [u[0], t01, t12, t23]
+        pair = over_z(add(u[1], t13), 1)
+        return [u[0], pair, t12]
 
     read_shape = shape((seg_rows, features), bf16)
     state_shape = shape(memory_in.shape[1:], f32)
@@ -393,29 +449,30 @@
         return (total + rows).astype(bf16)
 
     state = memory_in[0]
-    outs = []
-    for s in range(last):
-        sums = line_sum(parts[s])
-        readout, state = call(
-            functools.partial(both_kernel, 4, seg_rows, mem_rows),
-            [ids] + sums + [state],
-            [read_shape, state_shape],
-            scratch=[pltpu.VMEM(sums[0].shape, f32)],
-        )
-        outs.append(emit(readout, s))
-    sums = line_sum(parts[last][:planes])
+    sums = line_sum(queries)
     readout = call(
-        functools.partial(read_kernel, 4, seg_rows),
+        functools.partial(read_kernel, 3, seg_rows),
         [ids] + sums + [state],
         [read_shape],
+        room=8,
         scratch=[pltpu.VMEM(sums[0].shape, f32)],
     )[0]
-    outs.append(emit(readout, last))
-    sums = line_sum(parts[last][planes:])
+    outs = [emit(readout, 0)]
+    sums = line_sum(products[:planes])
+    readout, state = call(
+        functools.partial(both_kernel, 3, seg_rows, mem_rows),
+        [ids] + sums + [state],
+        [read_shape, state_shape],
+        room=12,
+        scratch=[pltpu.VMEM(sums[0].shape, f32)],
+    )
+    outs.append(emit(readout, 1))
+    sums = line_sum(products[planes:])
     state = call(
-        functools.partial(update_kernel, 4, mem_rows),
+        functools.partial(update_kernel, 3, mem_rows),
         [ids] + sums + [state],
         [state_shape],
+        room=8,
         scratch=[pltpu.VMEM(sums[0].shape, f32)],
     )[0]
     return (jnp.concatenate(outs, axis=0)[None], state[None])

time: 266 us -> 221 us (0.83)
  waiting for transfers between devices: 136 us -> 58.7 us
  starting transfers between devices: 74.9 us -> 112 us
  Pallas kernels: 40.4 us -> 25.4 us
  local copies, waits for them, and re-layouts: 3.09 us -> 14.3 us
    ppermute x22 -> x17, waiting for transfers between devices: 75.1 us -> 16.3 us  [edge(): return lax.ppermute(value, 'batch', pairs)]
    ppermute x10 -> x11, starting transfers between devices: 11 us -> 41.4 us  [over_z(): return lax.ppermute(value, 'batch', pairs)]
    ppermute x10 -> x11, waiting for transfers between devices: 34.6 us -> 15.4 us  [over_z(): return lax.ppermute(value, 'batch', pairs)]
    pallas_call x8, Pallas kernels: 40.4 us -> 25.4 us  [call(): pl.pallas_call(kernel, out_shape=outs, grid=grid, in_specs=[SM] + list(sp...]
    unnamed x77 -> x59, local copies, waits for them, and re-layouts: 1.2 us -> 11.2 us
    ppermute x22 -> x17, starting transfers between devices: 44.3 us -> 51.4 us  [edge(): return lax.ppermute(value, 'batch', pairs)]
  transfers between devices with their start and end apart: 55 -> 51, of which waited for: 21 -> 15; matrix products, arithmetic and copies ran while one was open for 3% -> 5% of each run, Pallas kernels for 14% -> 11%
where the time goes in v1:
time: 221 us; the launch traced here: 220 us
  starting transfers between devices  112 us (51%)
  waiting for transfers between devices  58.7 us (27%)
  Pallas kernels  25.4 us (11%)
  local copies, waits for them, and re-layouts  14.3 us (6%)
  other arithmetic  8.01 us (4%)
    ppermute x17, starting transfers between devices, edge(): return lax.ppermute(value, 'batch', pairs)  51.4 us
    ppermute x11, starting transfers between devices, over_z(): return lax.ppermute(value, 'batch', pairs)  41.4 us
    ppermute x15, waiting for transfers between devices, over_head(): return lax.ppermute(value, 'head', [(i, i ^ m) for i in range(heads)])  25.6 us
    pallas_call x8, Pallas kernels, call(): pl.pallas_call(kernel, out_shape=outs, grid=grid, in_specs=[SM] + list(sp...  25.4 us
    ppermute x15, starting transfers between devices, over_head(): return lax.ppermute(value, 'head', [(i, i ^ m) for i in range(heads)])  18.1 us
    ppermute x17, waiting for transfers between devices, edge(): return lax.ppermute(value, 'batch', pairs)  16.3 us
    ppermute x11, waiting for transfers between devices, over_z(): return lax.ppermute(value, 'batch', pairs)  15.4 us
    unnamed x59, local copies, waits for them, and re-layouts  11.2 us
  transfers between devices with their start and end apart: 51, of which 15 were waited for; matrix products, arithmetic and copies ran while one was open for 5% of the time, Pallas kernels for 11%

profile of v1, /device:TPU:0, one launch (start us, length us, event | category | flops | bytes accessed | tf_op | source)
XLA Modules:
  0.0 219.8 jit_solution(3666339682645551727)
XLA Ops:
  0.7 1.1 dynamic-slice_bitcast_fusion
  1.8 3.0 %collective-permute-start = (bf16[2,32,1024]{2,1,0:T(8,128)(2,1)S(1)}, bf16[2,32,1024]{2,1,0:T(8,128)(2,1)S(1)}, u32[]{:S(2)}, u32[]{:S(2)}) collective-permute-start(bf16[2,32,1024]{2,1,0:T(8,128)(2,1)S(1)} %get-tuple-element.68), channel_id=1, source_target_pairs={{0,8},{8,0},{16,24},{24,16},{1,9},{9,1},{17,25},{25,17},{2,10},{10... | collective-permute-start | bytes 393224 | tf_op jit(solution)/shard_map/ppermute | solution.py:342
  4.8 1.5 collective-permute-start.1
  6.5 2.3 %collective-permute-done.refs_1_ = bf16[2,32,1024]{2,1,0:T(8,128)(2,1)S(1)} collective-permute-done((bf16[2,32,1024]{2,1,0:T(8,128)(2,1)S(1)}, bf16[2,32,1024]{2,1,0:T(8,128)(2,1)S(1)}, u32[]{:S(2)}, u32[]{:S(2)}) %collective-permute-start) | collective-permute-done | bytes 131104 | tf_op jit(solution)/shard_map/ppermute | solution.py:342
  8.7 3.9 %collective-permute-done.1.refs_2_ = bf16[2,32,1024]{2,1,0:T(8,128)(2,1)S(1)} collective-permute-done((bf16[2,32,1024]{2,1,0:T(8,128)(2,1)S(1)}, bf16[2,32,1024]{2,1,0:T(8,128)(2,1)S(1)}, u32[]{:S(2)}, u32[]{:S(2)}) %collective-permute-start.1) | collective-permute-done | bytes 131104 | tf_op jit(solution)/shard_map/ppermute | solution.py:342
  12.6 0.8 shard_map.95
  13.5 1.6 collective-permute-start.29
  15.1 2.6 %collective-permute-start.30 = (bf16[32,1024]{1,0:T(8,128)(2,1)S(1)}, bf16[32,1024]{1,0:T(8,128)(2,1)S(1)}, u32[]{:S(2)}, u32[]{:S(2)}) collective-permute-start(bf16[32,1024]{1,0:T(8,128)(2,1)S(1)} %get-tuple-element.46), channel_id=1, source_target_pairs={{0,4},{1,5},{2,6},{3,7},{4,0},{5,1},{6,2},{7,3},{8,12},{9,13},{10,... | collective-permute-start | bytes 196616 | tf_op jit(solution)/shard_map/ppermute | solution.py:346
  17.9 3.6 %collective-permute-start.5 = (bf16[40,1024]{1,0:T(8,128)(2,1)S(1)}, bf16[40,1024]{1,0:T(8,128)(2,1)S(1)}, u32[]{:S(2)}, u32[]{:S(2)}) collective-permute-start(bf16[40,1024]{1,0:T(8,128)(2,1)S(1)} %get-tuple-element.35), channel_id=1, source_target_pairs={{0,6},{1,7},{2,4},{3,5},{4,2},{5,3},{6,0},{7,1},{8,14},{9,15},{10,... | collective-permute-start | bytes 245768 | tf_op jit(solution)/shard_map/ppermute | solution.py:346
  21.5 0.8 collective-permute-start.3
  22.4 4.2 %collective-permute-done.30 = bf16[32,1024]{1,0:T(8,128)(2,1)S(1)} collective-permute-done((bf16[32,1024]{1,0:T(8,128)(2,1)S(1)}, bf16[32,1024]{1,0:T(8,128)(2,1)S(1)}, u32[]{:S(2)}, u32[]{:S(2)}) %collective-permute-start.30) | collective-permute-done | bytes 65568 | tf_op jit(solution)/shard_map/ppermute | solution.py:346
  26.6 1.3 collective-permute-start.32
  27.9 0.8 collective-permute-start.33
  29.6 1.7 collective-permute-start.6
  31.3 1.0 fusion.2
  32.9 1.3 collective-permute-done.37.refs_19_
  34.2 1.7 collective-permute-start.16
  37.9 1.4 collective-permute-start.8
  39.3 11.1 %collective-permute-done.7.refs_2_ = bf16[4,32,1024]{2,1,0:T(8,128)(2,1)S(1)} collective-permute-done((bf16[4,32,1024]{2,1,0:T(8,128)(2,1)S(1)}, bf16[4,32,1024]{2,1,0:T(8,128)(2,1)S(1)}, u32[]{:S(2)}, u32[]{:S(2)}) %collective-permute-start.7) | collective-permute-done | bytes 262176 | tf_op jit(solution)/shard_map/ppermute | solution.py:342
  51.6 4.0 %collective-permute-done.16 = bf16[512,512]{1,0:T(8,128)(2,1)S(1)} collective-permute-done((bf16[512,512]{1,0:T(8,128)(2,1)}, bf16[512,512]{1,0:T(8,128)(2,1)S(1)}, u32[]{:S(2)}, u32[]{:S(2)}) %collective-permute-start.16) | collective-permute-done | bytes 524320 | tf_op jit(solution)/shard_map/ppermute | solution.py:346
  56.3 1.1 constant_dynamic-update-slice_fusion.1
  57.4 1.6 collective-permute-start.20
  59.0 0.8 constant_dynamic-update-slice_fusion.3
  60.5 0.8 constant_dynamic-update-slice_fusion.2
  61.4 1.4 collective-permute-start.19
  62.8 4.2 %shard_map.96 = (bf16[128,1024]{1,0:T(8,128)(2,1)S(1)}, bf16[128,1024]{1,0:T(8,128)(2,1)S(1)}, bf16[128,1024]{1,0:T(8,128)(2,1)S(1)}, bf16[128,1024]{1,0:T(8,128)(2,1)}) custom-call(s32[3]{0:T(128)S(1)} %pad_add_fusion.ids, bf16[4,32,1024]{2,1,0:T(8,128)(2,1)S(1)} %pad_maximum_fusion.refs_0_, bf16[4,32,1024]{2,1,0:T(8,128)(2,1)S(1)} %collective-permute-done.6.refs_1_, ...), custom_call_target="tpu_custom_call" | custom-call | flops 1073741824 | bytes 4194304 | tf_op jit(solution)/shard_map/pallas_call | solution.py:80
  69.1 24.3 %collective-permute-start.10 = (bf16[128,1024]{1,0:T(8,128)(2,1)}, bf16[128,1024]{1,0:T(8,128)(2,1)}, u32[]{:S(2)}, u32[]{:S(2)}) collective-permute-start(bf16[128,1024]{1,0:T(8,128)(2,1)} %get-tuple-element.39), channel_id=1, source_target_pairs={{0,2},{6,4},{1,3},{7,5},{8,10},{14,12},{9,11},{15,13},{16,18},{22,... | collective-permute-start | bytes 786440 | tf_op jit(solution)/shard_map/ppermute | solution.py:356
  93.5 0.9 copy-done.25
  94.4 7.5 %shard_map.99 = (bf16[264,1024]{1,0:T(8,128)(2,1)S(1)}, bf16[264,1024]{1,0:T(8,128)(2,1)S(1)}, bf16[264,1024]{1,0:T(8,128)(2,1)S(1)}, bf16[264,1024]{1,0:T(8,128...) custom-call(s32[3]{0:T(128)S(1)} %pad_add_fusion.ids, ...), custom_call_target="tpu_custom_call" | custom-call | flops 3221225472 | bytes 12009472 | tf_op jit(solution)/shard_map/pallas_call | solution.py:80
  106.5 2.0 collective-permute-start.46
  108.5 1.4 collective-permute-start.49
  110.0 1.1 add_convert_fusion.8
  111.1 2.1 collective-permute-done.46
  113.2 4.4 %collective-permute-start.38 = (bf16[264,1024]{1,0:T(8,128)(2,1)}, bf16[264,1024]{1,0:T(8,128)(2,1)S(1)}, u32[]{:S(2)}, u32[]{:S(2)}) collective-permute-start(bf16[264,1024]{1,0:T(8,128)(2,1)} %copy-done.4), channel_id=1, source_target_pairs={{0,2},{6,4},{1,3},{7,5},{8,10},{14,12},{9,11},{15,13},{16,18},{22,... | collective-permute-start | bytes 1622024 | tf_op jit(solution)/shard_map/ppermute | solution.py:356
  117.6 1.3 collective-permute-start.21
  118.9 1.1 add_convert_fusion.5
  120.1 4.8 %collective-permute-start.41 = (bf16[264,1024]{1,0:T(8,128)(2,1)S(1)}, bf16[264,1024]{1,0:T(8,128)(2,1)S(1)}, u32[]{:S(2)}, u32[]{:S(2)}) collective-permute-start(bf16[264,1024]{1,0:T(8,128)(2,1)S(1)} %copy-done.7), channel_id=1, source_target_pairs={{0,2},{6,4},{1,3},{7,5},{8,10},{14,12},{9,11},{15,13},{16,18},{22,... | collective-permute-start | bytes 1622024 | tf_op jit(solution)/shard_map/ppermute | solution.py:356
  124.8 1.3 broadcast_select_fusion.1.refs_3_
  126.2 4.5 %collective-permute-done.38 = bf16[264,1024]{1,0:T(8,128)(2,1)S(1)} collective-permute-done((bf16[264,1024]{1,0:T(8,128)(2,1)}, bf16[264,1024]{1,0:T(8,128)(2,1)S(1)}, u32[]{:S(2)}, u32[]{:S(2)}) %collective-permute-start.38) | collective-permute-done | bytes 540704 | tf_op jit(solution)/shard_map/ppermute | solution.py:356
  130.7 4.3 %collective-permute-start.13 = (bf16[128,1024]{1,0:T(8,128)(2,1)S(1)}, bf16[128,1024]{1,0:T(8,128)(2,1)S(1)}, u32[]{:S(2)}, u32[]{:S(2)}) collective-permute-start(bf16[128,1024]{1,0:T(8,128)(2,1)S(1)} %copy-done.16), channel_id=1, source_target_pairs={{0,2},{6,4},{1,3},{7,5},{8,10},{14,12},{9,11},{15,13},{16,18},{22,... | collective-permute-start | bytes 786440 | tf_op jit(solution)/shard_map/ppermute | solution.py:356
  135.2 7.0 %collective-permute-done.41 = bf16[264,1024]{1,0:T(8,128)(2,1)S(1)} collective-permute-done((bf16[264,1024]{1,0:T(8,128)(2,1)S(1)}, bf16[264,1024]{1,0:T(8,128)(2,1)S(1)}, u32[]{:S(2)}, u32[]{:S(2)}) %collective-permute-start.41) | collective-permute-done | bytes 540704 | tf_op jit(solution)/shard_map/ppermute | solution.py:356
  143.1 0.8 collective-permute-start.47
  144.2 2.6 %collective-permute-done.13 = bf16[128,1024]{1,0:T(8,128)(2,1)S(1)} collective-permute-done((bf16[128,1024]{1,0:T(8,128)(2,1)S(1)}, bf16[128,1024]{1,0:T(8,128)(2,1)S(1)}, u32[]{:S(2)}, u32[]{:S(2)}) %collective-permute-start.13) | collective-permute-done | bytes 262176 | tf_op jit(solution)/shard_map/ppermute | solution.py:356
  148.3 0.8 collective-permute-start.42
  149.2 24.7 %collective-permute-start.40 = (bf16[264,1024]{1,0:T(8,128)(2,1)S(1)}, bf16[264,1024]{1,0:T(8,128)(2,1)S(1)}, u32[]{:S(2)}, u32[]{:S(2)}) collective-permute-start(bf16[264,1024]{1,0:T(8,128)(2,1)S(1)} %add_convert_fusion.1), channel_id=1, source_target_pairs={{0,2},{1,3},{2,0},{3,1},{4,6},{5,7},{6,4},{7,5},{8,10},{9,11},{10,... | collective-permute-start | bytes 1622024 | tf_op jit(solution)/shard_map/ppermute | solution.py:346
  173.9 1.0 add_convert_fusion.6
  175.0 1.1 add_convert_fusion.3
  176.9 6.4 %collective-permute-done.40.refs_1_ = bf16[264,1024]{1,0:T(8,128)(2,1)S(1)} collective-permute-done((bf16[264,1024]{1,0:T(8,128)(2,1)S(1)}, bf16[264,1024]{1,0:T(8,128)(2,1)S(1)}, u32[]{:S(2)}, u32[]{:S(2)}) %collective-permute-start.40) | collective-permute-done | bytes 540704 | tf_op jit(solution)/shard_map/ppermute | solution.py:346
  183.3 3.9 %collective-permute-start.12 = (bf16[128,1024]{1,0:T(8,128)(2,1)S(1)}, bf16[128,1024]{1,0:T(8,128)(2,1)S(1)}, u32[]{:S(2)}, u32[]{:S(2)}) collective-permute-start(bf16[128,1024]{1,0:T(8,128)(2,1)S(1)} %add_convert_fusion.7), channel_id=1, source_target_pairs={{0,2},{1,3},{2,0},{3,1},{4,6},{5,7},{6,4},{7,5},{8,10},{9,11},{10,... | collective-permute-start | bytes 786440 | tf_op jit(solution)/shard_map/ppermute | solution.py:346
  187.3 3.2 %shard_map.100 = (bf16[128,1024]{1,0:T(8,128)(2,1)S(1)}, f32[8,128,128]{2,1,0:T(8,128)S(1)}) custom-call(s32[3]{0:T(128)S(1)} %pad_add_fusion.ids, bf16[264,1024]{1,0:T(8,128)(2,1)S(1)} %copy-done.9, bf16[264,1024]{1,0:T(8,128)(2,1)S(1)} %collective-permute-done.40.refs_1_, bf16[264,1024]{1,0:T(8,128)(2,1)S(1)} %collective-permute-done.42.refs_2_, ...), custom_call_target="tpu_custom_call" | custom-call | bytes 2932736 | tf_op jit(solution)/shard_map/pallas_call | solution.py:80
  190.5 0.9 collective-permute-start.50
  191.4 1.8 collective-permute-start.48
  193.2 2.5 %shard_map.101 = (f32[128,1024]{1,0:T(8,128)S(1)}, bf16[128,1024]{1,0:T(8,128)(2,1)S(1)}, bf16[128,1024]{1,0:T(8,128)(2,1)S(1)}, bf16[128,1024]{1,0:T(8,128)(2,1)S(1)}) custom-call(s32[3]{0:T(128)S(1)} %pad_add_fusion.ids, bf16[128,1024]{1,0:T(8,128)(2,1)S(1)} %get-tuple-element.52.refs_0_, bf16[1024,512]{1,0:T(8,128)(2,1)S(1)} %copy-done, ...), custom_call_target="tpu_custom_call" | custom-call | flops 1073741824 | bytes 9961472 | tf_op jit(solution)/shard_map/pallas_call | solution.py:80
  196.4 1.8 shard_map.97.refs_0_
  198.2 1.0 collective-permute-start.44
  199.1 2.0 collective-permute-start.45
  201.1 2.5 %shard_map.98 = (f32[128,1024]{1,0:T(8,128)S(1)}, bf16[128,1024]{1,0:T(8,128)(2,1)S(1)}, bf16[128,1024]{1,0:T(8,128)(2,1)S(1)}, bf16[128,1024]{1,0:T(8,128)(2,1)S(1)}) custom-call(s32[3]{0:T(128)S(1)} %pad_add_fusion.ids, bf16[128,1024]{1,0:T(8,128)(2,1)S(1)} %shard_map.97.refs_0_, bf16[1024,512]{1,0:T(8,128)(2,1)S(1)} %copy-done, ...), custom_call_target="tpu_custom_call" | custom-call | flops 1073741824 | bytes 9961472 | tf_op jit(solution)/shard_map/pallas_call | solution.py:80
  204.3 0.9 collective-permute-start.27
  205.2 2.0 collective-permute-start.28
  207.2 2.9 %shard_map.102 = f32[8,128,128]{2,1,0:T(8,128)} custom-call(s32[3]{0:T(128)S(1)} %pad_add_fusion.ids, bf16[136,1024]{1,0:T(8,128)(2,1)S(1)} %get-tuple-element.57.refs_0_, bf16[136,1024]{1,0:T(8,128)(2,1)S(1)} %collective-permute-done.48.refs_1_, bf16[136,1024]{1,0:T(8,128)(2,1)S(1)} %collective-permute-done.50.refs_2_, ...), custom_call_target="tpu_custom_call" | custom-call | bytes 1884160 | tf_op jit(solution)/shard_map/pallas_call | solution.py:80
  210.1 2.8 %collective-permute-done.44 = bf16[128,1024]{1,0:T(8,128)(2,1)S(1)} collective-permute-done((bf16[128,1024]{1,0:T(8,128)(2,1)S(1)}, bf16[128,1024]{1,0:T(8,128)(2,1)S(1)}, u32[]{:S(2)}, u32[]{:S(2)}) %collective-permute-start.44) | collective-permute-done | bytes 262176 | tf_op jit(solution)/shard_map/ppermute | solution.py:342
  212.9 1.3 collective-permute-done.26
  214.2 4.3 %collective-permute-done.27 = bf16[128,1024]{1,0:T(8,128)(2,1)S(1)} collective-permute-done((bf16[128,1024]{1,0:T(8,128)(2,1)S(1)}, bf16[128,1024]{1,0:T(8,128)(2,1)S(1)}, u32[]{:S(2)}, u32[]{:S(2)}) %collective-permute-start.27) | collective-permute-done | bytes 262176 | tf_op jit(solution)/shard_map/ppermute | solution.py:342
  219.0 0.8 maximum_bitcast_fusion
  (129 shorter events, 18.5 us)
Async XLA Ops:
  0.6 12.0 %copy-start.19 = (s32[1,2,64]{2,1,0:T(2,128)S(1)}, s32[1,2,64]{2,1,0:T(2,128)}, u32[]{:S(2)}) copy-start(s32[1,2,64]{2,1,0:T(2,128)} %param.14) | copy-start | bytes 1540
  1.8 6.9 %collective-permute-start = (bf16[2,32,1024]{2,1,0:T(8,128)(2,1)S(1)}, bf16[2,32,1024]{2,1,0:T(8,128)(2,1)S(1)}, u32[]{:S(2)}, u32[]{:S(2)}) collective-permute-start(bf16[2,32,1024]{2,1,0:T(8,128)(2,1)S(1)} %get-tuple-element.68), channel_id=1, source_target_pairs={{0,8},{8,0},{16,24},{24,16},{1,9},{9,1},{17,25},{25,17},{2,10},{10... | collective-permute-start | bytes 393224 | tf_op jit(solution)/shard_map/ppermute | solution.py:342
  4.8 7.8 %collective-permute-start.1 = (bf16[2,32,1024]{2,1,0:T(8,128)(2,1)S(1)}, bf16[2,32,1024]{2,1,0:T(8,128)(2,1)S(1)}, u32[]{:S(2)}, u32[]{:S(2)}) collective-permute-start(bf16[2,32,1024]{2,1,0:T(8,128)(2,1)S(1)} %get-tuple-element.67), channel_id=1, source_target_pairs={{0,16},{8,24},{16,0},{24,8},{1,17},{9,25},{17,1},{25,9},{2,18},{10... | collective-permute-start | bytes 393224 | tf_op jit(solution)/shard_map/ppermute | solution.py:342
  6.4 6.3 %collective-permute-start.2 = (bf16[2,32,1024]{2,1,0:T(8,128)(2,1)S(1)}, bf16[2,32,1024]{2,1,0:T(8,128)(2,1)S(1)}, u32[]{:S(2)}, u32[]{:S(2)}) collective-permute-start(bf16[2,32,1024]{2,1,0:T(8,128)(2,1)S(1)} %get-tuple-element.66), channel_id=1, source_target_pairs={{0,24},{8,16},{16,8},{24,0},{1,25},{9,17},{17,9},{25,1},{2,26},{10... | collective-permute-start | bytes 393224 | tf_op jit(solution)/shard_map/ppermute | solution.py:342
  12.6 18.7 %copy-start = (bf16[1024,512]{1,0:T(8,128)(2,1)S(1)}, bf16[1024,512]{1,0:T(8,128)(2,1)}, u32[]{:S(2)}) copy-start(bf16[1024,512]{1,0:T(8,128)(2,1)} %refs_1_.3) | copy-start | bytes 3145732
  13.5 8.1 %collective-permute-start.29 = (bf16[32,1024]{1,0:T(8,128)(2,1)S(1)}, bf16[32,1024]{1,0:T(8,128)(2,1)S(1)}, u32[]{:S(2)}, u32[]{:S(2)}) collective-permute-start(bf16[32,1024]{1,0:T(8,128)(2,1)S(1)} %get-tuple-element.45), channel_id=1, source_target_pairs={{0,2},{1,3},{2,0},{3,1},{4,6},{5,7},{6,4},{7,5},{8,10},{9,11},{10,... | collective-permute-start | bytes 196616 | tf_op jit(solution)/shard_map/ppermute | solution.py:346
  15.1 11.5 %collective-permute-start.30 = (bf16[32,1024]{1,0:T(8,128)(2,1)S(1)}, bf16[32,1024]{1,0:T(8,128)(2,1)S(1)}, u32[]{:S(2)}, u32[]{:S(2)}) collective-permute-start(bf16[32,1024]{1,0:T(8,128)(2,1)S(1)} %get-tuple-element.46), channel_id=1, source_target_pairs={{0,4},{1,5},{2,6},{3,7},{4,0},{5,1},{6,2},{7,3},{8,12},{9,13},{10,... | collective-permute-start | bytes 196616 | tf_op jit(solution)/shard_map/ppermute | solution.py:346
  17.7 8.9 %collective-permute-start.31 = (bf16[32,1024]{1,0:T(8,128)(2,1)S(1)}, bf16[32,1024]{1,0:T(8,128)(2,1)S(1)}, u32[]{:S(2)}, u32[]{:S(2)}) collective-permute-start(bf16[32,1024]{1,0:T(8,128)(2,1)S(1)} %get-tuple-element.47), channel_id=1, source_target_pairs={{0,6},{1,7},{2,4},{3,5},{4,2},{5,3},{6,0},{7,1},{8,14},{9,15},{10,... | collective-permute-start | bytes 196616 | tf_op jit(solution)/shard_map/ppermute | solution.py:346
  17.9 10.8 %collective-permute-start.5 = (bf16[40,1024]{1,0:T(8,128)(2,1)S(1)}, bf16[40,1024]{1,0:T(8,128)(2,1)S(1)}, u32[]{:S(2)}, u32[]{:S(2)}) collective-permute-start(bf16[40,1024]{1,0:T(8,128)(2,1)S(1)} %get-tuple-element.35), channel_id=1, source_target_pairs={{0,6},{1,7},{2,4},{3,5},{4,2},{5,3},{6,0},{7,1},{8,14},{9,15},{10,... | collective-permute-start | bytes 245768 | tf_op jit(solution)/shard_map/ppermute | solution.py:346
  21.5 8.0 %collective-permute-start.4 = (bf16[40,1024]{1,0:T(8,128)(2,1)S(1)}, bf16[40,1024]{1,0:T(8,128)(2,1)S(1)}, u32[]{:S(2)}, u32[]{:S(2)}) collective-permute-start(bf16[40,1024]{1,0:T(8,128)(2,1)S(1)} %get-tuple-element.34), channel_id=1, source_target_pairs={{0,4},{1,5},{2,6},{3,7},{4,0},{5,1},{6,2},{7,3},{8,12},{9,13},{10,... | collective-permute-start | bytes 245768 | tf_op jit(solution)/shard_map/ppermute | solution.py:346
  21.5 8.0 %collective-permute-start.3 = (bf16[40,1024]{1,0:T(8,128)(2,1)S(1)}, bf16[40,1024]{1,0:T(8,128)(2,1)S(1)}, u32[]{:S(2)}, u32[]{:S(2)}) collective-permute-start(bf16[40,1024]{1,0:T(8,128)(2,1)S(1)} %get-tuple-element.33), channel_id=1, source_target_pairs={{0,2},{1,3},{2,0},{3,1},{4,6},{5,7},{6,4},{7,5},{8,10},{9,11},{10,... | collective-permute-start | bytes 245768 | tf_op jit(solution)/shard_map/ppermute | solution.py:346
  26.6 9.3 %collective-permute-start.32 = (bf16[4,32,1024]{2,1,0:T(8,128)(2,1)S(1)}, bf16[4,32,1024]{2,1,0:T(8,128)(2,1)S(1)}, u32[]{:S(2)}, u32[]{:S(2)}) collective-permute-start(bf16[4,32,1024]{2,1,0:T(8,128)(2,1)S(1)} %pad_maximum_fusion.1.refs_4_), channel_id=1, source_target_pairs={{0,8},{8,0},{16,24},{24,16},{1,9},{9,1},{17,25},{25,17},{2,10},{10... | collective-permute-start | bytes 786440 | tf_op jit(solution)/shard_map/ppermute | solution.py:342
  27.9 9.3 %collective-permute-start.33 = (bf16[4,32,1024]{2,1,0:T(8,128)(2,1)S(1)}, bf16[4,32,1024]{2,1,0:T(8,128)(2,1)S(1)}, u32[]{:S(2)}, u32[]{:S(2)}) collective-permute-start(bf16[4,32,1024]{2,1,0:T(8,128)(2,1)S(1)} %pad_maximum_fusion.1.refs_4_), channel_id=1, source_target_pairs={{0,16},{8,24},{16,0},{24,8},{1,17},{9,25},{17,1},{25,9},{2,18},{10... | collective-permute-start | bytes 786440 | tf_op jit(solution)/shard_map/ppermute | solution.py:342
  29.6 9.7 %collective-permute-start.6 = (bf16[4,32,1024]{2,1,0:T(8,128)(2,1)S(1)}, bf16[4,32,1024]{2,1,0:T(8,128)(2,1)S(1)}, u32[]{:S(2)}, u32[]{:S(2)}) collective-permute-start(bf16[4,32,1024]{2,1,0:T(8,128)(2,1)S(1)} %pad_maximum_fusion.refs_0_), channel_id=1, source_target_pairs={{0,8},{8,0},{16,24},{24,16},{1,9},{9,1},{17,25},{25,17},{2,10},{10... | collective-permute-start | bytes 786440 | tf_op jit(solution)/shard_map/ppermute | solution.py:342
  32.3 18.5 %collective-permute-start.15 = (bf16[512,512]{1,0:T(8,128)(2,1)}, bf16[512,512]{1,0:T(8,128)(2,1)}, u32[]{:S(2)}, u32[]{:S(2)}) collective-permute-start(bf16[512,512]{1,0:T(8,128)(2,1)} %get-tuple-element.63), channel_id=1, source_target_pairs={{0,2},{1,3},{2,0},{3,1},{4,6},{5,7},{6,4},{7,5},{8,10},{9,11},{10,... | collective-permute-start | bytes 1572872 | tf_op jit(solution)/shard_map/ppermute | solution.py:346
  32.8 1.4 collective-permute-start.37
  34.2 21.4 %collective-permute-start.16 = (bf16[512,512]{1,0:T(8,128)(2,1)}, bf16[512,512]{1,0:T(8,128)(2,1)S(1)}, u32[]{:S(2)}, u32[]{:S(2)}) collective-permute-start(bf16[512,512]{1,0:T(8,128)(2,1)} %get-tuple-element.62), channel_id=1, source_target_pairs={{0,2},{1,3},{2,0},{3,1},{4,6},{5,7},{6,4},{7,5},{8,10},{9,11},{10,... | collective-permute-start | bytes 1572872 | tf_op jit(solution)/shard_map/ppermute | solution.py:346
  36.7 13.7 %collective-permute-start.7 = (bf16[4,32,1024]{2,1,0:T(8,128)(2,1)S(1)}, bf16[4,32,1024]{2,1,0:T(8,128)(2,1)S(1)}, u32[]{:S(2)}, u32[]{:S(2)}) collective-permute-start(bf16[4,32,1024]{2,1,0:T(8,128)(2,1)S(1)} %pad_maximum_fusion.refs_0_), channel_id=1, source_target_pairs={{0,16},{8,24},{16,0},{24,8},{1,17},{9,25},{17,1},{25,9},{2,18},{10... | collective-permute-start | bytes 786440 | tf_op jit(solution)/shard_map/ppermute | solution.py:342
  37.9 12.5 %collective-permute-start.8 = (bf16[4,32,1024]{2,1,0:T(8,128)(2,1)S(1)}, bf16[4,32,1024]{2,1,0:T(8,128)(2,1)S(1)}, u32[]{:S(2)}, u32[]{:S(2)}) collective-permute-start(bf16[4,32,1024]{2,1,0:T(8,128)(2,1)S(1)} %pad_maximum_fusion.refs_0_), channel_id=1, source_target_pairs={{0,24},{8,16},{16,8},{24,0},{1,25},{9,17},{17,9},{25,1},{2,26},{10... | collective-permute-start | bytes 786440 | tf_op jit(solution)/shard_map/ppermute | solution.py:342
  39.3 23.5 %copy-start.24 = (bf16[4,32,1024]{2,1,0:T(8,128)(2,1)}, bf16[4,32,1024]{2,1,0:T(8,128)(2,1)S(1)}, u32[]{:S(2)}) copy-start(bf16[4,32,1024]{2,1,0:T(8,128)(2,1)S(1)} %collective-permute-done.6.refs_1_) | copy-start | bytes 786436
  39.3 22.1 %collective-permute-start.9 = (bf16[512,1024]{1,0:T(8,128)(2,1)}, bf16[512,1024]{1,0:T(8,128)(2,1)S(1)}, u32[]{:S(2)}, u32[]{:S(2)}) collective-permute-start(bf16[512,1024]{1,0:T(8,128)(2,1)} %refs_12_.1), channel_id=1, source_target_pairs={{0,1},{1,0},{2,3},{3,2},{4,5},{5,4},{6,7},{7,6},{8,9},{9,8},{10,11... | collective-permute-start | bytes 3145736 | tf_op jit(solution)/shard_map/ppermute | solution.py:349
  50.4 43.1 %collective-permute-start.35 = (bf16[512,1024]{1,0:T(8,128)(2,1)}, bf16[512,1024]{1,0:T(8,128)(2,1)S(1)}, u32[]{:S(2)}, u32[]{:S(2)}) collective-permute-start(bf16[512,1024]{1,0:T(8,128)(2,1)} %refs_13_.1), channel_id=1, source_target_pairs={{0,1},{1,0},{2,3},{3,2},{4,5},{5,4},{6,7},{7,6},{8,9},{9,8},{10,11... | collective-permute-start | bytes 3145736 | tf_op jit(solution)/shard_map/ppermute | solution.py:349
  50.4 43.1 %collective-permute-start.36 = (bf16[512,1024]{1,0:T(8,128)(2,1)}, bf16[512,1024]{1,0:T(8,128)(2,1)S(1)}, u32[]{:S(2)}, u32[]{:S(2)}) collective-permute-start(bf16[512,1024]{1,0:T(8,128)(2,1)} %refs_14_.1), channel_id=1, source_target_pairs={{0,1},{1,0},{2,3},{3,2},{4,5},{5,4},{6,7},{7,6},{8,9},{9,8},{10,11... | collective-permute-start | bytes 3145736 | tf_op jit(solution)/shard_map/ppermute | solution.py:349
  50.9 6.5 %collective-permute-start.17 = (bf16[512,512]{1,0:T(8,128)(2,1)}, bf16[512,512]{1,0:T(8,128)(2,1)S(1)}, u32[]{:S(2)}, u32[]{:S(2)}) collective-permute-start(bf16[512,512]{1,0:T(8,128)(2,1)} %get-tuple-element.63), channel_id=1, source_target_pairs={{2,4},{4,2},{3,5},{5,3},{10,12},{12,10},{11,13},{13,11},{18,20},{2... | collective-permute-start | bytes 1572872 | tf_op jit(solution)/shard_map/ppermute | solution.py:356
  55.6 4.3 %collective-permute-start.18 = (bf16[512,512]{1,0:T(8,128)(2,1)}, bf16[512,512]{1,0:T(8,128)(2,1)S(1)}, u32[]{:S(2)}, u32[]{:S(2)}) collective-permute-start(bf16[512,512]{1,0:T(8,128)(2,1)} %get-tuple-element.62), channel_id=1, source_target_pairs={{2,4},{4,2},{3,5},{5,3},{10,12},{12,10},{11,13},{13,11},{18,20},{2... | collective-permute-start | bytes 1572872 | tf_op jit(solution)/shard_map/ppermute | solution.py:356
  57.4 60.2 %collective-permute-start.20 = (bf16[1024,512]{1,0:T(8,128)(2,1)S(1)}, bf16[1024,512]{1,0:T(8,128)(2,1)}, u32[]{:S(2)}, u32[]{:S(2)}) collective-permute-start(bf16[1024,512]{1,0:T(8,128)(2,1)S(1)} %constant_dynamic-update-slice_fusion.refs_2_), channel_id=1, source_target_pairs={{2,4},{4,2},{3,5},{5,3},{10,12},{12,10},{11,13},{13,11},{18,20},{2... | collective-permute-start | bytes 3145736 | tf_op jit(solution)/shard_map/ppermute | solution.py:356
  59.9 9.3 %collective-permute-start.34 = (bf16[4,32,1024]{2,1,0:T(8,128)(2,1)S(1)}, bf16[4,32,1024]{2,1,0:T(8,128)(2,1)S(1)}, u32[]{:S(2)}, u32[]{:S(2)}) collective-permute-start(bf16[4,32,1024]{2,1,0:T(8,128)(2,1)S(1)} %pad_maximum_fusion.1.refs_4_), channel_id=1, source_target_pairs={{0,24},{8,16},{16,8},{24,0},{1,25},{9,17},{17,9},{25,1},{2,26},{10... | collective-permute-start | bytes 786440 | tf_op jit(solution)/shard_map/ppermute | solution.py:342
  61.4 32.1 %copy-start.21 = (bf16[4,32,1024]{2,1,0:T(8,128)(2,1)S(1)}, bf16[4,32,1024]{2,1,0:T(8,128)(2,1)}, u32[]{:S(2)}) copy-start(bf16[4,32,1024]{2,1,0:T(8,128)(2,1)} %copy-done.20) | copy-start | bytes 786436
  61.4 32.1 %copy-start.23 = (bf16[4,32,1024]{2,1,0:T(8,128)(2,1)S(1)}, bf16[4,32,1024]{2,1,0:T(8,128)(2,1)}, u32[]{:S(2)}) copy-start(bf16[4,32,1024]{2,1,0:T(8,128)(2,1)} %copy-done.22) | copy-start | bytes 786436
  61.4 58.7 %collective-permute-start.19 = (bf16[1024,512]{1,0:T(8,128)(2,1)}, bf16[1024,512]{1,0:T(8,128)(2,1)}, u32[]{:S(2)}, u32[]{:S(2)}) collective-permute-start(bf16[1024,512]{1,0:T(8,128)(2,1)} %constant_dynamic-update-slice_fusion.2), channel_id=1, source_target_pairs={{4,6},{2,0},{5,7},{3,1},{12,14},{10,8},{13,15},{11,9},{20,22},{18,... | collective-permute-start | bytes 3145736 | tf_op jit(solution)/shard_map/ppermute | solution.py:356
  69.1 39.4 %collective-permute-start.10 = (bf16[128,1024]{1,0:T(8,128)(2,1)}, bf16[128,1024]{1,0:T(8,128)(2,1)}, u32[]{:S(2)}, u32[]{:S(2)}) collective-permute-start(bf16[128,1024]{1,0:T(8,128)(2,1)} %get-tuple-element.39), channel_id=1, source_target_pairs={{0,2},{6,4},{1,3},{7,5},{8,10},{14,12},{9,11},{15,13},{16,18},{22,... | collective-permute-start | bytes 786440 | tf_op jit(solution)/shard_map/ppermute | solution.py:356
  106.5 6.7 %collective-permute-start.46 = (bf16[136,1024]{1,0:T(8,128)(2,1)}, bf16[136,1024]{1,0:T(8,128)(2,1)}, u32[]{:S(2)}, u32[]{:S(2)}) collective-permute-start(bf16[136,1024]{1,0:T(8,128)(2,1)} %get-tuple-element.60), channel_id=1, source_target_pairs={{0,2},{6,4},{1,3},{7,5},{8,10},{14,12},{9,11},{15,13},{16,18},{22,... | collective-permute-start | bytes 835592 | tf_op jit(solution)/shard_map/ppermute | solution.py:356
  108.5 35.6 %collective-permute-start.22 = (bf16[1024,512]{1,0:T(8,128)(2,1)S(1)}, bf16[1024,512]{1,0:T(8,128)(2,1)S(1)}, u32[]{:S(2)}, u32[]{:S(2)}) collective-permute-start(bf16[1024,512]{1,0:T(8,128)(2,1)S(1)} %copy-done), channel_id=1, source_target_pairs={{0,1},{1,0},{2,3},{3,2},{4,5},{5,4},{6,7},{7,6},{8,9},{9,8},{10,11... | collective-permute-start | bytes 3145736 | tf_op jit(solution)/shard_map/ppermute | solution.py:349
  108.5 11.5 %copy-start.7 = (bf16[264,1024]{1,0:T(8,128)(2,1)S(1)}, bf16[264,1024]{1,0:T(8,128)(2,1)}, u32[]{:S(2)}) copy-start(bf16[264,1024]{1,0:T(8,128)(2,1)} %copy-done.6) | copy-start | bytes 1622020
  108.5 39.0 %collective-permute-start.49 = (bf16[136,1024]{1,0:T(8,128)(2,1)}, bf16[136,1024]{1,0:T(8,128)(2,1)S(1)}, u32[]{:S(2)}, u32[]{:S(2)}) collective-permute-start(bf16[136,1024]{1,0:T(8,128)(2,1)} %copy-done.12), channel_id=1, source_target_pairs={{0,2},{6,4},{1,3},{7,5},{8,10},{14,12},{9,11},{15,13},{16,18},{22,... | collective-permute-start | bytes 835592 | tf_op jit(solution)/shard_map/ppermute | solution.py:356
  113.2 17.6 %collective-permute-start.38 = (bf16[264,1024]{1,0:T(8,128)(2,1)}, bf16[264,1024]{1,0:T(8,128)(2,1)S(1)}, u32[]{:S(2)}, u32[]{:S(2)}) collective-permute-start(bf16[264,1024]{1,0:T(8,128)(2,1)} %copy-done.4), channel_id=1, source_target_pairs={{0,2},{6,4},{1,3},{7,5},{8,10},{14,12},{9,11},{15,13},{16,18},{22,... | collective-permute-start | bytes 1622024 | tf_op jit(solution)/shard_map/ppermute | solution.py:356
  117.6 25.5 %collective-permute-start.21 = (bf16[1024,512]{1,0:T(8,128)(2,1)}, bf16[1024,512]{1,0:T(8,128)(2,1)S(1)}, u32[]{:S(2)}, u32[]{:S(2)}) collective-permute-start(bf16[1024,512]{1,0:T(8,128)(2,1)} %collective-permute-done.20), channel_id=1, source_target_pairs={{4,6},{2,0},{5,7},{3,1},{12,14},{10,8},{13,15},{11,9},{20,22},{18,... | collective-permute-start | bytes 3145736 | tf_op jit(solution)/shard_map/ppermute | solution.py:356
  120.1 10.7 %copy-start.16 = (bf16[128,1024]{1,0:T(8,128)(2,1)S(1)}, bf16[128,1024]{1,0:T(8,128)(2,1)}, u32[]{:S(2)}) copy-start(bf16[128,1024]{1,0:T(8,128)(2,1)} %copy-done.15) | copy-start | bytes 786436
  120.1 22.2 %collective-permute-start.41 = (bf16[264,1024]{1,0:T(8,128)(2,1)S(1)}, bf16[264,1024]{1,0:T(8,128)(2,1)S(1)}, u32[]{:S(2)}, u32[]{:S(2)}) collective-permute-start(bf16[264,1024]{1,0:T(8,128)(2,1)S(1)} %copy-done.7), channel_id=1, source_target_pairs={{0,2},{6,4},{1,3},{7,5},{8,10},{14,12},{9,11},{15,13},{16,18},{22,... | collective-permute-start | bytes 1622024 | tf_op jit(solution)/shard_map/ppermute | solution.py:356
  126.2 16.7 %copy-start.5 = (bf16[264,1024]{1,0:T(8,128)(2,1)S(1)}, bf16[264,1024]{1,0:T(8,128)(2,1)}, u32[]{:S(2)}) copy-start(bf16[264,1024]{1,0:T(8,128)(2,1)} %copy-done.4) | copy-start | bytes 1622020
  130.7 16.1 %collective-permute-start.13 = (bf16[128,1024]{1,0:T(8,128)(2,1)S(1)}, bf16[128,1024]{1,0:T(8,128)(2,1)S(1)}, u32[]{:S(2)}, u32[]{:S(2)}) collective-permute-start(bf16[128,1024]{1,0:T(8,128)(2,1)S(1)} %copy-done.16), channel_id=1, source_target_pairs={{0,2},{6,4},{1,3},{7,5},{8,10},{14,12},{9,11},{15,13},{16,18},{22,... | collective-permute-start | bytes 786440 | tf_op jit(solution)/shard_map/ppermute | solution.py:356
  142.2 5.4 %collective-permute-start.39 = (bf16[264,1024]{1,0:T(8,128)(2,1)S(1)}, bf16[264,1024]{1,0:T(8,128)(2,1)S(1)}, u32[]{:S(2)}, u32[]{:S(2)}) collective-permute-start(bf16[264,1024]{1,0:T(8,128)(2,1)S(1)} %add_convert_fusion.2), channel_id=1, source_target_pairs={{2,4},{4,2},{3,5},{5,3},{10,12},{12,10},{11,13},{13,11},{18,20},{2... | collective-permute-start | bytes 1622024 | tf_op jit(solution)/shard_map/ppermute | solution.py:356
  143.1 6.0 %collective-permute-start.47 = (bf16[136,1024]{1,0:T(8,128)(2,1)S(1)}, bf16[136,1024]{1,0:T(8,128)(2,1)S(1)}, u32[]{:S(2)}, u32[]{:S(2)}) collective-permute-start(bf16[136,1024]{1,0:T(8,128)(2,1)S(1)} %add_convert_fusion.5), channel_id=1, source_target_pairs={{2,4},{4,2},{3,5},{5,3},{10,12},{12,10},{11,13},{13,11},{18,20},{2... | collective-permute-start | bytes 835592 | tf_op jit(solution)/shard_map/ppermute | solution.py:356
  144.1 46.4 %collective-permute-start.23 = (bf16[1024,512]{1,0:T(8,128)(2,1)S(1)}, bf16[1024,512]{1,0:T(8,128)(2,1)S(1)}, u32[]{:S(2)}, u32[]{:S(2)}) collective-permute-start(bf16[1024,512]{1,0:T(8,128)(2,1)S(1)} %constant_dynamic-update-slice_fusion.refs_2_), channel_id=1, source_target_pairs={{0,1},{1,0},{2,3},{3,2},{4,5},{5,4},{6,7},{7,6},{8,9},{9,8},{10,11... | collective-permute-start | bytes 3145736 | tf_op jit(solution)/shard_map/ppermute | solution.py:349
  146.8 1.5 collective-permute-start.11
  147.5 43.9 %collective-permute-start.24 = (bf16[1024,512]{1,0:T(8,128)(2,1)S(1)}, bf16[1024,512]{1,0:T(8,128)(2,1)S(1)}, u32[]{:S(2)}, u32[]{:S(2)}) collective-permute-start(bf16[1024,512]{1,0:T(8,128)(2,1)S(1)} %broadcast_select_fusion.1.refs_3_), channel_id=1, source_target_pairs={{0,1},{1,0},{2,3},{3,2},{4,5},{5,4},{6,7},{7,6},{8,9},{9,8},{10,11... | collective-permute-start | bytes 3145736 | tf_op jit(solution)/shard_map/ppermute | solution.py:349
  147.6 45.6 %collective-permute-start.25 = (bf16[1024,512]{1,0:T(8,128)(2,1)S(1)}, bf16[1024,512]{1,0:T(8,128)(2,1)S(1)}, u32[]{:S(2)}, u32[]{:S(2)}) collective-permute-start(bf16[1024,512]{1,0:T(8,128)(2,1)S(1)} %broadcast_select_fusion.refs_4_), channel_id=1, source_target_pairs={{0,1},{1,0},{2,3},{3,2},{4,5},{5,4},{6,7},{7,6},{8,9},{9,8},{10,11... | collective-permute-start | bytes 3145736 | tf_op jit(solution)/shard_map/ppermute | solution.py:349
  148.3 27.8 %copy-start.14 = (bf16[128,1024]{1,0:T(8,128)(2,1)S(1)}, bf16[128,1024]{1,0:T(8,128)(2,1)}, u32[]{:S(2)}) copy-start(bf16[128,1024]{1,0:T(8,128)(2,1)} %copy-done.13) | copy-start | bytes 786436
  148.3 38.9 %copy-start.11 = (bf16[136,1024]{1,0:T(8,128)(2,1)S(1)}, bf16[136,1024]{1,0:T(8,128)(2,1)}, u32[]{:S(2)}) copy-start(bf16[136,1024]{1,0:T(8,128)(2,1)} %copy-done.10) | copy-start | bytes 835588
  148.3 27.9 %collective-permute-start.42 = (bf16[264,1024]{1,0:T(8,128)(2,1)S(1)}, bf16[264,1024]{1,0:T(8,128)(2,1)S(1)}, u32[]{:S(2)}, u32[]{:S(2)}) collective-permute-start(bf16[264,1024]{1,0:T(8,128)(2,1)S(1)} %add_convert_fusion), channel_id=1, source_target_pairs={{2,4},{4,2},{3,5},{5,3},{10,12},{12,10},{11,13},{13,11},{18,20},{2... | collective-permute-start | bytes 1622024 | tf_op jit(solution)/shard_map/ppermute | solution.py:356
  149.2 34.1 %collective-permute-start.40 = (bf16[264,1024]{1,0:T(8,128)(2,1)S(1)}, bf16[264,1024]{1,0:T(8,128)(2,1)S(1)}, u32[]{:S(2)}, u32[]{:S(2)}) collective-permute-start(bf16[264,1024]{1,0:T(8,128)(2,1)S(1)} %add_convert_fusion.1), channel_id=1, source_target_pairs={{0,2},{1,3},{2,0},{3,1},{4,6},{5,7},{6,4},{7,5},{8,10},{9,11},{10,... | collective-permute-start | bytes 1622024 | tf_op jit(solution)/shard_map/ppermute | solution.py:346
  174.9 12.3 %copy-start.1 = (f32[1,8,128,128]{3,2,1,0:T(8,128)S(1)}, f32[1,8,128,128]{3,2,1,0:T(8,128)}, u32[]{:S(2)}) copy-start(f32[1,8,128,128]{3,2,1,0:T(8,128)} %param.15) | copy-start | bytes 1572868
  175.0 12.3 %copy-start.9 = (bf16[264,1024]{1,0:T(8,128)(2,1)S(1)}, bf16[264,1024]{1,0:T(8,128)(2,1)}, u32[]{:S(2)}) copy-start(bf16[264,1024]{1,0:T(8,128)(2,1)} %copy-done.8) | copy-start | bytes 1622020
  176.2 20.2 %collective-permute-start.14 = (bf16[128,1024]{1,0:T(8,128)(2,1)S(1)}, bf16[128,1024]{1,0:T(8,128)(2,1)S(1)}, u32[]{:S(2)}, u32[]{:S(2)}) collective-permute-start(bf16[128,1024]{1,0:T(8,128)(2,1)S(1)} %add_convert_fusion.6), channel_id=1, source_target_pairs={{2,4},{4,2},{3,5},{5,3},{10,12},{12,10},{11,13},{13,11},{18,20},{2... | collective-permute-start | bytes 786440 | tf_op jit(solution)/shard_map/ppermute | solution.py:356
  183.3 13.2 %collective-permute-start.12 = (bf16[128,1024]{1,0:T(8,128)(2,1)S(1)}, bf16[128,1024]{1,0:T(8,128)(2,1)S(1)}, u32[]{:S(2)}, u32[]{:S(2)}) collective-permute-start(bf16[128,1024]{1,0:T(8,128)(2,1)S(1)} %add_convert_fusion.7), channel_id=1, source_target_pairs={{0,2},{1,3},{2,0},{3,1},{4,6},{5,7},{6,4},{7,5},{8,10},{9,11},{10,... | collective-permute-start | bytes 786440 | tf_op jit(solution)/shard_map/ppermute | solution.py:346
  190.5 13.1 %collective-permute-start.50 = (bf16[136,1024]{1,0:T(8,128)(2,1)S(1)}, bf16[136,1024]{1,0:T(8,128)(2,1)S(1)}, u32[]{:S(2)}, u32[]{:S(2)}) collective-permute-start(bf16[136,1024]{1,0:T(8,128)(2,1)S(1)} %add_convert_fusion.3), channel_id=1, source_target_pairs={{2,4},{4,2},{3,5},{5,3},{10,12},{12,10},{11,13},{13,11},{18,20},{2... | collective-permute-start | bytes 835592 | tf_op jit(solution)/shard_map/ppermute | solution.py:356
  191.4 12.9 %collective-permute-start.48 = (bf16[136,1024]{1,0:T(8,128)(2,1)S(1)}, bf16[136,1024]{1,0:T(8,128)(2,1)S(1)}, u32[]{:S(2)}, u32[]{:S(2)}) collective-permute-start(bf16[136,1024]{1,0:T(8,128)(2,1)S(1)} %add_convert_fusion.4), channel_id=1, source_target_pairs={{0,2},{1,3},{2,0},{3,1},{4,6},{5,7},{6,4},{7,5},{8,10},{9,11},{10,... | collective-permute-start | bytes 835592 | tf_op jit(solution)/shard_map/ppermute | solution.py:346
  195.7 9.5 %collective-permute-start.43 = (bf16[128,1024]{1,0:T(8,128)(2,1)S(1)}, bf16[128,1024]{1,0:T(8,128)(2,1)S(1)}, u32[]{:S(2)}, u32[]{:S(2)}) collective-permute-start(bf16[128,1024]{1,0:T(8,128)(2,1)S(1)} %get-tuple-element.54), channel_id=1, source_target_pairs={{0,8},{8,0},{16,24},{24,16},{1,9},{9,1},{17,25},{25,17},{2,10},{10... | collective-permute-start | bytes 786440 | tf_op jit(solution)/shard_map/ppermute | solution.py:342
  198.2 14.7 %collective-permute-start.44 = (bf16[128,1024]{1,0:T(8,128)(2,1)S(1)}, bf16[128,1024]{1,0:T(8,128)(2,1)S(1)}, u32[]{:S(2)}, u32[]{:S(2)}) collective-permute-start(bf16[128,1024]{1,0:T(8,128)(2,1)S(1)} %get-tuple-element.55), channel_id=1, source_target_pairs={{0,16},{8,24},{16,0},{24,8},{1,17},{9,25},{17,1},{25,9},{2,18},{10... | collective-permute-start | bytes 786440 | tf_op jit(solution)/shard_map/ppermute | solution.py:342
  199.1 13.8 %collective-permute-start.45 = (bf16[128,1024]{1,0:T(8,128)(2,1)S(1)}, bf16[128,1024]{1,0:T(8,128)(2,1)S(1)}, u32[]{:S(2)}, u32[]{:S(2)}) collective-permute-start(bf16[128,1024]{1,0:T(8,128)(2,1)S(1)} %get-tuple-element.56), channel_id=1, source_target_pairs={{0,24},{8,16},{16,8},{24,0},{1,25},{9,17},{17,9},{25,1},{2,26},{10... | collective-permute-start | bytes 786440 | tf_op jit(solution)/shard_map/ppermute | solution.py:342
  203.6 14.9 %copy-start.26 = (bf16[1,256,1024]{2,1,0:T(8,128)(2,1)S(1)}, bf16[1,256,1024]{2,1,0:T(8,128)(2,1)}, u32[]{:S(2)}) copy-start(bf16[1,256,1024]{2,1,0:T(8,128)(2,1)} %param.8) | copy-start | bytes 1572868
  203.6 10.6 %collective-permute-start.26 = (bf16[128,1024]{1,0:T(8,128)(2,1)S(1)}, bf16[128,1024]{1,0:T(8,128)(2,1)S(1)}, u32[]{:S(2)}, u32[]{:S(2)}) collective-permute-start(bf16[128,1024]{1,0:T(8,128)(2,1)S(1)} %get-tuple-element.41), channel_id=1, source_target_pairs={{0,8},{8,0},{16,24},{24,16},{1,9},{9,1},{17,25},{25,17},{2,10},{10... | collective-permute-start | bytes 786440 | tf_op jit(solution)/shard_map/ppermute | solution.py:342
  204.3 14.2 %collective-permute-start.27 = (bf16[128,1024]{1,0:T(8,128)(2,1)S(1)}, bf16[128,1024]{1,0:T(8,128)(2,1)S(1)}, u32[]{:S(2)}, u32[]{:S(2)}) collective-permute-start(bf16[128,1024]{1,0:T(8,128)(2,1)S(1)} %get-tuple-element.42), channel_id=1, source_target_pairs={{0,16},{8,24},{16,0},{24,8},{1,17},{9,25},{17,1},{25,9},{2,18},{10... | collective-permute-start | bytes 786440 | tf_op jit(solution)/shard_map/ppermute | solution.py:342
  205.2 13.3 %collective-permute-start.28 = (bf16[128,1024]{1,0:T(8,128)(2,1)S(1)}, bf16[128,1024]{1,0:T(8,128)(2,1)S(1)}, u32[]{:S(2)}, u32[]{:S(2)}) collective-permute-start(bf16[128,1024]{1,0:T(8,128)(2,1)S(1)} %get-tuple-element.43), channel_id=1, source_target_pairs={{0,24},{8,16},{16,8},{24,0},{1,25},{9,17},{17,9},{25,1},{2,26},{10... | collective-permute-start | bytes 786440 | tf_op jit(solution)/shard_map/ppermute | solution.py:342
  (15 other events, 20.3 us)

commit v2 on v1

--- a/solution.py
+++ b/solution.py
@@ -180,7 +180,7 @@
     @pl.when(n == 0)
     def _():
         token = lax.broadcasted_iota(jnp.int32, (seg_rows, mem), 0).astype(jnp.float32)
-        contract = (((0,), (1,)), ((), ()))
+        contract = (((1,), (1,)), ((), ()))
         for s, source in enumerate((first, rows)):
             gather_pieces(heads, ids, pieces[s], source)
             for j in range(heads):
@@ -355,13 +355,12 @@
             pairs.append(((planes - 1 - i) * CORES + c, (planes - 2 - i) * CORES + c))
         return lax.ppermute(value, "batch", pairs)
 
-    halves = jnp.split(w_out, 2, axis=0)
-    near = [over_z(half, 1) for half in halves]
-    across = [edge(half, 1) for half in halves]
+    middle = w_out.shape[0] // 2
+    halves = [w_out[:middle]]
     x = hidden_in.reshape(SEGS, heads, piece, width)
     quarter = lambda m: lax.dynamic_index_in_dim(x, h ^ m, axis=1, keepdims=False)
     blocks = [quarter(0)] + [over_head(quarter(m), m) for m in range(1, heads)]
-    weights = [w_query, w_key, w_value, w_beta]
+    weights = [w_query, w_key, w_value, w_beta.T]
     partner = [over_core(w) for w in weights]
     normed = call(
         functools.partial(norm_kernel, heads, full_width),
@@ -370,6 +369,12 @@
         [pltpu.VMEM((heads, SEGS, piece, width), bf16)],
         room=8,
     )
+    halves.append(lax.optimization_barrier((w_out, normed[0]))[0][middle:])
+    near = [over_z(half, 1) for half in halves]
+    across = [edge(half, 1) for half in halves]
+    from_near = [edge(half, 1) for half in near]
+    outward = [edge(half, 2) for half in across]
+    farthest = [edge(half, 2) for half in from_near]
     pieces = []
     for s in range(SEGS):
         mine = normed[s * planes : (s + 1) * planes]
@@ -407,16 +412,19 @@
         grid=(features // tile,),
         specs=[whole(v) for v in pieces[0] + pieces[1] + pos]
         + tiles(weights[:3])
-        + [whole(w_beta)]
+        + [whole(weights[3])]
         + tiles(partner[:3])
-        + [whole(w_beta)],
+        + [whole(weights[3])],
         out_specs=[column_tile(count) for count in counts],
     )
-    y = [w_out, jnp.concatenate(near, axis=0)]
-    r11, r10 = jnp.concatenate(across, axis=0), edge(y[1], 1)
-    r21, r20 = edge(r11, 2), edge(r10, 2)
     outer = (z == 0) | (z == planes - 1)
-    y = y + [jnp.where(outer, r21, r10), jnp.where(outer, r20, r11)]
+    rows_of = lambda parts: jnp.concatenate(parts, axis=0)
+    y = [
+        w_out,
+        rows_of(near),
+        jnp.where(outer, rows_of(outward), rows_of(from_near)),
+        jnp.where(outer, rows_of(farthest), rows_of(across)),
+    ]
     y_partner = [over_core(v) for v in y]
     add = lambda a, c: (a.astype(f32) + c.astype(f32)).astype(bf16)
 

time: 221 us -> 207 us (0.937)
  starting transfers between devices: 112 us -> 79.9 us
  waiting for transfers between devices: 58.7 us -> 85.2 us
  other arithmetic: 8.01 us -> 4.12 us
  local copies, waits for them, and re-layouts: 14.3 us -> 11.6 us
    ppermute x17 -> x20, starting transfers between devices: 51.4 us -> 29.6 us  [edge(): return lax.ppermute(value, 'batch', pairs)]
    ppermute x11, waiting for transfers between devices: 15.4 us -> 27.2 us  [over_z(): return lax.ppermute(value, 'batch', pairs)]
    ppermute x11, starting transfers between devices: 41.4 us -> 30 us  [over_z(): return lax.ppermute(value, 'batch', pairs)]
    ppermute x17 -> x20, waiting for transfers between devices: 16.3 us -> 24.8 us  [edge(): return lax.ppermute(value, 'batch', pairs)]
    ppermute x15, waiting for transfers between devices: 25.6 us -> 33.2 us  [over_head(): return lax.ppermute(value, 'head', [(i, i ^ m) for i in range(heads)])]
    convert_element_type x9, other arithmetic: 5.11 us -> 1 us  [line_body(): add = lambda a, c: (a.astype(f32) + c.astype(f32)).astype(bf16)]
    unnamed x59 -> x33, local copies, waits for them, and re-layouts: 11.2 us -> 8.51 us
  transfers between devices with their start and end apart: 51 -> 54, of which waited for: 15 -> 18; matrix products, arithmetic and copies ran while one was open for 5% -> 3% of each run, Pallas kernels for 11% -> 12%
where the time goes in v2:
time: 207 us; the launch traced here: 206 us
  waiting for transfers between devices  85.2 us (41%)
  starting transfers between devices  79.9 us (39%)
  Pallas kernels  24.4 us (12%)
  local copies, waits for them, and re-layouts  11.6 us (6%)
  other arithmetic  4.12 us (2%)
    ppermute x15, waiting for transfers between devices, over_head(): return lax.ppermute(value, 'head', [(i, i ^ m) for i in range(heads)])  33.2 us
    ppermute x11, starting transfers between devices, over_z(): return lax.ppermute(value, 'batch', pairs)  30 us
    ppermute x20, starting transfers between devices, edge(): return lax.ppermute(value, 'batch', pairs)  29.6 us
    ppermute x11, waiting for transfers between devices, over_z(): return lax.ppermute(value, 'batch', pairs)  27.2 us
    ppermute x20, waiting for transfers between devices, edge(): return lax.ppermute(value, 'batch', pairs)  24.8 us
    pallas_call x8, Pallas kernels, call(): pl.pallas_call(kernel, out_shape=outs, grid=grid, in_specs=[SM] + list(sp...  24.4 us
    ppermute x15, starting transfers between devices, over_head(): return lax.ppermute(value, 'head', [(i, i ^ m) for i in range(heads)])  19 us
    unnamed x33, local copies, waits for them, and re-layouts  8.51 us
  transfers between devices with their start and end apart: 54, of which 18 were waited for; matrix products, arithmetic and copies ran while one was open for 3% of the time, Pallas kernels for 12%

profile of v2, /device:TPU:0, one launch (start us, length us, event | category | flops | bytes accessed | tf_op | source)
XLA Modules:
  0.0 206.5 jit_solution(8901690765427267019)
XLA Ops:
  0.7 1.1 dynamic-slice_bitcast_fusion
  1.8 3.0 %collective-permute-start = (bf16[2,32,1024]{2,1,0:T(8,128)(2,1)S(1)}, bf16[2,32,1024]{2,1,0:T(8,128)(2,1)S(1)}, u32[]{:S(2)}, u32[]{:S(2)}) collective-permute-start(bf16[2,32,1024]{2,1,0:T(8,128)(2,1)S(1)} %get-tuple-element.68), channel_id=1, source_target_pairs={{0,8},{8,0},{16,24},{24,16},{1,9},{9,1},{17,25},{25,17},{2,10},{10... | collective-permute-start | bytes 393224 | tf_op jit(solution)/shard_map/ppermute | solution.py:342
  4.9 1.5 collective-permute-start.1
  6.5 2.3 %collective-permute-done.refs_1_ = bf16[2,32,1024]{2,1,0:T(8,128)(2,1)S(1)} collective-permute-done((bf16[2,32,1024]{2,1,0:T(8,128)(2,1)S(1)}, bf16[2,32,1024]{2,1,0:T(8,128)(2,1)S(1)}, u32[]{:S(2)}, u32[]{:S(2)}) %collective-permute-start) | collective-permute-done | bytes 131104 | tf_op jit(solution)/shard_map/ppermute | solution.py:342
  8.7 3.9 %collective-permute-done.1.refs_2_ = bf16[2,32,1024]{2,1,0:T(8,128)(2,1)S(1)} collective-permute-done((bf16[2,32,1024]{2,1,0:T(8,128)(2,1)S(1)}, bf16[2,32,1024]{2,1,0:T(8,128)(2,1)S(1)}, u32[]{:S(2)}, u32[]{:S(2)}) %collective-permute-start.1) | collective-permute-done | bytes 131104 | tf_op jit(solution)/shard_map/ppermute | solution.py:342
  12.6 0.8 shard_map.95
  13.5 1.6 collective-permute-start.32
  15.1 2.6 %collective-permute-start.33 = (bf16[32,1024]{1,0:T(8,128)(2,1)S(1)}, bf16[32,1024]{1,0:T(8,128)(2,1)S(1)}, u32[]{:S(2)}, u32[]{:S(2)}) collective-permute-start(bf16[32,1024]{1,0:T(8,128)(2,1)S(1)} %get-tuple-element.48), channel_id=1, source_target_pairs={{0,4},{1,5},{2,6},{3,7},{4,0},{5,1},{6,2},{7,3},{8,12},{9,13},{10,... | collective-permute-start | bytes 196616 | tf_op jit(solution)/shard_map/ppermute | solution.py:346
  17.9 3.6 %collective-permute-start.5 = (bf16[40,1024]{1,0:T(8,128)(2,1)S(1)}, bf16[40,1024]{1,0:T(8,128)(2,1)S(1)}, u32[]{:S(2)}, u32[]{:S(2)}) collective-permute-start(bf16[40,1024]{1,0:T(8,128)(2,1)S(1)} %get-tuple-element.36), channel_id=1, source_target_pairs={{0,6},{1,7},{2,4},{3,5},{4,2},{5,3},{6,0},{7,1},{8,14},{9,15},{10,... | collective-permute-start | bytes 245768 | tf_op jit(solution)/shard_map/ppermute | solution.py:346
  21.6 5.0 %collective-permute-done.33 = bf16[32,1024]{1,0:T(8,128)(2,1)S(1)} collective-permute-done((bf16[32,1024]{1,0:T(8,128)(2,1)S(1)}, bf16[32,1024]{1,0:T(8,128)(2,1)S(1)}, u32[]{:S(2)}, u32[]{:S(2)}) %collective-permute-start.33) | collective-permute-done | bytes 65568 | tf_op jit(solution)/shard_map/ppermute | solution.py:346
  26.6 1.3 collective-permute-start.35
  27.9 0.8 collective-permute-start.36
  28.8 0.8 collective-permute-done.4.refs_10_
  29.6 1.5 collective-permute-start.37
  31.2 1.2 collective-permute-start.6
  32.4 0.8 collective-permute-start.7
  33.2 2.3 %collective-permute-done.35.refs_5_ = bf16[4,32,1024]{2,1,0:T(8,128)(2,1)S(1)} collective-permute-done((bf16[4,32,1024]{2,1,0:T(8,128)(2,1)S(1)}, bf16[4,32,1024]{2,1,0:T(8,128)(2,1)S(1)}, u32[]{:S(2)}, u32[]{:S(2)}) %collective-permute-start.35) | collective-permute-done | bytes 262176 | tf_op jit(solution)/shard_map/ppermute | solution.py:342
  36.3 5.8 %collective-permute-done.36.refs_6_ = bf16[4,32,1024]{2,1,0:T(8,128)(2,1)S(1)} collective-permute-done((bf16[4,32,1024]{2,1,0:T(8,128)(2,1)S(1)}, bf16[4,32,1024]{2,1,0:T(8,128)(2,1)S(1)}, u32[]{:S(2)}, u32[]{:S(2)}) %collective-permute-start.36) | collective-permute-done | bytes 262176 | tf_op jit(solution)/shard_map/ppermute | solution.py:342
  43.5 3.3 %collective-permute-done.6.refs_1_ = bf16[4,32,1024]{2,1,0:T(8,128)(2,1)S(1)} collective-permute-done((bf16[4,32,1024]{2,1,0:T(8,128)(2,1)S(1)}, bf16[4,32,1024]{2,1,0:T(8,128)(2,1)S(1)}, u32[]{:S(2)}, u32[]{:S(2)}) %collective-permute-start.6) | collective-permute-done | bytes 262176 | tf_op jit(solution)/shard_map/ppermute | solution.py:342
  47.5 3.4 %collective-permute-done.7.refs_2_ = bf16[4,32,1024]{2,1,0:T(8,128)(2,1)S(1)} collective-permute-done((bf16[4,32,1024]{2,1,0:T(8,128)(2,1)S(1)}, bf16[4,32,1024]{2,1,0:T(8,128)(2,1)S(1)}, u32[]{:S(2)}, u32[]{:S(2)}) %collective-permute-start.7) | collective-permute-done | bytes 262176 | tf_op jit(solution)/shard_map/ppermute | solution.py:342
  52.8 0.8 slice.29
  53.6 1.5 collective-permute-start.19
  55.9 1.8 collective-permute-start.16
  58.4 1.1 constant_dynamic-update-slice_fusion.1
  59.5 10.6 %collective-permute-done.16 = bf16[512,512]{1,0:T(8,128)(2,1)} collective-permute-done((bf16[512,512]{1,0:T(8,128)(2,1)}, bf16[512,512]{1,0:T(8,128)(2,1)}, u32[]{:S(2)}, u32[]{:S(2)}) %collective-permute-start.16) | collective-permute-done | bytes 524320 | tf_op jit(solution)/shard_map/ppermute | solution.py:346
  70.0 1.3 collective-permute-start.18
  71.3 1.3 collective-permute-start.20
  73.4 0.9 copy-done.5
  74.3 0.9 copy-done.7
  75.3 0.9 copy-done.9
  76.2 0.9 copy-done.11
  77.2 7.0 %shard_map.99 = (bf16[264,1024]{1,0:T(8,128)(2,1)S(1)}, bf16[264,1024]{1,0:T(8,128)(2,1)S(1)}, bf16[264,1024]{1,0:T(8,128)(2,1)S(1)}, bf16[264,1024]{1,0:T(8,128...) custom-call(s32[3]{0:T(128)S(1)} %pad_add_fusion.ids, ...), custom_call_target="tpu_custom_call" | custom-call | flops 3221225472 | bytes 12009472 | tf_op jit(solution)/shard_map/pallas_call | solution.py:80
  84.2 7.5 %collective-permute-start.41 = (bf16[264,1024]{1,0:T(8,128)(2,1)S(1)}, bf16[264,1024]{1,0:T(8,128)(2,1)S(1)}, u32[]{:S(2)}, u32[]{:S(2)}) collective-permute-start(bf16[264,1024]{1,0:T(8,128)(2,1)S(1)} %get-tuple-element.53), channel_id=1, source_target_pairs={{0,2},{6,4},{1,3},{7,5},{8,10},{14,12},{9,11},{15,13},{16,18},{22,... | collective-permute-start | bytes 1622024 | tf_op jit(solution)/shard_map/ppermute | solution.py:356
  91.7 3.7 %shard_map.96 = (bf16[128,1024]{1,0:T(8,128)(2,1)S(1)}, bf16[128,1024]{1,0:T(8,128)(2,1)S(1)}, bf16[128,1024]{1,0:T(8,128)(2,1)S(1)}, bf16[128,1024]{1,0:T(8,128)(2,1)S(1)}) custom-call(s32[3]{0:T(128)S(1)} %pad_add_fusion.ids, bf16[4,32,1024]{2,1,0:T(8,128)(2,1)S(1)} %pad_maximum_fusion.refs_0_, bf16[4,32,1024]{2,1,0:T(8,128)(2,1)S(1)} %copy-done.7, ...), custom_call_target="tpu_custom_call" | custom-call | flops 1073741824 | bytes 4194304 | tf_op jit(solution)/shard_map/pallas_call | solution.py:80
  95.4 1.3 collective-permute-start.10
  96.8 1.1 constant_dynamic-update-slice_fusion.refs_2_
  97.9 1.3 collective-permute-start.49
  99.3 1.3 collective-permute-start.44
  100.9 9.0 %collective-permute-done.10 = bf16[128,1024]{1,0:T(8,128)(2,1)S(1)} collective-permute-done((bf16[128,1024]{1,0:T(8,128)(2,1)S(1)}, bf16[128,1024]{1,0:T(8,128)(2,1)S(1)}, u32[]{:S(2)}, u32[]{:S(2)}) %collective-permute-start.10) | collective-permute-done | bytes 262176 | tf_op jit(solution)/shard_map/ppermute | solution.py:356
  109.9 1.3 collective-permute-start.23
  111.3 1.3 collective-permute-start.24
  112.8 3.1 %collective-permute-done.49 = bf16[136,1024]{1,0:T(8,128)(2,1)S(1)} collective-permute-done((bf16[136,1024]{1,0:T(8,128)(2,1)S(1)}, bf16[136,1024]{1,0:T(8,128)(2,1)S(1)}, u32[]{:S(2)}, u32[]{:S(2)}) %collective-permute-start.49) | collective-permute-done | bytes 278560 | tf_op jit(solution)/shard_map/ppermute | solution.py:356
  116.7 9.9 %collective-permute-done.23 = bf16[512,512]{1,0:T(8,128)(2,1)S(1)} collective-permute-done((bf16[512,512]{1,0:T(8,128)(2,1)S(1)}, bf16[512,512]{1,0:T(8,128)(2,1)S(1)}, u32[]{:S(2)}, u32[]{:S(2)}) %collective-permute-start.23) | collective-permute-done | bytes 524320 | tf_op jit(solution)/shard_map/ppermute | solution.py:356
  126.6 1.5 collective-permute-start.52
  128.1 3.8 %collective-permute-start.13 = (bf16[128,1024]{1,0:T(8,128)(2,1)S(1)}, bf16[128,1024]{1,0:T(8,128)(2,1)S(1)}, u32[]{:S(2)}, u32[]{:S(2)}) collective-permute-start(bf16[128,1024]{1,0:T(8,128)(2,1)S(1)} %get-tuple-element.39), channel_id=1, source_target_pairs={{0,2},{6,4},{1,3},{7,5},{8,10},{14,12},{9,11},{15,13},{16,18},{22,... | collective-permute-start | bytes 786440 | tf_op jit(solution)/shard_map/ppermute | solution.py:356
  133.5 1.4 maximum_select_fusion.1.refs_4_
  135.0 1.9 collective-permute-done.13
  139.1 14.3 %collective-permute-start.43 = (bf16[264,1024]{1,0:T(8,128)(2,1)S(1)}, bf16[264,1024]{1,0:T(8,128)(2,1)S(1)}, u32[]{:S(2)}, u32[]{:S(2)}) collective-permute-start(bf16[264,1024]{1,0:T(8,128)(2,1)S(1)} %add_convert_fusion.1), channel_id=1, source_target_pairs={{0,2},{1,3},{2,0},{3,1},{4,6},{5,7},{6,4},{7,5},{8,10},{9,11},{10,... | collective-permute-start | bytes 1622024 | tf_op jit(solution)/shard_map/ppermute | solution.py:346
  154.4 10.9 %collective-permute-done.43.refs_1_ = bf16[264,1024]{1,0:T(8,128)(2,1)S(1)} collective-permute-done((bf16[264,1024]{1,0:T(8,128)(2,1)S(1)}, bf16[264,1024]{1,0:T(8,128)(2,1)S(1)}, u32[]{:S(2)}, u32[]{:S(2)}) %collective-permute-start.43) | collective-permute-done | bytes 540704 | tf_op jit(solution)/shard_map/ppermute | solution.py:346
  165.3 3.9 %collective-permute-start.12 = (bf16[128,1024]{1,0:T(8,128)(2,1)S(1)}, bf16[128,1024]{1,0:T(8,128)(2,1)S(1)}, u32[]{:S(2)}, u32[]{:S(2)}) collective-permute-start(bf16[128,1024]{1,0:T(8,128)(2,1)S(1)} %add_convert_fusion.7), channel_id=1, source_target_pairs={{0,2},{1,3},{2,0},{3,1},{4,6},{5,7},{6,4},{7,5},{8,10},{9,11},{10,... | collective-permute-start | bytes 786440 | tf_op jit(solution)/shard_map/ppermute | solution.py:346
  169.3 3.3 %shard_map.100 = (bf16[128,1024]{1,0:T(8,128)(2,1)S(1)}, f32[8,128,128]{2,1,0:T(8,128)S(1)}) custom-call(s32[3]{0:T(128)S(1)} %pad_add_fusion.ids, bf16[264,1024]{1,0:T(8,128)(2,1)S(1)} %get-tuple-element.50.refs_0_, bf16[264,1024]{1,0:T(8,128)(2,1)S(1)} %collective-permute-done.43.refs_1_, bf16[264,1024]{1,0:T(8,128)(2,1)S(1)} %collective-permute-done.45.refs_2_, ...), custom_call_target="tpu_custom_call" | custom-call | bytes 2932736 | tf_op jit(solution)/shard_map/pallas_call | solution.py:80
  172.5 0.9 collective-permute-start.53
  173.4 1.9 collective-permute-start.51
  175.3 2.5 %shard_map.101 = (f32[128,1024]{1,0:T(8,128)S(1)}, bf16[128,1024]{1,0:T(8,128)(2,1)S(1)}, bf16[128,1024]{1,0:T(8,128)(2,1)S(1)}, bf16[128,1024]{1,0:T(8,128)(2,1)S(1)}) custom-call(s32[3]{0:T(128)S(1)} %pad_add_fusion.ids, bf16[128,1024]{1,0:T(8,128)(2,1)S(1)} %get-tuple-element.54.refs_0_, bf16[1024,512]{1,0:T(8,128)(2,1)S(1)} %copy-done, ...), custom_call_target="tpu_custom_call" | custom-call | flops 1073741824 | bytes 9961472 | tf_op jit(solution)/shard_map/pallas_call | solution.py:80
  177.7 2.9 %collective-permute-start.46 = (bf16[128,1024]{1,0:T(8,128)(2,1)S(1)}, bf16[128,1024]{1,0:T(8,128)(2,1)S(1)}, u32[]{:S(2)}, u32[]{:S(2)}) collective-permute-start(bf16[128,1024]{1,0:T(8,128)(2,1)S(1)} %get-tuple-element.56), channel_id=1, source_target_pairs={{0,8},{8,0},{16,24},{24,16},{1,9},{9,1},{17,25},{25,17},{2,10},{10... | collective-permute-start | bytes 786440 | tf_op jit(solution)/shard_map/ppermute | solution.py:342
  180.6 1.8 shard_map.97.refs_0_
  182.7 1.2 collective-permute-start.48
  184.0 2.5 %shard_map.98 = (f32[128,1024]{1,0:T(8,128)S(1)}, bf16[128,1024]{1,0:T(8,128)(2,1)S(1)}, bf16[128,1024]{1,0:T(8,128)(2,1)S(1)}, bf16[128,1024]{1,0:T(8,128)(2,1)S(1)}) custom-call(s32[3]{0:T(128)S(1)} %pad_add_fusion.ids, bf16[128,1024]{1,0:T(8,128)(2,1)S(1)} %shard_map.97.refs_0_, bf16[1024,512]{1,0:T(8,128)(2,1)S(1)} %copy-done, ...), custom_call_target="tpu_custom_call" | custom-call | flops 1073741824 | bytes 9961472 | tf_op jit(solution)/shard_map/pallas_call | solution.py:80
  186.4 2.1 collective-permute-start.29
  188.8 1.3 collective-permute-start.31
  190.1 2.9 %shard_map.102 = f32[8,128,128]{2,1,0:T(8,128)} custom-call(s32[3]{0:T(128)S(1)} %pad_add_fusion.ids, bf16[136,1024]{1,0:T(8,128)(2,1)S(1)} %get-tuple-element.59.refs_0_, bf16[136,1024]{1,0:T(8,128)(2,1)S(1)} %collective-permute-done.51.refs_1_, bf16[136,1024]{1,0:T(8,128)(2,1)S(1)} %collective-permute-done.53.refs_2_, ...), custom_call_target="tpu_custom_call" | custom-call | bytes 1884160 | tf_op jit(solution)/shard_map/pallas_call | solution.py:80
  193.0 5.5 %collective-permute-done.47 = bf16[128,1024]{1,0:T(8,128)(2,1)S(1)} collective-permute-done((bf16[128,1024]{1,0:T(8,128)(2,1)S(1)}, bf16[128,1024]{1,0:T(8,128)(2,1)S(1)}, u32[]{:S(2)}, u32[]{:S(2)}) %collective-permute-start.47) | collective-permute-done | bytes 262176 | tf_op jit(solution)/shard_map/ppermute | solution.py:342
  198.7 6.5 %collective-permute-done.30 = bf16[128,1024]{1,0:T(8,128)(2,1)S(1)} collective-permute-done((bf16[128,1024]{1,0:T(8,128)(2,1)S(1)}, bf16[128,1024]{1,0:T(8,128)(2,1)S(1)}, u32[]{:S(2)}, u32[]{:S(2)}) %collective-permute-start.30) | collective-permute-done | bytes 262176 | tf_op jit(solution)/shard_map/ppermute | solution.py:342
  205.7 0.8 maximum_bitcast_fusion
  (109 shorter events, 15.0 us)
Async XLA Ops:
  0.6 5.8 %copy-start.12 = (bf16[512,8]{0,1:T(8,128)(2,1)S(1)}, bf16[512,8]{0,1:T(8,128)(2,1)}, u32[]{:S(2)}) copy-start(bf16[512,8]{0,1:T(8,128)(2,1)} %param.12) | copy-start | bytes 24580
  0.6 12.0 %copy-start.2 = (s32[1,2,64]{2,1,0:T(2,128)S(1)}, s32[1,2,64]{2,1,0:T(2,128)}, u32[]{:S(2)}) copy-start(s32[1,2,64]{2,1,0:T(2,128)} %param.14) | copy-start | bytes 1540
  1.8 6.9 %collective-permute-start = (bf16[2,32,1024]{2,1,0:T(8,128)(2,1)S(1)}, bf16[2,32,1024]{2,1,0:T(8,128)(2,1)S(1)}, u32[]{:S(2)}, u32[]{:S(2)}) collective-permute-start(bf16[2,32,1024]{2,1,0:T(8,128)(2,1)S(1)} %get-tuple-element.68), channel_id=1, source_target_pairs={{0,8},{8,0},{16,24},{24,16},{1,9},{9,1},{17,25},{25,17},{2,10},{10... | collective-permute-start | bytes 393224 | tf_op jit(solution)/shard_map/ppermute | solution.py:342
  4.9 7.8 %collective-permute-start.1 = (bf16[2,32,1024]{2,1,0:T(8,128)(2,1)S(1)}, bf16[2,32,1024]{2,1,0:T(8,128)(2,1)S(1)}, u32[]{:S(2)}, u32[]{:S(2)}) collective-permute-start(bf16[2,32,1024]{2,1,0:T(8,128)(2,1)S(1)} %get-tuple-element.67), channel_id=1, source_target_pairs={{0,16},{8,24},{16,0},{24,8},{1,17},{9,25},{17,1},{25,9},{2,18},{10... | collective-permute-start | bytes 393224 | tf_op jit(solution)/shard_map/ppermute | solution.py:342
  6.4 6.3 %collective-permute-start.2 = (bf16[2,32,1024]{2,1,0:T(8,128)(2,1)S(1)}, bf16[2,32,1024]{2,1,0:T(8,128)(2,1)S(1)}, u32[]{:S(2)}, u32[]{:S(2)}) collective-permute-start(bf16[2,32,1024]{2,1,0:T(8,128)(2,1)S(1)} %get-tuple-element.66), channel_id=1, source_target_pairs={{0,24},{8,16},{16,8},{24,0},{1,25},{9,17},{17,9},{25,1},{2,26},{10... | collective-permute-start | bytes 393224 | tf_op jit(solution)/shard_map/ppermute | solution.py:342
  6.4 26.0 %collective-permute-start.40 = (bf16[8,512]{1,0:T(8,128)(2,1)S(1)}, bf16[8,512]{1,0:T(8,128)(2,1)S(1)}, u32[]{:S(2)}, u32[]{:S(2)}) collective-permute-start(bf16[8,512]{1,0:T(8,128)(2,1)S(1)} %bitcast.48), channel_id=1, source_target_pairs={{0,1},{1,0},{2,3},{3,2},{4,5},{5,4},{6,7},{7,6},{8,9},{9,8},{10,11... | collective-permute-start | bytes 24584 | tf_op jit(solution)/shard_map/ppermute | solution.py:349
  12.6 23.6 %copy-start = (bf16[1024,512]{1,0:T(8,128)(2,1)S(1)}, bf16[1024,512]{1,0:T(8,128)(2,1)}, u32[]{:S(2)}) copy-start(bf16[1024,512]{1,0:T(8,128)(2,1)} %refs_1_.3) | copy-start | bytes 3145732
  13.5 8.1 %collective-permute-start.32 = (bf16[32,1024]{1,0:T(8,128)(2,1)S(1)}, bf16[32,1024]{1,0:T(8,128)(2,1)S(1)}, u32[]{:S(2)}, u32[]{:S(2)}) collective-permute-start(bf16[32,1024]{1,0:T(8,128)(2,1)S(1)} %get-tuple-element.47), channel_id=1, source_target_pairs={{0,2},{1,3},{2,0},{3,1},{4,6},{5,7},{6,4},{7,5},{8,10},{9,11},{10,... | collective-permute-start | bytes 196616 | tf_op jit(solution)/shard_map/ppermute | solution.py:346
  15.1 11.5 %collective-permute-start.33 = (bf16[32,1024]{1,0:T(8,128)(2,1)S(1)}, bf16[32,1024]{1,0:T(8,128)(2,1)S(1)}, u32[]{:S(2)}, u32[]{:S(2)}) collective-permute-start(bf16[32,1024]{1,0:T(8,128)(2,1)S(1)} %get-tuple-element.48), channel_id=1, source_target_pairs={{0,4},{1,5},{2,6},{3,7},{4,0},{5,1},{6,2},{7,3},{8,12},{9,13},{10,... | collective-permute-start | bytes 196616 | tf_op jit(solution)/shard_map/ppermute | solution.py:346
  17.7 8.9 %collective-permute-start.34 = (bf16[32,1024]{1,0:T(8,128)(2,1)S(1)}, bf16[32,1024]{1,0:T(8,128)(2,1)S(1)}, u32[]{:S(2)}, u32[]{:S(2)}) collective-permute-start(bf16[32,1024]{1,0:T(8,128)(2,1)S(1)} %get-tuple-element.49), channel_id=1, source_target_pairs={{0,6},{1,7},{2,4},{3,5},{4,2},{5,3},{6,0},{7,1},{8,14},{9,15},{10,... | collective-permute-start | bytes 196616 | tf_op jit(solution)/shard_map/ppermute | solution.py:346
  17.9 10.0 %collective-permute-start.5 = (bf16[40,1024]{1,0:T(8,128)(2,1)S(1)}, bf16[40,1024]{1,0:T(8,128)(2,1)S(1)}, u32[]{:S(2)}, u32[]{:S(2)}) collective-permute-start(bf16[40,1024]{1,0:T(8,128)(2,1)S(1)} %get-tuple-element.36), channel_id=1, source_target_pairs={{0,6},{1,7},{2,4},{3,5},{4,2},{5,3},{6,0},{7,1},{8,14},{9,15},{10,... | collective-permute-start | bytes 245768 | tf_op jit(solution)/shard_map/ppermute | solution.py:346
  21.5 8.0 %collective-permute-start.4 = (bf16[40,1024]{1,0:T(8,128)(2,1)S(1)}, bf16[40,1024]{1,0:T(8,128)(2,1)S(1)}, u32[]{:S(2)}, u32[]{:S(2)}) collective-permute-start(bf16[40,1024]{1,0:T(8,128)(2,1)S(1)} %get-tuple-element.35), channel_id=1, source_target_pairs={{0,4},{1,5},{2,6},{3,7},{4,0},{5,1},{6,2},{7,3},{8,12},{9,13},{10,... | collective-permute-start | bytes 245768 | tf_op jit(solution)/shard_map/ppermute | solution.py:346
  26.6 4.5 %collective-permute-start.3 = (bf16[40,1024]{1,0:T(8,128)(2,1)S(1)}, bf16[40,1024]{1,0:T(8,128)(2,1)S(1)}, u32[]{:S(2)}, u32[]{:S(2)}) collective-permute-start(bf16[40,1024]{1,0:T(8,128)(2,1)S(1)} %get-tuple-element.34), channel_id=1, source_target_pairs={{0,2},{1,3},{2,0},{3,1},{4,6},{5,7},{6,4},{7,5},{8,10},{9,11},{10,... | collective-permute-start | bytes 245768 | tf_op jit(solution)/shard_map/ppermute | solution.py:346
  26.6 24.9 %copy-start.3 = (bf16[512,1024]{1,0:T(8,128)(2,1)S(1)}, bf16[512,1024]{1,0:T(8,128)(2,1)}, u32[]{:S(2)}) copy-start(bf16[512,1024]{1,0:T(8,128)(2,1)} %refs_13_.1) | copy-start | bytes 3145732
  26.6 8.9 %collective-permute-start.35 = (bf16[4,32,1024]{2,1,0:T(8,128)(2,1)S(1)}, bf16[4,32,1024]{2,1,0:T(8,128)(2,1)S(1)}, u32[]{:S(2)}, u32[]{:S(2)}) collective-permute-start(bf16[4,32,1024]{2,1,0:T(8,128)(2,1)S(1)} %pad_maximum_fusion.1.refs_4_), channel_id=1, source_target_pairs={{0,8},{8,0},{16,24},{24,16},{1,9},{9,1},{17,25},{25,17},{2,10},{10... | collective-permute-start | bytes 786440 | tf_op jit(solution)/shard_map/ppermute | solution.py:342
  27.9 14.1 %collective-permute-start.36 = (bf16[4,32,1024]{2,1,0:T(8,128)(2,1)S(1)}, bf16[4,32,1024]{2,1,0:T(8,128)(2,1)S(1)}, u32[]{:S(2)}, u32[]{:S(2)}) collective-permute-start(bf16[4,32,1024]{2,1,0:T(8,128)(2,1)S(1)} %pad_maximum_fusion.1.refs_4_), channel_id=1, source_target_pairs={{0,16},{8,24},{16,0},{24,8},{1,17},{9,25},{17,1},{25,9},{2,18},{10... | collective-permute-start | bytes 786440 | tf_op jit(solution)/shard_map/ppermute | solution.py:342
  29.6 12.5 %collective-permute-start.37 = (bf16[4,32,1024]{2,1,0:T(8,128)(2,1)S(1)}, bf16[4,32,1024]{2,1,0:T(8,128)(2,1)S(1)}, u32[]{:S(2)}, u32[]{:S(2)}) collective-permute-start(bf16[4,32,1024]{2,1,0:T(8,128)(2,1)S(1)} %pad_maximum_fusion.1.refs_4_), channel_id=1, source_target_pairs={{0,24},{8,16},{16,8},{24,0},{1,25},{9,17},{17,9},{25,1},{2,26},{10... | collective-permute-start | bytes 786440 | tf_op jit(solution)/shard_map/ppermute | solution.py:342
  31.2 15.6 %collective-permute-start.6 = (bf16[4,32,1024]{2,1,0:T(8,128)(2,1)S(1)}, bf16[4,32,1024]{2,1,0:T(8,128)(2,1)S(1)}, u32[]{:S(2)}, u32[]{:S(2)}) collective-permute-start(bf16[4,32,1024]{2,1,0:T(8,128)(2,1)S(1)} %pad_maximum_fusion.refs_0_), channel_id=1, source_target_pairs={{0,8},{8,0},{16,24},{24,16},{1,9},{9,1},{17,25},{25,17},{2,10},{10... | collective-permute-start | bytes 786440 | tf_op jit(solution)/shard_map/ppermute | solution.py:342
  32.4 18.5 %collective-permute-start.7 = (bf16[4,32,1024]{2,1,0:T(8,128)(2,1)S(1)}, bf16[4,32,1024]{2,1,0:T(8,128)(2,1)S(1)}, u32[]{:S(2)}, u32[]{:S(2)}) collective-permute-start(bf16[4,32,1024]{2,1,0:T(8,128)(2,1)S(1)} %pad_maximum_fusion.refs_0_), channel_id=1, source_target_pairs={{0,16},{8,24},{16,0},{24,8},{1,17},{9,25},{17,1},{25,9},{2,18},{10... | collective-permute-start | bytes 786440 | tf_op jit(solution)/shard_map/ppermute | solution.py:342
  35.5 16.1 %collective-permute-start.8 = (bf16[4,32,1024]{2,1,0:T(8,128)(2,1)S(1)}, bf16[4,32,1024]{2,1,0:T(8,128)(2,1)S(1)}, u32[]{:S(2)}, u32[]{:S(2)}) collective-permute-start(bf16[4,32,1024]{2,1,0:T(8,128)(2,1)S(1)} %pad_maximum_fusion.refs_0_), channel_id=1, source_target_pairs={{0,24},{8,16},{16,8},{24,0},{1,25},{9,17},{17,9},{25,1},{2,26},{10... | collective-permute-start | bytes 786440 | tf_op jit(solution)/shard_map/ppermute | solution.py:342
  42.1 11.6 %collective-permute-start.15 = (bf16[512,512]{1,0:T(8,128)(2,1)S(1)}, bf16[512,512]{1,0:T(8,128)(2,1)}, u32[]{:S(2)}, u32[]{:S(2)}) collective-permute-start(bf16[512,512]{1,0:T(8,128)(2,1)S(1)} %slice.28), channel_id=1, source_target_pairs={{0,2},{1,3},{2,0},{3,1},{4,6},{5,7},{6,4},{7,5},{8,10},{9,11},{10,... | collective-permute-start | bytes 1572872 | tf_op jit(solution)/shard_map/ppermute | solution.py:346
  42.8 12.3 %collective-permute-start.17 = (bf16[512,512]{1,0:T(8,128)(2,1)S(1)}, bf16[512,512]{1,0:T(8,128)(2,1)S(1)}, u32[]{:S(2)}, u32[]{:S(2)}) collective-permute-start(bf16[512,512]{1,0:T(8,128)(2,1)S(1)} %slice.28), channel_id=1, source_target_pairs={{2,4},{4,2},{3,5},{5,3},{10,12},{12,10},{11,13},{13,11},{18,20},{2... | collective-permute-start | bytes 1572872 | tf_op jit(solution)/shard_map/ppermute | solution.py:356
  47.5 23.8 %collective-permute-start.9 = (bf16[512,1024]{1,0:T(8,128)(2,1)}, bf16[512,1024]{1,0:T(8,128)(2,1)}, u32[]{:S(2)}, u32[]{:S(2)}) collective-permute-start(bf16[512,1024]{1,0:T(8,128)(2,1)} %refs_12_.1), channel_id=1, source_target_pairs={{0,1},{1,0},{2,3},{3,2},{4,5},{5,4},{6,7},{7,6},{8,9},{9,8},{10,11... | collective-permute-start | bytes 3145736 | tf_op jit(solution)/shard_map/ppermute | solution.py:349
  51.6 21.1 %collective-permute-start.38 = (bf16[512,1024]{1,0:T(8,128)(2,1)S(1)}, bf16[512,1024]{1,0:T(8,128)(2,1)}, u32[]{:S(2)}, u32[]{:S(2)}) collective-permute-start(bf16[512,1024]{1,0:T(8,128)(2,1)S(1)} %copy-done.3), channel_id=1, source_target_pairs={{0,1},{1,0},{2,3},{3,2},{4,5},{5,4},{6,7},{7,6},{8,9},{9,8},{10,11... | collective-permute-start | bytes 3145736 | tf_op jit(solution)/shard_map/ppermute | solution.py:349
  52.3 21.1 %collective-permute-start.39 = (bf16[512,1024]{1,0:T(8,128)(2,1)}, bf16[512,1024]{1,0:T(8,128)(2,1)}, u32[]{:S(2)}, u32[]{:S(2)}) collective-permute-start(bf16[512,1024]{1,0:T(8,128)(2,1)} %refs_14_.1), channel_id=1, source_target_pairs={{0,1},{1,0},{2,3},{3,2},{4,5},{5,4},{6,7},{7,6},{8,9},{9,8},{10,11... | collective-permute-start | bytes 3145736 | tf_op jit(solution)/shard_map/ppermute | solution.py:349
  53.6 4.0 %collective-permute-start.19 = (bf16[512,512]{1,0:T(8,128)(2,1)}, bf16[512,512]{1,0:T(8,128)(2,1)}, u32[]{:S(2)}, u32[]{:S(2)}) collective-permute-start(bf16[512,512]{1,0:T(8,128)(2,1)} %slice.29), channel_id=1, source_target_pairs={{2,4},{4,2},{3,5},{5,3},{10,12},{12,10},{11,13},{13,11},{18,20},{2... | collective-permute-start | bytes 1572872 | tf_op jit(solution)/shard_map/ppermute | solution.py:356
  55.9 14.2 %collective-permute-start.16 = (bf16[512,512]{1,0:T(8,128)(2,1)}, bf16[512,512]{1,0:T(8,128)(2,1)}, u32[]{:S(2)}, u32[]{:S(2)}) collective-permute-start(bf16[512,512]{1,0:T(8,128)(2,1)} %slice.29), channel_id=1, source_target_pairs={{0,2},{1,3},{2,0},{3,1},{4,6},{5,7},{6,4},{7,5},{8,10},{9,11},{10,... | collective-permute-start | bytes 1572872 | tf_op jit(solution)/shard_map/ppermute | solution.py:346
  57.7 37.8 %collective-permute-start.21 = (bf16[512,512]{1,0:T(8,128)(2,1)}, bf16[512,512]{1,0:T(8,128)(2,1)S(1)}, u32[]{:S(2)}, u32[]{:S(2)}) collective-permute-start(bf16[512,512]{1,0:T(8,128)(2,1)} %collective-permute-done.15), channel_id=1, source_target_pairs={{2,4},{4,2},{3,5},{5,3},{10,12},{12,10},{11,13},{13,11},{18,20},{2... | collective-permute-start | bytes 1572872 | tf_op jit(solution)/shard_map/ppermute | solution.py:356
  70.0 27.8 %collective-permute-start.18 = (bf16[512,512]{1,0:T(8,128)(2,1)}, bf16[512,512]{1,0:T(8,128)(2,1)S(1)}, u32[]{:S(2)}, u32[]{:S(2)}) collective-permute-start(bf16[512,512]{1,0:T(8,128)(2,1)} %copy-done.14), channel_id=1, source_target_pairs={{4,6},{2,0},{5,7},{3,1},{12,14},{10,8},{13,15},{11,9},{20,22},{18,... | collective-permute-start | bytes 1572872 | tf_op jit(solution)/shard_map/ppermute | solution.py:356
  71.3 26.6 %collective-permute-start.20 = (bf16[512,512]{1,0:T(8,128)(2,1)}, bf16[512,512]{1,0:T(8,128)(2,1)S(1)}, u32[]{:S(2)}, u32[]{:S(2)}) collective-permute-start(bf16[512,512]{1,0:T(8,128)(2,1)} %collective-permute-done.19), channel_id=1, source_target_pairs={{4,6},{2,0},{5,7},{3,1},{12,14},{10,8},{13,15},{11,9},{20,22},{18,... | collective-permute-start | bytes 1572872 | tf_op jit(solution)/shard_map/ppermute | solution.py:356
  72.6 26.6 %collective-permute-start.22 = (bf16[512,512]{1,0:T(8,128)(2,1)}, bf16[512,512]{1,0:T(8,128)(2,1)S(1)}, u32[]{:S(2)}, u32[]{:S(2)}) collective-permute-start(bf16[512,512]{1,0:T(8,128)(2,1)} %collective-permute-done.16), channel_id=1, source_target_pairs={{2,4},{4,2},{3,5},{5,3},{10,12},{12,10},{11,13},{13,11},{18,20},{2... | collective-permute-start | bytes 1572872 | tf_op jit(solution)/shard_map/ppermute | solution.py:356
  73.4 1.0 copy-start.5
  74.3 0.9 copy-start.7
  75.3 0.9 copy-start.9
  84.2 27.1 %collective-permute-start.41 = (bf16[264,1024]{1,0:T(8,128)(2,1)S(1)}, bf16[264,1024]{1,0:T(8,128)(2,1)S(1)}, u32[]{:S(2)}, u32[]{:S(2)}) collective-permute-start(bf16[264,1024]{1,0:T(8,128)(2,1)S(1)} %get-tuple-element.53), channel_id=1, source_target_pairs={{0,2},{6,4},{1,3},{7,5},{8,10},{14,12},{9,11},{15,13},{16,18},{22,... | collective-permute-start | bytes 1622024 | tf_op jit(solution)/shard_map/ppermute | solution.py:356
  95.4 14.5 %collective-permute-start.10 = (bf16[128,1024]{1,0:T(8,128)(2,1)S(1)}, bf16[128,1024]{1,0:T(8,128)(2,1)S(1)}, u32[]{:S(2)}, u32[]{:S(2)}) collective-permute-start(bf16[128,1024]{1,0:T(8,128)(2,1)S(1)} %get-tuple-element.40), channel_id=1, source_target_pairs={{0,2},{6,4},{1,3},{7,5},{8,10},{14,12},{9,11},{15,13},{16,18},{22,... | collective-permute-start | bytes 786440 | tf_op jit(solution)/shard_map/ppermute | solution.py:356
  97.8 37.1 %collective-permute-start.25 = (bf16[1024,512]{1,0:T(8,128)(2,1)S(1)}, bf16[1024,512]{1,0:T(8,128)(2,1)S(1)}, u32[]{:S(2)}, u32[]{:S(2)}) collective-permute-start(bf16[1024,512]{1,0:T(8,128)(2,1)S(1)} %copy-done), channel_id=1, source_target_pairs={{0,1},{1,0},{2,3},{3,2},{4,5},{5,4},{6,7},{7,6},{8,9},{9,8},{10,11... | collective-permute-start | bytes 3145736 | tf_op jit(solution)/shard_map/ppermute | solution.py:349
  97.9 18.0 %collective-permute-start.49 = (bf16[136,1024]{1,0:T(8,128)(2,1)S(1)}, bf16[136,1024]{1,0:T(8,128)(2,1)S(1)}, u32[]{:S(2)}, u32[]{:S(2)}) collective-permute-start(bf16[136,1024]{1,0:T(8,128)(2,1)S(1)} %get-tuple-element.62), channel_id=1, source_target_pairs={{0,2},{6,4},{1,3},{7,5},{8,10},{14,12},{9,11},{15,13},{16,18},{22,... | collective-permute-start | bytes 835592 | tf_op jit(solution)/shard_map/ppermute | solution.py:356
  99.3 28.8 %collective-permute-start.44 = (bf16[264,1024]{1,0:T(8,128)(2,1)S(1)}, bf16[264,1024]{1,0:T(8,128)(2,1)S(1)}, u32[]{:S(2)}, u32[]{:S(2)}) collective-permute-start(bf16[264,1024]{1,0:T(8,128)(2,1)S(1)} %get-tuple-element.52), channel_id=1, source_target_pairs={{0,2},{6,4},{1,3},{7,5},{8,10},{14,12},{9,11},{15,13},{16,18},{22,... | collective-permute-start | bytes 1622024 | tf_op jit(solution)/shard_map/ppermute | solution.py:356
  109.9 16.7 %collective-permute-start.23 = (bf16[512,512]{1,0:T(8,128)(2,1)S(1)}, bf16[512,512]{1,0:T(8,128)(2,1)S(1)}, u32[]{:S(2)}, u32[]{:S(2)}) collective-permute-start(bf16[512,512]{1,0:T(8,128)(2,1)S(1)} %collective-permute-done.21), channel_id=1, source_target_pairs={{4,6},{2,0},{5,7},{3,1},{12,14},{10,8},{13,15},{11,9},{20,22},{18,... | collective-permute-start | bytes 1572872 | tf_op jit(solution)/shard_map/ppermute | solution.py:356
  111.3 21.6 %collective-permute-start.24 = (bf16[512,512]{1,0:T(8,128)(2,1)S(1)}, bf16[512,512]{1,0:T(8,128)(2,1)S(1)}, u32[]{:S(2)}, u32[]{:S(2)}) collective-permute-start(bf16[512,512]{1,0:T(8,128)(2,1)S(1)} %collective-permute-done.22), channel_id=1, source_target_pairs={{4,6},{2,0},{5,7},{3,1},{12,14},{10,8},{13,15},{11,9},{20,22},{18,... | collective-permute-start | bytes 1572872 | tf_op jit(solution)/shard_map/ppermute | solution.py:356
  115.9 21.7 %collective-permute-start.42 = (bf16[264,1024]{1,0:T(8,128)(2,1)S(1)}, bf16[264,1024]{1,0:T(8,128)(2,1)S(1)}, u32[]{:S(2)}, u32[]{:S(2)}) collective-permute-start(bf16[264,1024]{1,0:T(8,128)(2,1)S(1)} %add_convert_fusion.2), channel_id=1, source_target_pairs={{2,4},{4,2},{3,5},{5,3},{10,12},{12,10},{11,13},{13,11},{18,20},{2... | collective-permute-start | bytes 1622024 | tf_op jit(solution)/shard_map/ppermute | solution.py:356
  116.6 16.9 %copy-start.15 = (bf16[512,512]{1,0:T(8,128)(2,1)S(1)}, bf16[512,512]{1,0:T(8,128)(2,1)}, u32[]{:S(2)}) copy-start(bf16[512,512]{1,0:T(8,128)(2,1)} %copy-done.14) | copy-start | bytes 1572868
  126.6 10.3 %collective-permute-start.52 = (bf16[136,1024]{1,0:T(8,128)(2,1)S(1)}, bf16[136,1024]{1,0:T(8,128)(2,1)S(1)}, u32[]{:S(2)}, u32[]{:S(2)}) collective-permute-start(bf16[136,1024]{1,0:T(8,128)(2,1)S(1)} %get-tuple-element.61), channel_id=1, source_target_pairs={{0,2},{6,4},{1,3},{7,5},{8,10},{14,12},{9,11},{15,13},{16,18},{22,... | collective-permute-start | bytes 835592 | tf_op jit(solution)/shard_map/ppermute | solution.py:356
  128.1 8.9 %collective-permute-start.13 = (bf16[128,1024]{1,0:T(8,128)(2,1)S(1)}, bf16[128,1024]{1,0:T(8,128)(2,1)S(1)}, u32[]{:S(2)}, u32[]{:S(2)}) collective-permute-start(bf16[128,1024]{1,0:T(8,128)(2,1)S(1)} %get-tuple-element.39), channel_id=1, source_target_pairs={{0,2},{6,4},{1,3},{7,5},{8,10},{14,12},{9,11},{15,13},{16,18},{22,... | collective-permute-start | bytes 786440 | tf_op jit(solution)/shard_map/ppermute | solution.py:356
  132.8 6.3 %collective-permute-start.50 = (bf16[136,1024]{1,0:T(8,128)(2,1)S(1)}, bf16[136,1024]{1,0:T(8,128)(2,1)S(1)}, u32[]{:S(2)}, u32[]{:S(2)}) collective-permute-start(bf16[136,1024]{1,0:T(8,128)(2,1)S(1)} %add_convert_fusion.5), channel_id=1, source_target_pairs={{2,4},{4,2},{3,5},{5,3},{10,12},{12,10},{11,13},{13,11},{18,20},{2... | collective-permute-start | bytes 835592 | tf_op jit(solution)/shard_map/ppermute | solution.py:356
  134.9 37.6 %collective-permute-start.26 = (bf16[1024,512]{1,0:T(8,128)(2,1)S(1)}, bf16[1024,512]{1,0:T(8,128)(2,1)S(1)}, u32[]{:S(2)}, u32[]{:S(2)}) collective-permute-start(bf16[1024,512]{1,0:T(8,128)(2,1)S(1)} %constant_dynamic-update-slice_fusion.refs_2_), channel_id=1, source_target_pairs={{0,1},{1,0},{2,3},{3,2},{4,5},{5,4},{6,7},{7,6},{8,9},{9,8},{10,11... | collective-permute-start | bytes 3145736 | tf_op jit(solution)/shard_map/ppermute | solution.py:349
  136.9 36.4 %collective-permute-start.27 = (bf16[1024,512]{1,0:T(8,128)(2,1)S(1)}, bf16[1024,512]{1,0:T(8,128)(2,1)S(1)}, u32[]{:S(2)}, u32[]{:S(2)}) collective-permute-start(bf16[1024,512]{1,0:T(8,128)(2,1)S(1)} %maximum_select_fusion.refs_3_), channel_id=1, source_target_pairs={{0,1},{1,0},{2,3},{3,2},{4,5},{5,4},{6,7},{7,6},{8,9},{9,8},{10,11... | collective-permute-start | bytes 3145736 | tf_op jit(solution)/shard_map/ppermute | solution.py:349
  136.9 1.5 collective-permute-start.11
  137.6 37.6 %collective-permute-start.28 = (bf16[1024,512]{1,0:T(8,128)(2,1)S(1)}, bf16[1024,512]{1,0:T(8,128)(2,1)S(1)}, u32[]{:S(2)}, u32[]{:S(2)}) collective-permute-start(bf16[1024,512]{1,0:T(8,128)(2,1)S(1)} %maximum_select_fusion.1.refs_4_), channel_id=1, source_target_pairs={{0,1},{1,0},{2,3},{3,2},{4,5},{5,4},{6,7},{7,6},{8,9},{9,8},{10,11... | collective-permute-start | bytes 3145736 | tf_op jit(solution)/shard_map/ppermute | solution.py:349
  138.4 15.3 %collective-permute-start.45 = (bf16[264,1024]{1,0:T(8,128)(2,1)S(1)}, bf16[264,1024]{1,0:T(8,128)(2,1)S(1)}, u32[]{:S(2)}, u32[]{:S(2)}) collective-permute-start(bf16[264,1024]{1,0:T(8,128)(2,1)S(1)} %add_convert_fusion), channel_id=1, source_target_pairs={{2,4},{4,2},{3,5},{5,3},{10,12},{12,10},{11,13},{13,11},{18,20},{2... | collective-permute-start | bytes 1622024 | tf_op jit(solution)/shard_map/ppermute | solution.py:356
  139.1 26.1 %collective-permute-start.43 = (bf16[264,1024]{1,0:T(8,128)(2,1)S(1)}, bf16[264,1024]{1,0:T(8,128)(2,1)S(1)}, u32[]{:S(2)}, u32[]{:S(2)}) collective-permute-start(bf16[264,1024]{1,0:T(8,128)(2,1)S(1)} %add_convert_fusion.1), channel_id=1, source_target_pairs={{0,2},{1,3},{2,0},{3,1},{4,6},{5,7},{6,4},{7,5},{8,10},{9,11},{10,... | collective-permute-start | bytes 1622024 | tf_op jit(solution)/shard_map/ppermute | solution.py:346
  153.5 15.7 %copy-start.1 = (f32[1,8,128,128]{3,2,1,0:T(8,128)S(1)}, f32[1,8,128,128]{3,2,1,0:T(8,128)}, u32[]{:S(2)}) copy-start(f32[1,8,128,128]{3,2,1,0:T(8,128)} %param.15) | copy-start | bytes 1572868
  153.7 26.9 %collective-permute-start.14 = (bf16[128,1024]{1,0:T(8,128)(2,1)S(1)}, bf16[128,1024]{1,0:T(8,128)(2,1)S(1)}, u32[]{:S(2)}, u32[]{:S(2)}) collective-permute-start(bf16[128,1024]{1,0:T(8,128)(2,1)S(1)} %add_convert_fusion.6), channel_id=1, source_target_pairs={{2,4},{4,2},{3,5},{5,3},{10,12},{12,10},{11,13},{13,11},{18,20},{2... | collective-permute-start | bytes 786440 | tf_op jit(solution)/shard_map/ppermute | solution.py:356
  165.3 15.4 %collective-permute-start.12 = (bf16[128,1024]{1,0:T(8,128)(2,1)S(1)}, bf16[128,1024]{1,0:T(8,128)(2,1)S(1)}, u32[]{:S(2)}, u32[]{:S(2)}) collective-permute-start(bf16[128,1024]{1,0:T(8,128)(2,1)S(1)} %add_convert_fusion.7), channel_id=1, source_target_pairs={{0,2},{1,3},{2,0},{3,1},{4,6},{5,7},{6,4},{7,5},{8,10},{9,11},{10,... | collective-permute-start | bytes 786440 | tf_op jit(solution)/shard_map/ppermute | solution.py:346
  172.5 13.9 %collective-permute-start.53 = (bf16[136,1024]{1,0:T(8,128)(2,1)S(1)}, bf16[136,1024]{1,0:T(8,128)(2,1)S(1)}, u32[]{:S(2)}, u32[]{:S(2)}) collective-permute-start(bf16[136,1024]{1,0:T(8,128)(2,1)S(1)} %add_convert_fusion.3), channel_id=1, source_target_pairs={{2,4},{4,2},{3,5},{5,3},{10,12},{12,10},{11,13},{13,11},{18,20},{2... | collective-permute-start | bytes 835592 | tf_op jit(solution)/shard_map/ppermute | solution.py:356
  173.4 15.1 %collective-permute-start.51 = (bf16[136,1024]{1,0:T(8,128)(2,1)S(1)}, bf16[136,1024]{1,0:T(8,128)(2,1)S(1)}, u32[]{:S(2)}, u32[]{:S(2)}) collective-permute-start(bf16[136,1024]{1,0:T(8,128)(2,1)S(1)} %add_convert_fusion.4), channel_id=1, source_target_pairs={{0,2},{1,3},{2,0},{3,1},{4,6},{5,7},{6,4},{7,5},{8,10},{9,11},{10,... | collective-permute-start | bytes 835592 | tf_op jit(solution)/shard_map/ppermute | solution.py:346
  177.7 11.1 %collective-permute-start.46 = (bf16[128,1024]{1,0:T(8,128)(2,1)S(1)}, bf16[128,1024]{1,0:T(8,128)(2,1)S(1)}, u32[]{:S(2)}, u32[]{:S(2)}) collective-permute-start(bf16[128,1024]{1,0:T(8,128)(2,1)S(1)} %get-tuple-element.56), channel_id=1, source_target_pairs={{0,8},{8,0},{16,24},{24,16},{1,9},{9,1},{17,25},{25,17},{2,10},{10... | collective-permute-start | bytes 786440 | tf_op jit(solution)/shard_map/ppermute | solution.py:342
  182.4 16.1 %collective-permute-start.47 = (bf16[128,1024]{1,0:T(8,128)(2,1)S(1)}, bf16[128,1024]{1,0:T(8,128)(2,1)S(1)}, u32[]{:S(2)}, u32[]{:S(2)}) collective-permute-start(bf16[128,1024]{1,0:T(8,128)(2,1)S(1)} %get-tuple-element.57), channel_id=1, source_target_pairs={{0,16},{8,24},{16,0},{24,8},{1,17},{9,25},{17,1},{25,9},{2,18},{10... | collective-permute-start | bytes 786440 | tf_op jit(solution)/shard_map/ppermute | solution.py:342
  182.7 15.8 %collective-permute-start.48 = (bf16[128,1024]{1,0:T(8,128)(2,1)S(1)}, bf16[128,1024]{1,0:T(8,128)(2,1)S(1)}, u32[]{:S(2)}, u32[]{:S(2)}) collective-permute-start(bf16[128,1024]{1,0:T(8,128)(2,1)S(1)} %get-tuple-element.58), channel_id=1, source_target_pairs={{0,24},{8,16},{16,8},{24,0},{1,25},{9,17},{17,9},{25,1},{2,26},{10... | collective-permute-start | bytes 786440 | tf_op jit(solution)/shard_map/ppermute | solution.py:342
  186.4 18.8 %copy-start.13 = (bf16[1,256,1024]{2,1,0:T(8,128)(2,1)S(1)}, bf16[1,256,1024]{2,1,0:T(8,128)(2,1)}, u32[]{:S(2)}) copy-start(bf16[1,256,1024]{2,1,0:T(8,128)(2,1)} %param.8) | copy-start | bytes 1572868
  186.4 12.3 %collective-permute-start.29 = (bf16[128,1024]{1,0:T(8,128)(2,1)S(1)}, bf16[128,1024]{1,0:T(8,128)(2,1)S(1)}, u32[]{:S(2)}, u32[]{:S(2)}) collective-permute-start(bf16[128,1024]{1,0:T(8,128)(2,1)S(1)} %get-tuple-element.43), channel_id=1, source_target_pairs={{0,8},{8,0},{16,24},{24,16},{1,9},{9,1},{17,25},{25,17},{2,10},{10... | collective-permute-start | bytes 786440 | tf_op jit(solution)/shard_map/ppermute | solution.py:342
  188.5 16.7 %collective-permute-start.30 = (bf16[128,1024]{1,0:T(8,128)(2,1)S(1)}, bf16[128,1024]{1,0:T(8,128)(2,1)S(1)}, u32[]{:S(2)}, u32[]{:S(2)}) collective-permute-start(bf16[128,1024]{1,0:T(8,128)(2,1)S(1)} %get-tuple-element.44), channel_id=1, source_target_pairs={{0,16},{8,24},{16,0},{24,8},{1,17},{9,25},{17,1},{25,9},{2,18},{10... | collective-permute-start | bytes 786440 | tf_op jit(solution)/shard_map/ppermute | solution.py:342
  188.8 16.4 %collective-permute-start.31 = (bf16[128,1024]{1,0:T(8,128)(2,1)S(1)}, bf16[128,1024]{1,0:T(8,128)(2,1)S(1)}, u32[]{:S(2)}, u32[]{:S(2)}) collective-permute-start(bf16[128,1024]{1,0:T(8,128)(2,1)S(1)} %get-tuple-element.45), channel_id=1, source_target_pairs={{0,24},{8,16},{16,8},{24,0},{1,25},{9,17},{17,9},{25,1},{2,26},{10... | collective-permute-start | bytes 786440 | tf_op jit(solution)/shard_map/ppermute | solution.py:342
  (6 other events, 4.6 us)
